TPU v7x, 32 devices: a whole 2x2x4 slice. The times are simulated.
32 devices in a mesh: tp: 4 (over y, x), seq: 8 (over z, core).
Axes of the slice: x: 2, y: 2, z: 4, core: 2. Of those that a mesh axis runs over, the one named last changes fastest.
Arguments:
- query_rows: bfloat16 [2048, 8192], P('seq', 'tp'), may hold values from -24 to 24
- key_rows: bfloat16 [2048, 1024], P('seq', 'tp'), may hold values from -9 to 9
- value_rows: bfloat16 [2048, 1024], P('seq', 'tp'), may hold values from -9 to 9
- mixer_input: bfloat16 [2048, 8192], P('seq', 'tp'), may hold values from -6 to 6
- write_rows: bfloat16 [2048, 128], P('seq'), may hold values from -48 to 48
- read_rows: bfloat16 [2048, 128], P('seq'), may hold values from -48 to 48
- log_step: float32 [128, 2048], P('tp', 'seq'), may hold values from -20 to -4
- log_decay: float32 [128, 2048], P('tp', 'seq'), may hold values from -2 to 0
Outputs:
- grad_input: float32 [2048, 8192], P('seq', 'tp')
- grad_write: float32 [2048, 128], P('seq')
- grad_read: float32 [2048, 128], P('seq')
- grad_log_step: float32 [128, 2048], P('tp', 'seq')
All inputs are finite; a program needn't handle non-finite values.
Results may differ from a plain program's by a relative error of at most 0.0015.
Values may be sent and summed in bfloat16 or wider, within the bound.
No kernel may reach another device: no remote copies, remote signals or barrier semaphores. Data moves between devices by JAX's collectives and lax.ppermute only.
A program may use at most 128 MiB of HBM per device.

v0:
```python
import math

import jax
import jax.numpy as jnp
from jax import lax
from jax.experimental import pallas as pl
from jax.experimental.pallas import tpu as pltpu
from jax.sharding import PartitionSpec as P


HD = 128
F32, BF16, F16 = jnp.float32, jnp.bfloat16, jnp.float16


def nn(a, b):
    return lax.dot_general(a, b, (((1,), (0,)), ((), ())), preferred_element_type=F32)


def nt(a, b):
    return lax.dot_general(a, b, (((1,), (1,)), ((), ())), preferred_element_type=F32)


def tn(a, b):
    return lax.dot_general(a, b, (((0,), (0,)), ((), ())), preferred_element_type=F32)


def split2(a):
    hi = a.astype(BF16)
    return hi, (a - hi.astype(F32)).astype(BF16)


def split3(a):
    hi = a.astype(BF16)
    rest = a - hi.astype(F32)
    mid = rest.astype(BF16)
    return hi, mid, (rest - mid.astype(F32)).astype(BF16)


def iota(shape, dim):
    return lax.broadcasted_iota(jnp.int32, shape, dim)


def lower(t):
    return (iota((t, t), 0) >= iota((t, t), 1)).astype(BF16)


def spread_matrix(heads, width, times=1):
    row = iota((times * heads, width), 0) % heads
    return (iota((times * heads, width), 1) // (width // heads) == row).astype(BF16)


def spread(col, width):
    pieces = [p.astype(F32) for p in split3(col)]
    stacked = jnp.concatenate(pieces, axis=1).astype(BF16)
    return nn(stacked, spread_matrix(col.shape[1], width, 3))


def stack2(a):
    return jnp.concatenate(split2(a), axis=0)


def twice(a):
    return jnp.concatenate([a, a], axis=1)


def nt3(a, b):
    ah, al = split2(a)
    bh, bl = split2(b)
    both = nt(ah, jnp.concatenate([bh, bl], axis=0))
    half = both.shape[1] // 2
    return both[:, :half] + both[:, half:] + nt(al, bh)


def code_rows(state, extra):
    top = jnp.max(jnp.abs(state), axis=0, keepdims=True)
    power = jnp.ceil(jnp.log2(jnp.maximum(top, 1e-30)))
    rest = jnp.zeros((15 - len(extra), state.shape[1]), F32)
    return state * jnp.exp2(12.0 - power), jnp.concatenate([power, *extra, rest], axis=0)


def spread_row(row, width):
    return spread(jnp.broadcast_to(row, (8, row.shape[1])), width)[0:1]


def cum_col(ld):
    tri = lower(ld.shape[1])
    a, b, c = split3(ld)
    return nt(tri, a) + nt(tri, b) + nt(tri, c)


def cum_row(ld):
    tri = lower(ld.shape[1])
    a, b, c = split3(ld)
    return nt(a, tri) + nt(b, tri) + nt(c, tri)


def turn(rows):
    t = rows.shape[1]
    eye = (iota((t, t), 0) == iota((t, t), 1)).astype(BF16)
    a, b, c = split3(rows)
    return nt(eye, a) + nt(eye, b) + nt(eye, c)


def state_kernel(x_ref, w_ref, ls_ref, ld_ref, st0_ref, coded_ref, wexp_ref):
    t = x_ref.shape[0] // 2
    width = x_ref.shape[1]
    n = w_ref.shape[1]
    parts, tots = [], []
    for b in (0, 1):
        rows = slice(b * t, (b + 1) * t)
        ccol = cum_col(ld_ref[:, rows])
        tot = ccol[t - 1 : t, :]
        wexp = spread(jnp.exp(tot - ccol + turn(ls_ref[:, rows])), width)
        wexp_ref[rows, :] = wexp
        hi, lo = split2(x_ref[rows, :].astype(F32) * wexp)
        parts.append(tn(w_ref[rows, :], hi) + tn(w_ref[rows, :], lo))
        tots.append(tot)
    st0_ref[...] = parts[0]
    state = spread_row(jnp.exp(tots[1]), width) * parts[0] + parts[1]
    pieces = [p.astype(F32) for p in split3(spread_row(tots[0] + tots[1], width))]
    coded_ref[:n, :], coded_ref[n:, :] = code_rows(state, pieces)


def local_kernel(
    x_ref, w_ref, r_ref, ls_ref, ld_ref, st0_ref,
    y_ref, fs_ref, clsx_ref, crow_ref, cexp, clsrow, a_ref,
):
    t = x_ref.shape[0] // 2
    th = t // 2
    width = x_ref.shape[1]
    heads = ls_ref.shape[0]
    hw = width // heads
    per = 128 // hw
    for b in (0, 1):
        rows = slice(b * t, (b + 1) * t)
        ccol = cum_col(ld_ref[:, rows])
        cexp[...] = spread(ccol, width)
        fs = spread(jnp.exp(ccol), width)
        fs_ref[rows, :] = fs
        clsx_ref[rows, :] = spread(ccol - turn(ls_ref[:, rows]), width)
        crow = cum_row(ld_ref[:, rows])
        crow_ref[:, rows] = crow
        clsrow[...] = crow - ls_ref[:, rows]
        keep = iota((t, t), 0) >= iota((t, t), 1)
        a_ref[...] = jnp.where(keep, nt(r_ref[rows, :], w_ref[rows, :]), 0.0)
        if b == 1:
            y_ref[rows, :] = fs * nn(twice(r_ref[rows, :]), stack2(st0_ref[...]))

        def one(i, rows=rows, b=b):
            cols = pl.ds(pl.multiple_of(i * 128, 128), 128)
            xp = x_ref[rows, cols]
            xtop = jnp.concatenate([xp[:th], xp[:th]], axis=0)
            cc = cexp[:, cols]
            lane = iota((t, 128), 1)
            out = None
            for a in range(per):
                ci = cc[:, a * hw : a * hw + 1]
                cj = clsrow[pl.ds(i * per + a, 1), :]
                top = jnp.exp(jnp.minimum(ci[:th] - cj[:, :th], 0.0)) * a_ref[:th, :th]
                bot = jnp.exp(jnp.minimum(ci[th:] - cj, 0.0)) * a_ref[th:, :]
                yt = nn(jnp.concatenate(split2(top), axis=1), xtop)
                b1, b2 = split2(bot)
                yb = nn(b1, xp) + nn(b2, xp)
                mine = jnp.concatenate([yt, yb], axis=0)
                out = mine if out is None else jnp.where(lane >= a * hw, mine, out)
            if b == 1:
                out = out + y_ref[rows, cols]
            return cols, out

        def two(i, _, rows=rows, one=one):
            done = [one(2 * i), one(2 * i + 1)]
            for cols, out in done:
                y_ref[rows, cols] = out
            return 0

        lax.fori_loop(0, width // 256, two, 0)


def keys_twice(kv_ref, g, kw):
    k = kv_ref[:, g * HD : (g + 1) * HD]
    return jnp.concatenate([k, k], axis=1), kv_ref[:, kw + g * HD : kw + (g + 1) * HD].T


def own_kernel(q_ref, kv_ref, qs_ref, acc_ref, m_ref, l_ref, k2, vt, bias, s0a, s1a, s0b, s1b):
    t = q_ref.shape[0] // 2
    kw = kv_ref.shape[1] // 2
    kvh = kw // HD
    group = q_ref.shape[1] // HD // kvh
    scale = 1.0 / math.sqrt(HD)
    bias[...] = jnp.where(iota((t, t), 0) <= iota((t, t), 1), 0.0, -1e30)
    for g in range(kvh):
        k2[...], vt[...] = keys_twice(kv_ref, g, kw)

        def scores(h, s0, s1, g=g):
            at = g * group + h
            q = q_ref[:, pl.ds(pl.multiple_of(at * HD, HD), HD)].astype(F32) * scale
            both = jnp.concatenate(split2(q), axis=1)
            qs_ref[:, pl.ds(pl.multiple_of(at * 2 * HD, 2 * HD), 2 * HD)] = both
            s0[...] = nt(k2[:t, :], both[:t]) + bias[...]
            s1[:t, :] = nt(k2[:t, :], both[t:])
            s1[t:, :] = nt(k2[t:, :], both[t:]) + bias[...]

        def soft(h, s0, s1, g=g):
            at = g * group + h
            cols = pl.ds(pl.multiple_of(at * HD, HD), HD)
            for b, s_ref in ((0, s0), (1, s1)):
                rows = slice(b * t, (b + 1) * t)
                s = s_ref[...]
                top = jnp.max(s, axis=0, keepdims=True)
                e = jnp.exp(s - top)
                m_ref[pl.ds(at, 1), rows] = top
                l_ref[pl.ds(at, 1), rows] = jnp.sum(e, axis=0, keepdims=True)
                acc_ref[cols, rows] = nn(vt[:, : (b + 1) * t], e.astype(BF16))

        scores(0, s0a, s1a)

        def pair(i, _):
            scores(2 * i + 1, s0b, s1b)
            soft(2 * i, s0a, s1a)
            scores(jnp.minimum(2 * i + 2, group - 1), s0a, s1a)
            soft(2 * i + 1, s0b, s1b)
            return 0

        lax.fori_loop(0, group // 2, pair, 0)


def far_kernel(flag, qs_ref, kv_ref, acc_in, m_in, l_in, acc_ref, m_ref, l_ref, k2, vt, sa, sb):
    t = qs_ref.shape[0] // 2
    kw = kv_ref.shape[1] // 2
    kvh = kw // HD
    group = qs_ref.shape[1] // (2 * HD) // kvh

    @pl.when(flag[0] == 0)
    def _():
        acc_ref[...] = acc_in[...]
        m_ref[...] = m_in[...]
        l_ref[...] = l_in[...]

    @pl.when(flag[0] == 1)
    def _():
        for g in range(kvh):
            k2[...], vt[...] = keys_twice(kv_ref, g, kw)

            def scores(h, s_ref, g=g):
                at = g * group + h
                s_ref[...] = nt(k2[...], qs_ref[:, pl.ds(pl.multiple_of(at * 2 * HD, 2 * HD), 2 * HD)])

            def soft(h, s_ref, g=g):
                at = g * group + h
                cols = pl.ds(pl.multiple_of(at * HD, HD), HD)
                row = pl.ds(at, 1)
                for b in (0, 1):
                    rows = slice(b * t, (b + 1) * t)
                    s = s_ref[:, rows]
                    old = m_in[row, rows]
                    new = jnp.maximum(old, jnp.max(s, axis=0, keepdims=True))
                    e = jnp.exp(s - new)
                    fade = jnp.exp(old - new)
                    m_ref[row, rows] = new
                    l_ref[row, rows] = l_in[row, rows] * fade + jnp.sum(e, axis=0, keepdims=True)
                    acc_ref[cols, rows] = acc_in[cols, rows] * fade + nn(vt[...], e.astype(BF16))

            scores(0, sa)

            def pair(i, _):
                scores(2 * i + 1, sb)
                soft(2 * i, sa)
                scores(jnp.minimum(2 * i + 2, group - 1), sa)
                soft(2 * i + 1, sb)
                return 0

            lax.fori_loop(0, group // 2, pair, 0)


def residual_kernel(y_ref, acc_ref, l_ref, r_ref, fs_ref, sin_ref, res_ref, d1_ref, coded_ref):
    t = y_ref.shape[0] // 2
    width = y_ref.shape[1]
    n = r_ref.shape[1]
    state = sin_ref[...]
    first = fs_ref[t - 1 : t, :]
    parts = []
    for b in (0, 1):
        rows = slice(b * t, (b + 1) * t)
        fs = fs_ref[rows, :]
        r = r_ref[rows, :]
        heads = [
            (acc_ref[h * HD : (h + 1) * HD, rows] / l_ref[h : h + 1, rows]).astype(BF16).T
            for h in range(width // HD)
        ]
        teach = jnp.concatenate(heads, axis=1).astype(F32)
        res = y_ref[rows, :] + fs * nn(twice(r), stack2(state * first if b else state)) - teach
        res_ref[rows, :] = res
        hi, lo = split2(res * fs)
        parts.append(tn(r, hi) + tn(r, lo))
    d1_ref[...] = parts[1]
    coded_ref[:n, :], coded_ref[n:, :] = code_rows(parts[0] + first * parts[1], [])


def back_kernel(
    res_ref, x_ref, w_ref, r_ref, clsx_ref, crow_ref, fs_ref, wexp_ref, sin_ref, st0_ref, d1_ref,
    back_ref, gw_ref, gr_ref, a_ref, pair,
):
    t = x_ref.shape[0] // 2
    th = t // 2
    width = x_ref.shape[1]
    heads = crow_ref.shape[0]
    hw = width // heads
    per = 128 // hw
    first = fs_ref[t - 1 : t, :]
    for b in (0, 1):
        rows = slice(b * t, (b + 1) * t)
        keep = iota((t, t), 1) >= iota((t, t), 0)
        w = w_ref[rows, :]
        r = r_ref[rows, :]
        a_ref[...] = jnp.where(keep, nt(w, r), 0.0)
        pair[...] = jnp.zeros_like(pair)
        if b == 0:
            d1 = d1_ref[...]
            wexp = wexp_ref[rows, :]
            back_ref[rows, :] = wexp * nn(twice(w), stack2(d1))
            gw = nt3(x_ref[rows, :].astype(F32) * wexp, d1)
            state = sin_ref[...]
        else:
            gw = None
            state = first * sin_ref[...] + st0_ref[...]
        gr = nt3(res_ref[rows, :] * fs_ref[rows, :], state)

        def one(i, rows=rows, b=b):
            cols = pl.ds(pl.multiple_of(i * 128, 128), 128)
            xp = x_ref[rows, cols]
            rh, rl = split2(res_ref[rows, cols])
            both = jnp.concatenate([rh, rl], axis=1)
            cc = clsx_ref[rows, cols]
            lane = iota((t, 128), 1)
            out, above, below = None, 0.0, 0.0
            for a in range(per):
                cj = cc[:, a * hw : a * hw + 1]
                ci = crow_ref[pl.ds(i * per + a, 1), rows]
                xx = twice(jnp.where((lane // hw) == a, xp, jnp.zeros_like(xp)))
                e1 = jnp.exp(jnp.minimum(ci - cj[:th], 0.0))
                e2 = jnp.exp(jnp.minimum(ci[:, th:] - cj[th:], 0.0))
                h1, l1 = split2(e1 * a_ref[:th, :])
                h2, l2 = split2(e2 * a_ref[th:, th:])
                p1 = nn(h1, both)
                p2 = nn(h2, both[th:])
                u1 = p1[:, :128] + p1[:, 128:] + nn(l1, rh)
                u2 = p2[:, :128] + p2[:, 128:] + nn(l2, rh[th:])
                u = jnp.concatenate([u1, u2], axis=0)
                out = u if out is None else jnp.where(lane >= a * hw, u, out)
                above += e1 * nt(xx[:th], both)
                below += e2 * nt(xx[th:], both[th:])
            if b == 0:
                out = out + back_ref[rows, cols]
            return cols, out, above, below

        def two(i, _, rows=rows, one=one):
            done = [one(2 * i), one(2 * i + 1)]
            for cols, out, _, _ in done:
                back_ref[rows, cols] = out
            pair[:th, :] += done[0][2] + done[1][2]
            pair[th:, th:] += done[0][3] + done[1][3]
            return 0

        lax.fori_loop(0, width // 256, two, 0)
        ph, plo = split2(jnp.where(keep, pair[...], 0.0))
        gr_ref[rows, :] = gr + tn(ph, w) + tn(plo, w)
        mixed = nn(ph, r) + nn(plo, r)
        gw_ref[rows, :] = mixed if gw is None else mixed + gw


def ready_kernel(x_ref, ls_ref, ld_ref, extra_ref, wexp_ref, xh_ref, xl_ref):
    t = x_ref.shape[0]
    ccol = cum_col(ld_ref[...])
    wexp = spread(
        jnp.exp(ccol[t - 1 : t, :] + extra_ref[...] - ccol + turn(ls_ref[...])), x_ref.shape[1]
    )
    wexp_ref[...] = wexp
    xh_ref[...], xl_ref[...] = split2(x_ref[...].astype(F32) * wexp)


def write_kernel(xh_ref, xl_ref, g_ref, gw0_ref, gw_ref):
    gh, gl = split2(g_ref[...])
    n = gh.shape[0]
    both = nt(xh_ref[...], jnp.concatenate([gh, gl], axis=0))
    gw_ref[...] = gw0_ref[...] + both[:, :n] + both[:, n:] + nt(xl_ref[...], gh)


def final_kernel(back_ref, wexp_ref, x_ref, w_ref, g_ref, gi_ref, gls_ref):
    width = x_ref.shape[1]
    heads = gls_ref.shape[0]
    out = back_ref[...] + wexp_ref[...] * nn(twice(w_ref[...]), stack2(g_ref[...]))
    gi_ref[...] = out
    ph, plo = split2(x_ref[...].astype(F32) * out)
    mat = spread_matrix(heads, width)
    gls_ref[...] = nt(mat, ph) + nt(mat, plo)


VM = pl.BlockSpec(memory_space=pltpu.VMEM)


def call(kernel, outs, args, scratch=(), flops=0, in_specs=None, alias=None):
    shapes = [jax.ShapeDtypeStruct(s, d) for s, d in outs]
    moved = sum(a.size * a.dtype.itemsize for a in args)
    return pl.pallas_call(
        kernel,
        out_shape=shapes,
        in_specs=in_specs or [VM] * len(args),
        out_specs=[VM] * len(shapes),
        scratch_shapes=list(scratch),
        input_output_aliases=alias or {},
        cost_estimate=pl.CostEstimate(flops=flops, bytes_accessed=moved, transcendentals=0),
        compiler_params=pltpu.CompilerParams(vmem_limit_bytes=16 * 2**20),
    )(*args)


def decode(coded, rows, weight):
    power = coded[rows : rows + 1].astype(F32)
    return coded[:rows].astype(F32) * (jnp.exp2(power - 12.0) * weight)


def on_device(q, k, v, x, wr, rd, ls, ld):
    t = q.shape[0]
    count = lax.axis_size("seq")
    tp = lax.axis_size("tp")
    chips = count // 2
    index = lax.axis_index("seq")
    core, chip = index % 2, index // 2
    heads = ls.shape[0]
    hh = heads // 2
    n = wr.shape[1]
    hc = x.shape[1] // 2
    qc = q.shape[1] // 2
    kvh = k.shape[1] // HD
    kw = k.shape[1] // 2 if kvh % 2 == 0 else k.shape[1]

    def swap(a, bits):
        return lax.ppermute(a, "seq", [(i, i ^ bits) for i in range(count)])

    def half(a, which, width, axis=1):
        return lax.dynamic_slice_in_dim(a, which * width, width, axis=axis)

    def joined(own, other, axis=0):
        a = jnp.where(core == 0, own, other)
        b = jnp.where(core == 0, other, own)
        return jnp.concatenate([a, b], axis=axis)

    def near(a):
        return {1 << b: swap(a, 2 << b) for b in range(chips.bit_length() - 1)}

    def relay(got, token):
        got = dict(got)
        for d in range(1, chips):
            if d not in got:
                low = d & -d
                held, _ = lax.optimization_barrier((got[d - low], token))
                got[d] = swap(held, 2 * low)
        return [got[d] for d in range(1, chips)]

    def kv_half(which):
        if kvh % 2 == 0:
            return jnp.concatenate([half(k, which, kw), half(v, which, kw)], axis=1)
        return jnp.concatenate([k, v], axis=1)

    kv = joined(kv_half(core), swap(kv_half(1 - core), 1))
    keys_near = near(kv)
    x1, q1, wr1, rd1, _ = lax.optimization_barrier((x, q, wr, rd, kv))
    rates = swap(jnp.concatenate([ls, ld], axis=0), 1)
    lsc = joined(half(ls, core, hh, 0), half(rates, core, hh, 0), 1)
    ldc = joined(half(ld, core, hh, 0), half(rates[heads:], core, hh, 0), 1)
    mates = swap(jnp.concatenate([half(x1, 1 - core, hc), wr1, rd1], axis=1), 1)
    xc = joined(half(x1, core, hc), mates[:, :hc])
    wc = joined(wr1, mates[:, hc : hc + n])
    rc = joined(rd1, mates[:, hc + n :])
    qg = joined(half(q1, core, qc), swap(half(q1, 1 - core, qc), 1))

    mm = 2 * 2 * t * hc * n
    code = ((n + 16, hc), F32)
    st0, coded, wexpc = call(
        state_kernel, [((n, hc), F32), code, ((2 * t, hc), F32)], (xc, wc, lsc, ldc),
        flops=4 * mm,
    )
    mine = coded.astype(F16)
    states_near = near(mine)
    qh = qc // HD
    carry = [((qc, 2 * t), F32), ((qh, 2 * t), F32), ((qh, 2 * t), F32)]
    qs, *soft = call(
        own_kernel, [((2 * t, 2 * qc), BF16), *carry], (qg, kv),
        scratch=[pltpu.VMEM((2 * t, 2 * HD), BF16), pltpu.VMEM((HD, 2 * t), BF16), pltpu.VMEM((t, t), F32)]
        + [pltpu.VMEM((t, t), F32), pltpu.VMEM((2 * t, t), F32)] * 2,
        flops=4 * (2 * t) ** 2 * qc,
    )
    ybase, fs, clsx, crow = call(
        local_kernel,
        [((2 * t, hc), F32), ((2 * t, hc), F32), ((2 * t, hc), F32), ((hh, 2 * t), F32)],
        (xc, wc, rc, lsc, ldc, st0),
        scratch=[pltpu.VMEM((t, hc), F32), pltpu.VMEM((hh, t), F32), pltpu.VMEM((t, t), F32)],
        flops=8 * mm,
    )
    far = relay(keys_near, soft[1])
    states = relay(states_near, soft[1])
    decays = [jnp.sum(f[n + 1 : n + 4].astype(F32), axis=0, keepdims=True) for f in states]

    def weight(d, later):
        p = chip ^ d
        low, high = (chip, p) if later else (p, chip)
        between = jnp.zeros((1, hc), F32)
        for m in range(1, chips):
            at = chip ^ m
            between += jnp.where((at > low) & (at < high), decays[m - 1], 0.0)
        return jnp.where((p > chip) if later else (p < chip), jnp.exp(between), 0.0)

    def combine(got, later):
        return sum(decode(g, n, weight(d, later)) for d, g in enumerate(got, 1))

    for d, keys in enumerate(far, 1):
        flag = jnp.reshape((chip ^ d) < chip, (1,)).astype(jnp.int32)
        soft = call(
            far_kernel, carry, (flag, qs, keys, *soft),
            scratch=[pltpu.VMEM((2 * t, 2 * HD), BF16), pltpu.VMEM((HD, 2 * t), BF16)] + [pltpu.VMEM((2 * t, 2 * t), F32)] * 2,
            flops=4 * (2 * t) ** 2 * qc, alias={3: 0, 4: 1, 5: 2},
            in_specs=[pl.BlockSpec(memory_space=pltpu.SMEM)] + [VM] * 5,
        )
    incoming = combine(states, False)
    res, d1, dcode = call(
        residual_kernel, [((2 * t, hc), F32), ((n, hc), F32), code],
        (ybase, soft[0], soft[2], rc, fs, incoming), flops=8 * mm,
    )
    sent = dcode.astype(F16)
    coming = [swap(sent, 2 * d) for d in range(1, chips)]
    back, gw, gr = call(
        back_kernel, [((2 * t, hc), F32), ((2 * t, n), F32), ((2 * t, n), F32)],
        (res, xc, wc, rc, clsx, crow, fs, wexpc, incoming, st0, d1),
        scratch=[pltpu.VMEM((t, t), F32), pltpu.VMEM((t, t), F32)],
        flops=16 * mm,
    )
    other_total = jnp.sum(rates[heads:], axis=1)[None, :]
    extra = jnp.where(core == 0, other_total, 0.0)
    wexp, xh, xl = call(
        ready_kernel, [((t, 2 * hc), F32), ((t, 2 * hc), BF16), ((t, 2 * hc), BF16)],
        (x, ls, ld, extra), flops=2 * mm,
    )

    def home(a):
        return half(a, core, t, 0), swap(half(a, 1 - core, t, 0), 1)

    def tp_sum(a):
        bit = 1
        while bit < tp:
            a = a + lax.ppermute(a, "tp", [(i, i ^ bit) for i in range(tp)])
            bit *= 2
        return a

    back_all = joined(*home(back), 1)
    own, other = home(jnp.concatenate([gw, gr], axis=1))
    grads = own + other
    gw0, gr0 = grads[:, :n], grads[:, n:]
    grad_read = tp_sum(gr0)
    *coming, grad_read, wexp, back_all = lax.optimization_barrier((*coming, grad_read, wexp, back_all))
    arriving = combine(coming, True)
    arrived = joined(arriving, swap(arriving, 1), 1)
    (gwp,) = call(write_kernel, [((t, n), F32)], (xh, xl, arrived, gw0), flops=4 * mm)
    grad_write = tp_sum(gwp)
    gi, gls = call(
        final_kernel, [((t, 2 * hc), F32), ((heads, t), F32)], (back_all, wexp, x, wr, arrived),
        flops=8 * mm,
    )
    return (gi, grad_write, grad_read, gls)


def solution(mesh):
    in_specs = (
        P("seq", "tp"), P("seq", "tp"), P("seq", "tp"), P("seq", "tp"),
        P("seq", None), P("seq", None), P("tp", "seq"), P("tp", "seq"),
    )
    out_specs = (P("seq", "tp"), P("seq", None), P("seq", None), P("tp", "seq"))
    return jax.shard_map(
        on_device, mesh=mesh, in_specs=in_specs, out_specs=out_specs, check_vma=False
    )
```

profile of v0, /device:TPU:0, one launch (start us, length us, event | category | flops | bytes accessed | tf_op | source)
XLA Modules:
  0.0 110.4 jit_solution(12830597080617552880)
XLA Ops:
  0.7 0.9 pad_maximum_fusion.10
  1.6 0.6 collective-permute-start.2
  2.1 1.0 constant_dynamic-slice_fusion.6
  3.1 0.1 collective-permute-start
  3.3 0.1 slice_reduce_fusion
  3.5 1.1 collective-permute-done
  4.5 0.1 broadcast_select_fusion.7
  4.6 0.0 copy-start.4
  4.7 0.2 collective-permute-start.3
  5.0 0.1 pad_maximum_fusion.4
  5.1 0.4 collective-permute-start.1
  5.5 3.8 %collective-permute-start.4 = (bf16[512,256]{1,0:T(8,128)(2,1)S(1)}, bf16[512,256]{1,0:T(8,128)(2,1)S(1)}, u32[]{:S(2)}, u32[]{:S(2)}) collective-permute-start(bf16[512,256]{1,0:T(8,128)(2,1)S(1)} %pad_maximum_fusion.5.kv_ref), channel_id=1, source_target_pairs={{0,4},{1,5},{2,6},{3,7},{4,0},{5,1},{6,2},{7,3},{8,12},{9,13},{10,... | collective-permute-start | bytes 786440 | tf_op jit(solution)/shard_map/ppermute | solution.py:437
  9.3 1.6 %collective-permute-start.6 = (bf16[512,256]{1,0:T(8,128)(2,1)S(1)}, bf16[512,256]{1,0:T(8,128)(2,1)S(1)}, u32[]{:S(2)}, u32[]{:S(2)}) collective-permute-start(bf16[512,256]{1,0:T(8,128)(2,1)S(1)} %pad_maximum_fusion.5.kv_ref), channel_id=1, source_target_pairs={{0,2},{1,3},{2,0},{3,1},{4,6},{5,7},{6,4},{7,5},{8,10},{9,11},{10,... | collective-permute-start | bytes 786440 | tf_op jit(solution)/shard_map/ppermute | solution.py:437
  10.9 0.3 broadcast_select_fusion.1
  11.2 0.1 pad_maximum_fusion.2.q_ref
  11.3 0.3 broadcast_select_fusion.3
  11.5 0.1 pad_maximum_fusion.1.x_ref
  11.7 2.0 %shard_map.111 = (f32[128,1024]{1,0:T(8,128)S(1)}, f32[144,1024]{1,0:T(8,128)S(1)}, f32[512,1024]{1,0:T(8,128)S(1)}) custom-call(bf16[512,1024]{1,0:T(8,128)(2,1)S(1)} %pad_maximum_fusion.1.x_ref, bf16[512,128]{1,0:T(8,128)(2,1)S(1)} %pad_maximum_fusion.8.w_ref, f32[16,512]{1,0:T(8,128)S(1)} %pad_maximum_fusion.11.ls_ref, ...), custom_call_target="tpu_custom_call" | custom-call | flops 536870912 | bytes 1245184 | tf_op jit(solution)/shard_map/pallas_call | solution.py:404
  13.7 0.4 collective-permute-start.8
  14.1 3.1 %shard_map.113 = (bf16[512,2048]{1,0:T(8,128)(2,1)S(1)}, f32[1024,512]{1,0:T(8,128)S(1)}, f32[8,512]{1,0:T(8,128)S(1)}, f32[8,512]{1,0:T(8,128)S(1)}) custom-call(bf16[512,1024]{1,0:T(8,128)(2,1)S(1)} %pad_maximum_fusion.2.q_ref, bf16[512,256]{1,0:T(8,128)(2,1)S(1)} %pad_maximum_fusion.5.kv_ref), custom_call_target="tpu_custom_call" | custom-call | flops 1073741824 | bytes 1310720 | tf_op jit(solution)/shard_map/pallas_call | solution.py:404
  17.2 4.9 %collective-permute-done.4.kv_ref = bf16[512,256]{1,0:T(8,128)(2,1)S(1)} collective-permute-done((bf16[512,256]{1,0:T(8,128)(2,1)S(1)}, bf16[512,256]{1,0:T(8,128)(2,1)S(1)}, u32[]{:S(2)}, u32[]{:S(2)}) %collective-permute-start.4) | collective-permute-done | bytes 262176 | tf_op jit(solution)/shard_map/ppermute | solution.py:437
  22.2 0.7 collective-permute-start.5
  22.9 1.3 %collective-permute-start.7 = (f16[144,1024]{1,0:T(8,128)(2,1)S(1)}, f16[144,1024]{1,0:T(8,128)(2,1)S(1)}, u32[]{:S(2)}, u32[]{:S(2)}) collective-permute-start(f16[144,1024]{1,0:T(8,128)(2,1)S(1)} %convert_element_type.72), channel_id=1, source_target_pairs={{0,2},{1,3},{2,0},{3,1},{4,6},{5,7},{6,4},{7,5},{8,10},{9,11},{10,... | collective-permute-start | bytes 884744 | tf_op jit(solution)/shard_map/ppermute | solution.py:437
  24.2 6.9 %shard_map.112 = (f32[512,1024]{1,0:T(8,128)S(1)}, f32[512,1024]{1,0:T(8,128)S(1)}, f32[512,1024]{1,0:T(8,128)S(1)}, f32[16,512]{1,0:T(8,128)S(1)}) custom-call(bf16[512,1024]{1,0:T(8,128)(2,1)S(1)} %pad_maximum_fusion.1.x_ref, bf16[512,128]{1,0:T(8,128)(2,1)S(1)} %pad_maximum_fusion.8.w_ref, bf16[512,128]{1,0:T(8,128)(2,1)S(1)} %pad_maximum_fusion.9.r_ref, ...), custom_call_target="tpu_custom_call" | custom-call | flops 1073741824 | bytes 1900544 | tf_op jit(solution)/shard_map/pallas_call | solution.py:404
  31.1 3.4 %collective-permute-done.8 = f16[144,1024]{1,0:T(8,128)(2,1)S(1)} collective-permute-done((f16[144,1024]{1,0:T(8,128)(2,1)S(1)}, f16[144,1024]{1,0:T(8,128)(2,1)S(1)}, u32[]{:S(2)}, u32[]{:S(2)}) %collective-permute-start.8) | collective-permute-done | bytes 294944 | tf_op jit(solution)/shard_map/ppermute | solution.py:437
  34.5 0.6 collective-permute-start.9
  35.2 0.3 shard_map.114
  35.5 0.3 shard_map.115
  35.8 0.7 collective-permute-done.5.kv_ref
  36.5 0.5 shard_map.116
  37.0 5.8 %collective-permute-done.7 = f16[144,1024]{1,0:T(8,128)(2,1)S(1)} collective-permute-done((f16[144,1024]{1,0:T(8,128)(2,1)S(1)}, f16[144,1024]{1,0:T(8,128)(2,1)S(1)}, u32[]{:S(2)}, u32[]{:S(2)}) %collective-permute-start.7) | collective-permute-done | bytes 294944 | tf_op jit(solution)/shard_map/ppermute | solution.py:437
  42.9 4.7 %collective-permute-done.9 = f16[144,1024]{1,0:T(8,128)(2,1)S(1)} collective-permute-done((f16[144,1024]{1,0:T(8,128)(2,1)S(1)}, f16[144,1024]{1,0:T(8,128)(2,1)S(1)}, u32[]{:S(2)}, u32[]{:S(2)}) %collective-permute-start.9) | collective-permute-done | bytes 294944 | tf_op jit(solution)/shard_map/ppermute | solution.py:437
  47.7 0.2 multiply_add_fusion.1.sin_ref
  47.9 1.5 %shard_map.117 = (f32[512,1024]{1,0:T(8,128)S(1)}, f32[128,1024]{1,0:T(8,128)S(1)}, f32[144,1024]{1,0:T(8,128)S(1)}) custom-call(f32[512,1024]{1,0:T(8,128)S(1)} %get-tuple-element.50.y_ref, f32[1024,512]{1,0:T(8,128)S(1)} %get-tuple-element.63.acc_ref, f32[8,512]{1,0:T(8,128)S(1)} %get-tuple-element.64.l_ref, bf16[512,128]{1,0:T(8,128)(2,1)S(1)} %pad_maximum_fusion.9.r_ref, ...), custom_call_target="tpu_custom_call" | custom-call | flops 1073741824 | bytes 6963200 | tf_op jit(solution)/shard_map/pallas_call | solution.py:404
  49.4 8.1 %shard_map.118 = (f32[512,1024]{1,0:T(8,128)S(1)}, f32[512,128]{1,0:T(8,128)S(1)}, f32[512,128]{1,0:T(8,128)S(1)}) custom-call(f32[512,1024]{1,0:T(8,128)S(1)} %get-tuple-element.69.res_ref, bf16[512,1024]{1,0:T(8,128)(2,1)S(1)} %pad_maximum_fusion.1.x_ref, bf16[512,128]{1,0:T(8,128)(2,1)S(1)} %pad_maximum_fusion.8.w_ref, ...), custom_call_target="tpu_custom_call" | custom-call | flops 2147483648 | bytes 11304960 | tf_op jit(solution)/shard_map/pallas_call | solution.py:404
  57.6 0.8 copy-done.6
  58.4 0.1 collective-permute-start.13
  58.5 1.0 constant_dynamic-slice_fusion
  59.6 0.5 collective-permute-start.16
  60.1 0.1 collective-permute-done.13
  60.2 1.1 %dynamic-slice_add_fusion = f32[256,256]{1,0:T(8,128)S(1)} fusion(f32[256,256]{1,0:T(8,128)} %collective-permute-done.13, f32[512,256]{1,0:T(8,128)} %copy-done.6, s32[]{:T(128)S(6)} %select_n.490), kind=kLoop, calls=%fused_computation.14 | loop fusion | flops 65536 | bytes 786436 | tf_op jit(solution)/shard_map/add | solution.py:555
  61.3 1.4 %collective-permute-start.14 = (f32[256,128]{1,0:T(8,128)S(1)}, f32[256,128]{1,0:T(8,128)S(1)}, u32[]{:S(2)}, u32[]{:S(2)}) collective-permute-start(f32[256,128]{1,0:T(8,128)S(1)} %slice.98), channel_id=1, source_target_pairs={{0,8},{8,0},{16,24},{24,16},{1,9},{9,1},{17,25},{25,17},{2,10},{10... | collective-permute-start | bytes 393224 | tf_op jit(solution)/shard_map/ppermute | solution.py:549
  62.7 4.2 %collective-permute-done.14 = f32[256,128]{1,0:T(8,128)S(1)} collective-permute-done((f32[256,128]{1,0:T(8,128)S(1)}, f32[256,128]{1,0:T(8,128)S(1)}, u32[]{:S(2)}, u32[]{:S(2)}) %collective-permute-start.14) | collective-permute-done | bytes 131104 | tf_op jit(solution)/shard_map/ppermute | solution.py:549
  66.9 1.4 %collective-permute-start.15 = (f32[256,128]{1,0:T(8,128)S(1)}, f32[256,128]{1,0:T(8,128)S(1)}, u32[]{:S(2)}, u32[]{:S(2)}) collective-permute-start(f32[256,128]{1,0:T(8,128)S(1)} %get-tuple-element.103), channel_id=1, source_target_pairs={{0,16},{8,24},{16,0},{24,8},{1,17},{9,25},{17,1},{25,9},{2,18},{10... | collective-permute-start | bytes 393224 | tf_op jit(solution)/shard_map/ppermute | solution.py:549
  68.3 1.0 shard_map.119
  69.3 0.8 collective-permute-start.10
  70.2 5.3 %collective-permute-start.11 = (f16[144,1024]{1,0:T(8,128)(2,1)S(1)}, f16[144,1024]{1,0:T(8,128)(2,1)S(1)}, u32[]{:S(2)}, u32[]{:S(2)}) collective-permute-start(f16[144,1024]{1,0:T(8,128)(2,1)S(1)} %convert_element_type.82), channel_id=1, source_target_pairs={{0,4},{1,5},{2,6},{3,7},{4,0},{5,1},{6,2},{7,3},{8,12},{9,13},{10,... | collective-permute-start | bytes 884744 | tf_op jit(solution)/shard_map/ppermute | solution.py:437
  75.4 0.7 add.164
  76.1 1.4 %dynamic-slice_select_fusion.1 = (f32[256,1024]{1,0:T(8,128)S(1)}, f32[256,1024]{1,0:T(8,128)S(1)}) fusion(f32[256,1024]{1,0:T(8,128)} %collective-permute-done.16, f32[512,1024]{1,0:T(8,128)S(1)} %get-tuple-element.77, s32[]{:T(128)S(6)} %select_n.490, pred[]{:T(512)S(6)} %eq.4), kind=kLoop, calls=%fused_computation.5 | loop fusion | flops 524288 | bytes 4194309 | tf_op jit(solution)/shard_map/jit(_where)/select_n | solution.py:443
  77.5 0.2 pad_maximum_fusion.back_ref
  77.8 4.6 %collective-permute-done.10 = f16[144,1024]{1,0:T(8,128)(2,1)S(1)} collective-permute-done((f16[144,1024]{1,0:T(8,128)(2,1)S(1)}, f16[144,1024]{1,0:T(8,128)(2,1)S(1)}, u32[]{:S(2)}, u32[]{:S(2)}) %collective-permute-start.10) | collective-permute-done | bytes 294944 | tf_op jit(solution)/shard_map/ppermute | solution.py:437
  82.3 13.6 %collective-permute-done.11 = f16[144,1024]{1,0:T(8,128)(2,1)S(1)} collective-permute-done((f16[144,1024]{1,0:T(8,128)(2,1)S(1)}, f16[144,1024]{1,0:T(8,128)(2,1)S(1)}, u32[]{:S(2)}, u32[]{:S(2)}) %collective-permute-start.11) | collective-permute-done | bytes 294944 | tf_op jit(solution)/shard_map/ppermute | solution.py:437
  96.0 0.2 multiply_add_fusion
  96.2 0.1 collective-permute-start.17
  96.3 1.9 %collective-permute-done.17 = f32[128,1024]{1,0:T(8,128)S(1)} collective-permute-done((f32[128,1024]{1,0:T(8,128)S(1)}, f32[128,1024]{1,0:T(8,128)S(1)}, u32[]{:S(2)}, u32[]{:S(2)}) %collective-permute-start.17) | collective-permute-done | bytes 524320 | tf_op jit(solution)/shard_map/ppermute | solution.py:437
  98.2 0.1 broadcast_select_fusion.5
  98.3 0.1 pad_maximum_fusion.3.g_ref
  98.3 0.8 shard_map.121
  99.1 1.5 %collective-permute-start.18 = (f32[256,128]{1,0:T(8,128)S(1)}, f32[256,128]{1,0:T(8,128)S(1)}, u32[]{:S(2)}, u32[]{:S(2)}) collective-permute-start(f32[256,128]{1,0:T(8,128)S(1)} %shard_map.121), channel_id=1, source_target_pairs={{0,8},{8,0},{16,24},{24,16},{1,9},{9,1},{17,25},{25,17},{2,10},{10... | collective-permute-start | bytes 393224 | tf_op jit(solution)/shard_map/ppermute | solution.py:549
  100.6 4.1 %collective-permute-done.18 = f32[256,128]{1,0:T(8,128)S(1)} collective-permute-done((f32[256,128]{1,0:T(8,128)S(1)}, f32[256,128]{1,0:T(8,128)S(1)}, u32[]{:S(2)}, u32[]{:S(2)}) %collective-permute-start.18) | collective-permute-done | bytes 131104 | tf_op jit(solution)/shard_map/ppermute | solution.py:549
  104.7 0.6 collective-permute-start.19
  105.3 2.2 %shard_map.120 = (f32[256,2048]{1,0:T(8,128)}, f32[32,256]{1,0:T(8,128)}) custom-call(f32[256,2048]{1,0:T(8,128)S(1)} %pad_maximum_fusion.back_ref, f32[256,2048]{1,0:T(8,128)S(1)} %get-tuple-element.79.wexp_ref, bf16[256,2048]{1,0:T(8,128)(2,1)S(1)} %copy-done, bf16[256,128]{1,0:T(8,128)(2,1)S(1)} %copy-done.1, f32[128,2048]{1,0:T(8,128)S(1)} %pad_maximum_fusion.3.g_ref), custom_call_target="tpu_custom_call" | custom-call | flops 1073741824 | bytes 6356992 | tf_op jit(solution)/shard_map/pallas_call | solution.py:404
  107.5 2.3 %collective-permute-done.19 = f32[256,128]{1,0:T(8,128)S(1)} collective-permute-done((f32[256,128]{1,0:T(8,128)S(1)}, f32[256,128]{1,0:T(8,128)S(1)}, u32[]{:S(2)}, u32[]{:S(2)}) %collective-permute-start.19) | collective-permute-done | bytes 131104 | tf_op jit(solution)/shard_map/ppermute | solution.py:549
  109.8 0.7 add.171
  (54 shorter events, 0.6 us)
Async XLA Ops:
  0.6 4.3 %copy-start = (bf16[256,2048]{1,0:T(8,128)(2,1)S(1)}, bf16[256,2048]{1,0:T(8,128)(2,1)}, u32[]{:S(2)}) copy-start(bf16[256,2048]{1,0:T(8,128)(2,1)} %x_ref.3) | copy-start | bytes 3145732
  0.6 4.0 %copy-start.7 = (bf16[256,2048]{1,0:T(8,128)(2,1)S(1)}, bf16[256,2048]{1,0:T(8,128)(2,1)}, u32[]{:S(2)}) copy-start(bf16[256,2048]{1,0:T(8,128)(2,1)} %param.8) | copy-start | bytes 3145732
  1.6 3.4 %copy-start.1 = (bf16[256,128]{1,0:T(8,128)(2,1)S(1)}, bf16[256,128]{1,0:T(8,128)(2,1)}, u32[]{:S(2)}) copy-start(bf16[256,128]{1,0:T(8,128)(2,1)} %w_ref.1) | copy-start | bytes 196612
  1.6 3.4 %copy-start.8 = (bf16[256,128]{1,0:T(8,128)(2,1)S(1)}, bf16[256,128]{1,0:T(8,128)(2,1)}, u32[]{:S(2)}) copy-start(bf16[256,128]{1,0:T(8,128)(2,1)} %param.13) | copy-start | bytes 196612
  1.6 1.8 %collective-permute-start.2 = (f32[64,256]{1,0:T(8,128)S(1)}, f32[64,256]{1,0:T(8,128)S(1)}, u32[]{:S(2)}, u32[]{:S(2)}) collective-permute-start(f32[64,256]{1,0:T(8,128)S(1)} %pad_maximum_fusion.10), channel_id=1, source_target_pairs={{0,1},{1,0},{2,3},{3,2},{4,5},{5,4},{6,7},{7,6},{8,9},{9,8},{10,11... | collective-permute-start | bytes 196616 | tf_op jit(solution)/shard_map/ppermute | solution.py:437
  3.1 1.4 %collective-permute-start = (bf16[256,256]{1,0:T(8,128)(2,1)S(1)}, bf16[256,256]{1,0:T(8,128)(2,1)S(1)}, u32[]{:S(2)}, u32[]{:S(2)}) collective-permute-start(bf16[256,256]{1,0:T(8,128)(2,1)S(1)} %pad_maximum_fusion.7), channel_id=1, source_target_pairs={{0,1},{1,0},{2,3},{3,2},{4,5},{5,4},{6,7},{7,6},{8,9},{9,8},{10,11... | collective-permute-start | bytes 393224 | tf_op jit(solution)/shard_map/ppermute | solution.py:437
  4.6 0.9 copy-start.4
  4.6 0.9 copy-start.5
  4.7 6.2 %collective-permute-start.3 = (bf16[256,1024]{1,0:T(8,128)(2,1)S(1)}, bf16[256,1024]{1,0:T(8,128)(2,1)S(1)}, u32[]{:S(2)}, u32[]{:S(2)}) collective-permute-start(bf16[256,1024]{1,0:T(8,128)(2,1)S(1)} %constant_dynamic-slice_fusion.2), channel_id=1, source_target_pairs={{0,1},{1,0},{2,3},{3,2},{4,5},{5,4},{6,7},{7,6},{8,9},{9,8},{10,11... | collective-permute-start | bytes 1572872 | tf_op jit(solution)/shard_map/ppermute | solution.py:437
  5.1 6.2 %collective-permute-start.1 = (bf16[256,1280]{1,0:T(8,128)(2,1)S(1)}, bf16[256,1280]{1,0:T(8,128)(2,1)S(1)}, u32[]{:S(2)}, u32[]{:S(2)}) collective-permute-start(bf16[256,1280]{1,0:T(8,128)(2,1)S(1)} %pad_maximum_fusion.4), channel_id=1, source_target_pairs={{0,1},{1,0},{2,3},{3,2},{4,5},{5,4},{6,7},{7,6},{8,9},{9,8},{10,11... | collective-permute-start | bytes 1966088 | tf_op jit(solution)/shard_map/ppermute | solution.py:437
  5.5 16.7 %collective-permute-start.4 = (bf16[512,256]{1,0:T(8,128)(2,1)S(1)}, bf16[512,256]{1,0:T(8,128)(2,1)S(1)}, u32[]{:S(2)}, u32[]{:S(2)}) collective-permute-start(bf16[512,256]{1,0:T(8,128)(2,1)S(1)} %pad_maximum_fusion.5.kv_ref), channel_id=1, source_target_pairs={{0,4},{1,5},{2,6},{3,7},{4,0},{5,1},{6,2},{7,3},{8,12},{9,13},{10,... | collective-permute-start | bytes 786440 | tf_op jit(solution)/shard_map/ppermute | solution.py:437
  9.3 25.9 %collective-permute-start.6 = (bf16[512,256]{1,0:T(8,128)(2,1)S(1)}, bf16[512,256]{1,0:T(8,128)(2,1)S(1)}, u32[]{:S(2)}, u32[]{:S(2)}) collective-permute-start(bf16[512,256]{1,0:T(8,128)(2,1)S(1)} %pad_maximum_fusion.5.kv_ref), channel_id=1, source_target_pairs={{0,2},{1,3},{2,0},{3,1},{4,6},{5,7},{6,4},{7,5},{8,10},{9,11},{10,... | collective-permute-start | bytes 786440 | tf_op jit(solution)/shard_map/ppermute | solution.py:437
  13.7 20.8 %collective-permute-start.8 = (f16[144,1024]{1,0:T(8,128)(2,1)S(1)}, f16[144,1024]{1,0:T(8,128)(2,1)S(1)}, u32[]{:S(2)}, u32[]{:S(2)}) collective-permute-start(f16[144,1024]{1,0:T(8,128)(2,1)S(1)} %convert_element_type.72), channel_id=1, source_target_pairs={{0,4},{1,5},{2,6},{3,7},{4,0},{5,1},{6,2},{7,3},{8,12},{9,13},{10,... | collective-permute-start | bytes 884744 | tf_op jit(solution)/shard_map/ppermute | solution.py:437
  22.2 14.3 %collective-permute-start.5 = (bf16[512,256]{1,0:T(8,128)(2,1)S(1)}, bf16[512,256]{1,0:T(8,128)(2,1)S(1)}, u32[]{:S(2)}, u32[]{:S(2)}) collective-permute-start(bf16[512,256]{1,0:T(8,128)(2,1)S(1)} %collective-permute-done.4.kv_ref), channel_id=1, source_target_pairs={{0,2},{1,3},{2,0},{3,1},{4,6},{5,7},{6,4},{7,5},{8,10},{9,11},{10,... | collective-permute-start | bytes 786440 | tf_op jit(solution)/shard_map/ppermute | solution.py:437
  22.9 19.9 %collective-permute-start.7 = (f16[144,1024]{1,0:T(8,128)(2,1)S(1)}, f16[144,1024]{1,0:T(8,128)(2,1)S(1)}, u32[]{:S(2)}, u32[]{:S(2)}) collective-permute-start(f16[144,1024]{1,0:T(8,128)(2,1)S(1)} %convert_element_type.72), channel_id=1, source_target_pairs={{0,2},{1,3},{2,0},{3,1},{4,6},{5,7},{6,4},{7,5},{8,10},{9,11},{10,... | collective-permute-start | bytes 884744 | tf_op jit(solution)/shard_map/ppermute | solution.py:437
  34.5 13.1 %collective-permute-start.9 = (f16[144,1024]{1,0:T(8,128)(2,1)S(1)}, f16[144,1024]{1,0:T(8,128)(2,1)S(1)}, u32[]{:S(2)}, u32[]{:S(2)}) collective-permute-start(f16[144,1024]{1,0:T(8,128)(2,1)S(1)} %collective-permute-done.8), channel_id=1, source_target_pairs={{0,2},{1,3},{2,0},{3,1},{4,6},{5,7},{6,4},{7,5},{8,10},{9,11},{10,... | collective-permute-start | bytes 884744 | tf_op jit(solution)/shard_map/ppermute | solution.py:437
  49.4 8.1 %copy-start.2 = (f32[144,1024]{1,0:T(8,128)}, f32[144,1024]{1,0:T(8,128)S(1)}, u32[]{:S(2)}) copy-start(f32[144,1024]{1,0:T(8,128)S(1)} %get-tuple-element.68) | copy-start | bytes 1769476
  57.6 0.8 copy-start.6
  58.4 1.7 %collective-permute-start.13 = (f32[256,256]{1,0:T(8,128)S(1)}, f32[256,256]{1,0:T(8,128)}, u32[]{:S(2)}, u32[]{:S(2)}) collective-permute-start(f32[256,256]{1,0:T(8,128)S(1)} %constant_dynamic-slice_fusion.1), channel_id=1, source_target_pairs={{0,1},{1,0},{2,3},{3,2},{4,5},{5,4},{6,7},{7,6},{8,9},{9,8},{10,11... | collective-permute-start | bytes 786440 | tf_op jit(solution)/shard_map/ppermute | solution.py:437
  59.6 16.6 %collective-permute-start.16 = (f32[256,1024]{1,0:T(8,128)}, f32[256,1024]{1,0:T(8,128)}, u32[]{:S(2)}, u32[]{:S(2)}) collective-permute-start(f32[256,1024]{1,0:T(8,128)} %constant_dynamic-slice_fusion), channel_id=1, source_target_pairs={{0,1},{1,0},{2,3},{3,2},{4,5},{5,4},{6,7},{7,6},{8,9},{9,8},{10,11... | collective-permute-start | bytes 3145736 | tf_op jit(solution)/shard_map/ppermute | solution.py:437
  60.1 9.2 %copy-start.3 = (f32[144,1024]{1,0:T(8,128)S(1)}, f32[144,1024]{1,0:T(8,128)}, u32[]{:S(2)}) copy-start(f32[144,1024]{1,0:T(8,128)} %copy-done.2) | copy-start | bytes 1769476
  61.3 5.5 %collective-permute-start.14 = (f32[256,128]{1,0:T(8,128)S(1)}, f32[256,128]{1,0:T(8,128)S(1)}, u32[]{:S(2)}, u32[]{:S(2)}) collective-permute-start(f32[256,128]{1,0:T(8,128)S(1)} %slice.98), channel_id=1, source_target_pairs={{0,8},{8,0},{16,24},{24,16},{1,9},{9,1},{17,25},{25,17},{2,10},{10... | collective-permute-start | bytes 393224 | tf_op jit(solution)/shard_map/ppermute | solution.py:549
  66.9 8.6 %collective-permute-start.15 = (f32[256,128]{1,0:T(8,128)S(1)}, f32[256,128]{1,0:T(8,128)S(1)}, u32[]{:S(2)}, u32[]{:S(2)}) collective-permute-start(f32[256,128]{1,0:T(8,128)S(1)} %get-tuple-element.103), channel_id=1, source_target_pairs={{0,16},{8,24},{16,0},{24,8},{1,17},{9,25},{17,1},{25,9},{2,18},{10... | collective-permute-start | bytes 393224 | tf_op jit(solution)/shard_map/ppermute | solution.py:549
  69.3 13.0 %collective-permute-start.10 = (f16[144,1024]{1,0:T(8,128)(2,1)S(1)}, f16[144,1024]{1,0:T(8,128)(2,1)S(1)}, u32[]{:S(2)}, u32[]{:S(2)}) collective-permute-start(f16[144,1024]{1,0:T(8,128)(2,1)S(1)} %convert_element_type.82), channel_id=1, source_target_pairs={{0,2},{1,3},{2,0},{3,1},{4,6},{5,7},{6,4},{7,5},{8,10},{9,11},{10,... | collective-permute-start | bytes 884744 | tf_op jit(solution)/shard_map/ppermute | solution.py:437
  70.2 25.8 %collective-permute-start.11 = (f16[144,1024]{1,0:T(8,128)(2,1)S(1)}, f16[144,1024]{1,0:T(8,128)(2,1)S(1)}, u32[]{:S(2)}, u32[]{:S(2)}) collective-permute-start(f16[144,1024]{1,0:T(8,128)(2,1)S(1)} %convert_element_type.82), channel_id=1, source_target_pairs={{0,4},{1,5},{2,6},{3,7},{4,0},{5,1},{6,2},{7,3},{8,12},{9,13},{10,... | collective-permute-start | bytes 884744 | tf_op jit(solution)/shard_map/ppermute | solution.py:437
  75.4 20.5 %collective-permute-start.12 = (f16[144,1024]{1,0:T(8,128)(2,1)S(1)}, f16[144,1024]{1,0:T(8,128)(2,1)S(1)}, u32[]{:S(2)}, u32[]{:S(2)}) collective-permute-start(f16[144,1024]{1,0:T(8,128)(2,1)S(1)} %convert_element_type.82), channel_id=1, source_target_pairs={{0,6},{1,7},{2,4},{3,5},{4,2},{5,3},{6,0},{7,1},{8,14},{9,15},{10,... | collective-permute-start | bytes 884744 | tf_op jit(solution)/shard_map/ppermute | solution.py:437
  96.2 2.0 %collective-permute-start.17 = (f32[128,1024]{1,0:T(8,128)S(1)}, f32[128,1024]{1,0:T(8,128)S(1)}, u32[]{:S(2)}, u32[]{:S(2)}) collective-permute-start(f32[128,1024]{1,0:T(8,128)S(1)} %multiply_add_fusion), channel_id=1, source_target_pairs={{0,1},{1,0},{2,3},{3,2},{4,5},{5,4},{6,7},{7,6},{8,9},{9,8},{10,11... | collective-permute-start | bytes 1572872 | tf_op jit(solution)/shard_map/ppermute | solution.py:437
  99.1 5.6 %collective-permute-start.18 = (f32[256,128]{1,0:T(8,128)S(1)}, f32[256,128]{1,0:T(8,128)S(1)}, u32[]{:S(2)}, u32[]{:S(2)}) collective-permute-start(f32[256,128]{1,0:T(8,128)S(1)} %shard_map.121), channel_id=1, source_target_pairs={{0,8},{8,0},{16,24},{24,16},{1,9},{9,1},{17,25},{25,17},{2,10},{10... | collective-permute-start | bytes 393224 | tf_op jit(solution)/shard_map/ppermute | solution.py:549
  104.7 5.0 %collective-permute-start.19 = (f32[256,128]{1,0:T(8,128)S(1)}, f32[256,128]{1,0:T(8,128)S(1)}, u32[]{:S(2)}, u32[]{:S(2)}) collective-permute-start(f32[256,128]{1,0:T(8,128)S(1)} %add.170), channel_id=1, source_target_pairs={{0,16},{8,24},{16,0},{24,8},{1,17},{9,25},{17,1},{25,9},{2,18},{10... | collective-permute-start | bytes 393224 | tf_op jit(solution)/shard_map/ppermute | solution.py:549
where the time goes:
time: 113 us; the launch traced here: 110 us
  waiting for transfers between devices  51.5 us (46%)
  Pallas kernels  26.6 us (24%)
  starting transfers between devices  21.4 us (19%)
  other arithmetic  6.79 us (6%)
  local copies, waits for them, and re-layouts  2.97 us (3%)
  between operations  1.23 us (1%)
    ppermute x16, waiting for transfers between devices, swap(): return lax.ppermute(a, 'seq', [(i, i ^ bits) for i in range(count)])  41 us
    pallas_call x11, Pallas kernels, call(): pl.pallas_call(kernel, out_shape=shapes, in_specs=in_specs or [VM] * len(...  26.6 us
    ppermute x16, starting transfers between devices, swap(): return lax.ppermute(a, 'seq', [(i, i ^ bits) for i in range(count)])  16.5 us
    ppermute x4, waiting for transfers between devices, tp_sum(): a = a + lax.ppermute(a, 'tp', [(i, i ^ bit) for i in range(tp)])  10.5 us
    ppermute x4, starting transfers between devices, tp_sum(): a = a + lax.ppermute(a, 'tp', [(i, i ^ bit) for i in range(tp)])  4.88 us
  transfers between devices with their start and end apart: 20, of which 13 were waited for; matrix products, arithmetic and copies ran while one was open for 6% of the time, Pallas kernels for 15%

commit v1 on v0

--- a/solution.py
+++ b/solution.py
@@ -1,3 +1,4 @@
+import functools
 import math
 
 import jax
@@ -74,7 +75,8 @@
 def code_rows(state, extra):
     top = jnp.max(jnp.abs(state), axis=0, keepdims=True)
     power = jnp.ceil(jnp.log2(jnp.maximum(top, 1e-30)))
-    rest = jnp.zeros((15 - len(extra), state.shape[1]), F32)
+    used = sum(e.shape[0] for e in extra)
+    rest = jnp.zeros((15 - used, state.shape[1]), F32)
     return state * jnp.exp2(12.0 - power), jnp.concatenate([power, *extra, rest], axis=0)
 
 
@@ -119,6 +121,20 @@
     state = spread_row(jnp.exp(tots[1]), width) * parts[0] + parts[1]
     pieces = [p.astype(F32) for p in split3(spread_row(tots[0] + tots[1], width))]
     coded_ref[:n, :], coded_ref[n:, :] = code_rows(state, pieces)
+
+
+def merge_kernel(flag, own_ref, got_ref, out_ref, *, group):
+    n = own_ref.shape[0] - 16
+    used = 3 * group
+    own_rows = own_ref[n + 1 : n + 1 + used, :]
+    got_rows = got_ref[n + 1 : n + 1 + used, :]
+    own = own_ref[:n, :] * jnp.exp2(own_ref[n : n + 1, :] - 12.0)
+    got = got_ref[:n, :] * jnp.exp2(got_ref[n : n + 1, :] - 12.0)
+    own_fade = jnp.exp(jnp.sum(own_rows, axis=0, keepdims=True))
+    got_fade = jnp.exp(jnp.sum(got_rows, axis=0, keepdims=True))
+    earlier = flag[0] == 1
+    merged = own * jnp.where(earlier, 1.0, got_fade) + got * jnp.where(earlier, own_fade, 1.0)
+    out_ref[:n, :], out_ref[n:, :] = code_rows(merged, [own_rows, got_rows])
 
 
 def local_kernel(
@@ -453,7 +469,9 @@
             if d not in got:
                 low = d & -d
                 held, _ = lax.optimization_barrier((got[d - low], token))
-                got[d] = swap(held, 2 * low)
+                need = [c for c in range(chips) if c ^ d < c or c ^ low ^ d < c ^ low]
+                pairs = [(2 * c + k, 2 * (c ^ low) + k) for c in need for k in (0, 1)]
+                got[d] = lax.ppermute(held, "seq", pairs)
         return [got[d] for d in range(1, chips)]
 
     def kv_half(which):
@@ -479,8 +497,11 @@
         state_kernel, [((n, hc), F32), code, ((2 * t, hc), F32)], (xc, wc, lsc, ldc),
         flops=4 * mm,
     )
-    mine = coded.astype(F16)
-    states_near = near(mine)
+
+    def state_stage(coded, bit):
+        return swap(coded.astype(F16), 2 << bit).astype(F32)
+
+    stages = [state_stage(coded, 0)] if chips > 1 else []
     qh = qc // HD
     carry = [((qc, 2 * t), F32), ((qh, 2 * t), F32), ((qh, 2 * t), F32)]
     qs, *soft = call(
@@ -496,21 +517,38 @@
         scratch=[pltpu.VMEM((t, hc), F32), pltpu.VMEM((hh, t), F32), pltpu.VMEM((t, t), F32)],
         flops=8 * mm,
     )
+    for bit in range(1, chips.bit_length() - 1):
+        flag = jnp.reshape((chip >> (bit - 1)) % 2, (1,)).astype(jnp.int32)
+        (coded,) = call(
+            functools.partial(merge_kernel, group=1 << (bit - 1)), [code], (flag, coded, stages[-1]),
+            in_specs=[pl.BlockSpec(memory_space=pltpu.SMEM), VM, VM],
+        )
+        stages.append(state_stage(coded, bit))
+    decays = {}
+    for bit, got in enumerate(stages):
+        for m in range(1 << bit):
+            at = n + 1 + 3 * m
+            decays[(1 << bit) + m] = jnp.sum(got[at : at + 3], axis=0, keepdims=True)
+
+    def between(low, high, most):
+        out = jnp.zeros((1, hc), F32)
+        for m in range(1, most):
+            at = chip ^ m
+            out += jnp.where((at > low) & (at < high), decays[m], 0.0)
+        return out
+
+    incoming = jnp.zeros((n, hc), F32)
+    for bit, got in enumerate(stages):
+        fade = jnp.exp(between(-1, chip, 1 << bit))
+        incoming += decode(got, n, jnp.where((chip >> bit) % 2 == 1, fade, 0.0))
     far = relay(keys_near, soft[1])
-    states = relay(states_near, soft[1])
-    decays = [jnp.sum(f[n + 1 : n + 4].astype(F32), axis=0, keepdims=True) for f in states]
-
-    def weight(d, later):
-        p = chip ^ d
-        low, high = (chip, p) if later else (p, chip)
-        between = jnp.zeros((1, hc), F32)
-        for m in range(1, chips):
-            at = chip ^ m
-            between += jnp.where((at > low) & (at < high), decays[m - 1], 0.0)
-        return jnp.where((p > chip) if later else (p < chip), jnp.exp(between), 0.0)
-
-    def combine(got, later):
-        return sum(decode(g, n, weight(d, later)) for d, g in enumerate(got, 1))
+
+    def combine(got):
+        out = 0.0
+        for d, g in enumerate(got, 1):
+            fade = jnp.exp(between(chip, chip ^ d, chips))
+            out += decode(g, n, jnp.where((chip ^ d) > chip, fade, 0.0))
+        return out
 
     for d, keys in enumerate(far, 1):
         flag = jnp.reshape((chip ^ d) < chip, (1,)).astype(jnp.int32)
@@ -520,7 +558,6 @@
             flops=4 * (2 * t) ** 2 * qc, alias={3: 0, 4: 1, 5: 2},
             in_specs=[pl.BlockSpec(memory_space=pltpu.SMEM)] + [VM] * 5,
         )
-    incoming = combine(states, False)
     res, d1, dcode = call(
         residual_kernel, [((2 * t, hc), F32), ((n, hc), F32), code],
         (ybase, soft[0], soft[2], rc, fs, incoming), flops=8 * mm,
@@ -555,8 +592,7 @@
     grads = own + other
     gw0, gr0 = grads[:, :n], grads[:, n:]
     grad_read = tp_sum(gr0)
-    *coming, grad_read, wexp, back_all = lax.optimization_barrier((*coming, grad_read, wexp, back_all))
-    arriving = combine(coming, True)
+    arriving = combine(coming)
     arrived = joined(arriving, swap(arriving, 1), 1)
     (gwp,) = call(write_kernel, [((t, n), F32)], (xh, xl, arrived, gw0), flops=4 * mm)
     grad_write = tp_sum(gwp)

time: 113 us -> 110 us (0.973)
  the two profiles are of different devices: /device:TPU:0 before, /device:TPU:8 now
where the time goes in v1:
time: 110 us
  waiting for transfers between devices  46.7 us (42%)
  Pallas kernels  30.3 us (28%)
  starting transfers between devices  25.3 us (23%)
  other arithmetic  5.18 us (5%)
  local copies, waits for them, and re-layouts  1.3 us (1%)
  between operations  1.15 us (1%)
    ppermute x14, waiting for transfers between devices, swap(): return lax.ppermute(a, 'seq', [(i, i ^ bits) for i in range(count)])  38.5 us
    pallas_call x12, Pallas kernels, call(): pl.pallas_call(kernel, out_shape=shapes, in_specs=in_specs or [VM] * len(...  30.3 us
    ppermute x14, starting transfers between devices, swap(): return lax.ppermute(a, 'seq', [(i, i ^ bits) for i in range(count)])  19.3 us
    ppermute x4, waiting for transfers between devices, tp_sum(): a = a + lax.ppermute(a, 'tp', [(i, i ^ bit) for i in range(tp)])  8.18 us
    ppermute x4, starting transfers between devices, tp_sum(): a = a + lax.ppermute(a, 'tp', [(i, i ^ bit) for i in range(tp)])  5.28 us
  transfers between devices with their start and end apart: 19, of which 12 were waited for; matrix products, arithmetic and copies ran while one was open for 4% of the time, Pallas kernels for 26%

profile of v1, /device:TPU:8, one launch (start us, length us, event | category | flops | bytes accessed | tf_op | source)
XLA Modules:
  0.0 109.8 jit_solution(15805741374294535854)
XLA Ops:
  0.7 0.9 pad_maximum_fusion.10
  1.6 0.0 copy-start.5
  1.6 1.0 constant_dynamic-slice_fusion.6
  2.6 0.5 collective-permute-start
  3.2 0.1 slice_reduce_fusion.3
  3.3 0.8 dynamic-slice_select_fusion.3
  4.0 0.1 collective-permute-done
  4.2 0.1 broadcast_select_fusion.7
  4.3 0.4 collective-permute-start.3
  4.7 2.6 %collective-permute-start.4 = (bf16[512,256]{1,0:T(8,128)(2,1)S(1)}, bf16[512,256]{1,0:T(8,128)(2,1)S(1)}, u32[]{:S(2)}, u32[]{:S(2)}) collective-permute-start(bf16[512,256]{1,0:T(8,128)(2,1)S(1)} %pad_maximum_fusion.5.kv_ref), channel_id=1, source_target_pairs={{0,4},{1,5},{2,6},{3,7},{4,0},{5,1},{6,2},{7,3},{8,12},{9,13},{10,... | collective-permute-start | bytes 786440 | tf_op jit(solution)/shard_map/ppermute | solution.py:453
  7.3 0.4 collective-permute-start.6
  7.9 0.1 pad_maximum_fusion.4
  7.9 0.1 collective-permute-start.1
  8.0 0.2 broadcast_select_fusion.1
  8.3 0.1 pad_maximum_fusion.2.q_ref
  8.3 3.1 %shard_map.113 = (bf16[512,2048]{1,0:T(8,128)(2,1)S(1)}, f32[1024,512]{1,0:T(8,128)S(1)}, f32[8,512]{1,0:T(8,128)S(1)}, f32[8,512]{1,0:T(8,128)S(1)}) custom-call(bf16[512,1024]{1,0:T(8,128)(2,1)S(1)} %pad_maximum_fusion.2.q_ref, bf16[512,256]{1,0:T(8,128)(2,1)S(1)} %pad_maximum_fusion.5.kv_ref), custom_call_target="tpu_custom_call" | custom-call | flops 1073741824 | bytes 1310720 | tf_op jit(solution)/shard_map/pallas_call | solution.py:420
  11.5 7.3 %collective-permute-done.4.kv_ref = bf16[512,256]{1,0:T(8,128)(2,1)S(1)} collective-permute-done((bf16[512,256]{1,0:T(8,128)(2,1)S(1)}, bf16[512,256]{1,0:T(8,128)(2,1)S(1)}, u32[]{:S(2)}, u32[]{:S(2)}) %collective-permute-start.4) | collective-permute-done | bytes 262176 | tf_op jit(solution)/shard_map/ppermute | solution.py:453
  18.8 0.7 collective-permute-start.5
  19.4 0.4 collective-permute-done.6.kv_ref
  19.8 3.9 %shard_map.114 = (f32[1024,512]{1,0:T(8,128)S(1)}, f32[8,512]{1,0:T(8,128)S(1)}, f32[8,512]{1,0:T(8,128)S(1)}) custom-call(s32[1]{0:T(128)} %bitcast.2.flag, bf16[512,2048]{1,0:T(8,128)(2,1)S(1)} %get-tuple-element.45.qs_ref, bf16[512,256]{1,0:T(8,128)(2,1)S(1)} %collective-permute-done.6.kv_ref, ...), custom_call_target="tpu_custom_call", output_to_operand_aliasing={{0}: (3, {}), {1}: (4, {}), {2}: (5, {})} | custom-call | flops 1073741824 | bytes 4489220 | tf_op jit(solution)/shard_map/pallas_call | solution.py:420
  23.8 0.3 shard_map.115
  24.1 0.3 broadcast_select_fusion.3
  24.4 0.1 pad_maximum_fusion.1.x_ref
  24.5 2.0 %shard_map.111 = (f32[128,1024]{1,0:T(8,128)S(1)}, f32[144,1024]{1,0:T(8,128)S(1)}, f32[512,1024]{1,0:T(8,128)S(1)}) custom-call(bf16[512,1024]{1,0:T(8,128)(2,1)S(1)} %pad_maximum_fusion.1.x_ref, bf16[512,128]{1,0:T(8,128)(2,1)S(1)} %pad_maximum_fusion.8.w_ref, f32[16,512]{1,0:T(8,128)S(1)} %pad_maximum_fusion.11.ls_ref, ...), custom_call_target="tpu_custom_call" | custom-call | flops 536870912 | bytes 1245184 | tf_op jit(solution)/shard_map/pallas_call | solution.py:420
  26.5 0.1 collective-permute-start.7
  26.6 6.9 %shard_map.112 = (f32[512,1024]{1,0:T(8,128)S(1)}, f32[512,1024]{1,0:T(8,128)S(1)}, f32[512,1024]{1,0:T(8,128)S(1)}, f32[16,512]{1,0:T(8,128)S(1)}) custom-call(bf16[512,1024]{1,0:T(8,128)(2,1)S(1)} %pad_maximum_fusion.1.x_ref, bf16[512,128]{1,0:T(8,128)(2,1)S(1)} %pad_maximum_fusion.8.w_ref, bf16[512,128]{1,0:T(8,128)(2,1)S(1)} %pad_maximum_fusion.9.r_ref, ...), custom_call_target="tpu_custom_call" | custom-call | flops 1073741824 | bytes 1900544 | tf_op jit(solution)/shard_map/pallas_call | solution.py:420
  33.5 0.5 shard_map.116
  34.0 1.2 %collective-permute-done.7 = f16[144,1024]{1,0:T(8,128)(2,1)S(1)} collective-permute-done((f16[144,1024]{1,0:T(8,128)(2,1)S(1)}, f16[144,1024]{1,0:T(8,128)(2,1)S(1)}, u32[]{:S(2)}, u32[]{:S(2)}) %collective-permute-start.7) | collective-permute-done | bytes 294944 | tf_op jit(solution)/shard_map/ppermute | solution.py:453
  35.2 0.2 shard_map.117
  35.5 10.5 %collective-permute-start.8 = (f16[144,1024]{1,0:T(8,128)(2,1)S(1)}, f16[144,1024]{1,0:T(8,128)(2,1)S(1)}, u32[]{:S(2)}, u32[]{:S(2)}) collective-permute-start(f16[144,1024]{1,0:T(8,128)(2,1)S(1)} %convert_element_type.56), channel_id=1, source_target_pairs={{0,4},{1,5},{2,6},{3,7},{4,0},{5,1},{6,2},{7,3},{8,12},{9,13},{10,... | collective-permute-start | bytes 884744 | tf_op jit(solution)/shard_map/ppermute | solution.py:453
  46.1 12.7 %collective-permute-done.8 = f16[144,1024]{1,0:T(8,128)(2,1)S(1)} collective-permute-done((f16[144,1024]{1,0:T(8,128)(2,1)S(1)}, f16[144,1024]{1,0:T(8,128)(2,1)S(1)}, u32[]{:S(2)}, u32[]{:S(2)}) %collective-permute-start.8) | collective-permute-done | bytes 294944 | tf_op jit(solution)/shard_map/ppermute | solution.py:453
  58.9 0.1 fusion.sin_ref
  59.1 1.4 %shard_map.118 = (f32[512,1024]{1,0:T(8,128)S(1)}, f32[128,1024]{1,0:T(8,128)S(1)}, f32[144,1024]{1,0:T(8,128)S(1)}) custom-call(f32[512,1024]{1,0:T(8,128)S(1)} %get-tuple-element.43.y_ref, f32[1024,512]{1,0:T(8,128)S(1)} %get-tuple-element.56.acc_ref, f32[8,512]{1,0:T(8,128)S(1)} %get-tuple-element.57.l_ref, bf16[512,128]{1,0:T(8,128)(2,1)S(1)} %pad_maximum_fusion.9.r_ref, ...), custom_call_target="tpu_custom_call" | custom-call | flops 1073741824 | bytes 6963200 | tf_op jit(solution)/shard_map/pallas_call | solution.py:420
  60.5 2.3 %collective-permute-start.10 = (f16[144,1024]{1,0:T(8,128)(2,1)S(1)}, f16[144,1024]{1,0:T(8,128)(2,1)S(1)}, u32[]{:S(2)}, u32[]{:S(2)}) collective-permute-start(f16[144,1024]{1,0:T(8,128)(2,1)S(1)} %convert_element_type.58), channel_id=1, source_target_pairs={{0,2},{1,3},{2,0},{3,1},{4,6},{5,7},{6,4},{7,5},{8,10},{9,11},{10,... | collective-permute-start | bytes 884744 | tf_op jit(solution)/shard_map/ppermute | solution.py:453
  62.8 1.3 %collective-permute-start.11 = (f16[144,1024]{1,0:T(8,128)(2,1)S(1)}, f16[144,1024]{1,0:T(8,128)(2,1)S(1)}, u32[]{:S(2)}, u32[]{:S(2)}) collective-permute-start(f16[144,1024]{1,0:T(8,128)(2,1)S(1)} %convert_element_type.58), channel_id=1, source_target_pairs={{0,4},{1,5},{2,6},{3,7},{4,0},{5,1},{6,2},{7,3},{8,12},{9,13},{10,... | collective-permute-start | bytes 884744 | tf_op jit(solution)/shard_map/ppermute | solution.py:453
  64.0 0.5 collective-permute-start.12
  64.5 8.1 %shard_map.119 = (f32[512,1024]{1,0:T(8,128)S(1)}, f32[512,128]{1,0:T(8,128)S(1)}, f32[512,128]{1,0:T(8,128)S(1)}) custom-call(f32[512,1024]{1,0:T(8,128)S(1)} %get-tuple-element.60.res_ref, bf16[512,1024]{1,0:T(8,128)(2,1)S(1)} %pad_maximum_fusion.1.x_ref, bf16[512,128]{1,0:T(8,128)(2,1)S(1)} %pad_maximum_fusion.8.w_ref, ...), custom_call_target="tpu_custom_call" | custom-call | flops 2147483648 | bytes 11304960 | tf_op jit(solution)/shard_map/pallas_call | solution.py:420
  72.7 0.1 collective-permute-start.14
  72.8 0.0 copy-start.2
  72.8 0.0 copy-start.3
  72.8 0.1 constant_dynamic-slice_fusion.1
  72.9 0.5 collective-permute-start.9
  73.5 1.4 %collective-permute-done.10 = f16[144,1024]{1,0:T(8,128)(2,1)S(1)} collective-permute-done((f16[144,1024]{1,0:T(8,128)(2,1)S(1)}, f16[144,1024]{1,0:T(8,128)(2,1)S(1)}, u32[]{:S(2)}, u32[]{:S(2)}) %collective-permute-start.10) | collective-permute-done | bytes 294944 | tf_op jit(solution)/shard_map/ppermute | solution.py:453
  74.8 9.3 %collective-permute-done.11 = f16[144,1024]{1,0:T(8,128)(2,1)S(1)} collective-permute-done((f16[144,1024]{1,0:T(8,128)(2,1)S(1)}, f16[144,1024]{1,0:T(8,128)(2,1)S(1)}, u32[]{:S(2)}, u32[]{:S(2)}) %collective-permute-start.11) | collective-permute-done | bytes 294944 | tf_op jit(solution)/shard_map/ppermute | solution.py:453
  84.1 6.1 %collective-permute-done.12 = f16[144,1024]{1,0:T(8,128)(2,1)S(1)} collective-permute-done((f16[144,1024]{1,0:T(8,128)(2,1)S(1)}, f16[144,1024]{1,0:T(8,128)(2,1)S(1)}, u32[]{:S(2)}, u32[]{:S(2)}) %collective-permute-start.12) | collective-permute-done | bytes 294944 | tf_op jit(solution)/shard_map/ppermute | solution.py:453
  90.3 0.2 multiply_add_fusion
  90.4 0.1 collective-permute-start.13
  90.6 1.6 %collective-permute-start.17 = (f32[256,128]{1,0:T(8,128)S(1)}, f32[256,128]{1,0:T(8,128)S(1)}, u32[]{:S(2)}, u32[]{:S(2)}) collective-permute-start(f32[256,128]{1,0:T(8,128)S(1)} %slice.95), channel_id=1, source_target_pairs={{0,8},{8,0},{16,24},{24,16},{1,9},{9,1},{17,25},{25,17},{2,10},{10... | collective-permute-start | bytes 393224 | tf_op jit(solution)/shard_map/ppermute | solution.py:586
  92.2 1.0 shard_map.120
  93.2 3.4 %collective-permute-done.17 = f32[256,128]{1,0:T(8,128)S(1)} collective-permute-done((f32[256,128]{1,0:T(8,128)S(1)}, f32[256,128]{1,0:T(8,128)S(1)}, u32[]{:S(2)}, u32[]{:S(2)}) %collective-permute-start.17) | collective-permute-done | bytes 131104 | tf_op jit(solution)/shard_map/ppermute | solution.py:586
  96.6 1.6 %collective-permute-start.18 = (f32[256,128]{1,0:T(8,128)S(1)}, f32[256,128]{1,0:T(8,128)S(1)}, u32[]{:S(2)}, u32[]{:S(2)}) collective-permute-start(f32[256,128]{1,0:T(8,128)S(1)} %get-tuple-element.90), channel_id=1, source_target_pairs={{0,16},{8,24},{16,0},{24,8},{1,17},{9,25},{17,1},{25,9},{2,18},{10... | collective-permute-start | bytes 393224 | tf_op jit(solution)/shard_map/ppermute | solution.py:586
  98.2 0.1 broadcast_select_fusion.5
  98.2 0.1 pad_maximum_fusion.3.g_ref
  98.3 0.7 shard_map.122
  99.1 1.6 %collective-permute-start.15 = (f32[256,128]{1,0:T(8,128)S(1)}, f32[256,128]{1,0:T(8,128)S(1)}, u32[]{:S(2)}, u32[]{:S(2)}) collective-permute-start(f32[256,128]{1,0:T(8,128)S(1)} %shard_map.122), channel_id=1, source_target_pairs={{0,8},{8,0},{16,24},{24,16},{1,9},{9,1},{17,25},{25,17},{2,10},{10... | collective-permute-start | bytes 393224 | tf_op jit(solution)/shard_map/ppermute | solution.py:586
  100.6 1.0 collective-permute-done.18
  101.7 0.7 add.133
  102.3 1.8 %collective-permute-done.15 = f32[256,128]{1,0:T(8,128)S(1)} collective-permute-done((f32[256,128]{1,0:T(8,128)S(1)}, f32[256,128]{1,0:T(8,128)S(1)}, u32[]{:S(2)}, u32[]{:S(2)}) %collective-permute-start.15) | collective-permute-done | bytes 131104 | tf_op jit(solution)/shard_map/ppermute | solution.py:586
  104.1 0.6 collective-permute-start.16
  104.7 0.2 dynamic-slice_select_fusion.1
  104.9 0.2 pad_maximum_fusion.back_ref
  105.1 2.1 %shard_map.121 = (f32[256,2048]{1,0:T(8,128)}, f32[32,256]{1,0:T(8,128)}) custom-call(f32[256,2048]{1,0:T(8,128)S(1)} %pad_maximum_fusion.back_ref, f32[256,2048]{1,0:T(8,128)S(1)} %get-tuple-element.66.wexp_ref, bf16[256,2048]{1,0:T(8,128)(2,1)S(1)} %copy-done, bf16[256,128]{1,0:T(8,128)(2,1)S(1)} %copy-done.1, f32[128,2048]{1,0:T(8,128)S(1)} %pad_maximum_fusion.3.g_ref), custom_call_target="tpu_custom_call" | custom-call | flops 1073741824 | bytes 6356992 | tf_op jit(solution)/shard_map/pallas_call | solution.py:420
  107.2 2.0 %collective-permute-done.16 = f32[256,128]{1,0:T(8,128)S(1)} collective-permute-done((f32[256,128]{1,0:T(8,128)S(1)}, f32[256,128]{1,0:T(8,128)S(1)}, u32[]{:S(2)}, u32[]{:S(2)}) %collective-permute-start.16) | collective-permute-done | bytes 131104 | tf_op jit(solution)/shard_map/ppermute | solution.py:586
  109.2 0.7 add.131
  (47 shorter events, 0.7 us)
Async XLA Ops:
  0.6 7.2 %copy-start = (bf16[256,2048]{1,0:T(8,128)(2,1)S(1)}, bf16[256,2048]{1,0:T(8,128)(2,1)}, u32[]{:S(2)}) copy-start(bf16[256,2048]{1,0:T(8,128)(2,1)} %x_ref.3) | copy-start | bytes 3145732
  0.6 3.6 %copy-start.4 = (bf16[256,2048]{1,0:T(8,128)(2,1)S(1)}, bf16[256,2048]{1,0:T(8,128)(2,1)}, u32[]{:S(2)}) copy-start(bf16[256,2048]{1,0:T(8,128)(2,1)} %param.8) | copy-start | bytes 3145732
  1.6 1.6 %collective-permute-start.2 = (f32[64,256]{1,0:T(8,128)S(1)}, f32[64,256]{1,0:T(8,128)S(1)}, u32[]{:S(2)}, u32[]{:S(2)}) collective-permute-start(f32[64,256]{1,0:T(8,128)S(1)} %pad_maximum_fusion.10), channel_id=1, source_target_pairs={{0,1},{1,0},{2,3},{3,2},{4,5},{5,4},{6,7},{7,6},{8,9},{9,8},{10,11... | collective-permute-start | bytes 196616 | tf_op jit(solution)/shard_map/ppermute | solution.py:453
  1.6 6.2 %copy-start.1 = (bf16[256,128]{1,0:T(8,128)(2,1)S(1)}, bf16[256,128]{1,0:T(8,128)(2,1)}, u32[]{:S(2)}) copy-start(bf16[256,128]{1,0:T(8,128)(2,1)} %w_ref.1) | copy-start | bytes 196612
  1.6 6.2 %copy-start.5 = (bf16[256,128]{1,0:T(8,128)(2,1)S(1)}, bf16[256,128]{1,0:T(8,128)(2,1)}, u32[]{:S(2)}) copy-start(bf16[256,128]{1,0:T(8,128)(2,1)} %param.13) | copy-start | bytes 196612
  2.6 1.5 %collective-permute-start = (bf16[256,256]{1,0:T(8,128)(2,1)S(1)}, bf16[256,256]{1,0:T(8,128)(2,1)S(1)}, u32[]{:S(2)}, u32[]{:S(2)}) collective-permute-start(bf16[256,256]{1,0:T(8,128)(2,1)S(1)} %pad_maximum_fusion.7), channel_id=1, source_target_pairs={{0,1},{1,0},{2,3},{3,2},{4,5},{5,4},{6,7},{7,6},{8,9},{9,8},{10,11... | collective-permute-start | bytes 393224 | tf_op jit(solution)/shard_map/ppermute | solution.py:453
  4.3 3.7 %collective-permute-start.3 = (bf16[256,1024]{1,0:T(8,128)(2,1)S(1)}, bf16[256,1024]{1,0:T(8,128)(2,1)S(1)}, u32[]{:S(2)}, u32[]{:S(2)}) collective-permute-start(bf16[256,1024]{1,0:T(8,128)(2,1)S(1)} %constant_dynamic-slice_fusion.2), channel_id=1, source_target_pairs={{0,1},{1,0},{2,3},{3,2},{4,5},{5,4},{6,7},{7,6},{8,9},{9,8},{10,11... | collective-permute-start | bytes 1572872 | tf_op jit(solution)/shard_map/ppermute | solution.py:453
  4.7 14.0 %collective-permute-start.4 = (bf16[512,256]{1,0:T(8,128)(2,1)S(1)}, bf16[512,256]{1,0:T(8,128)(2,1)S(1)}, u32[]{:S(2)}, u32[]{:S(2)}) collective-permute-start(bf16[512,256]{1,0:T(8,128)(2,1)S(1)} %pad_maximum_fusion.5.kv_ref), channel_id=1, source_target_pairs={{0,4},{1,5},{2,6},{3,7},{4,0},{5,1},{6,2},{7,3},{8,12},{9,13},{10,... | collective-permute-start | bytes 786440 | tf_op jit(solution)/shard_map/ppermute | solution.py:453
  7.3 12.5 %collective-permute-start.6 = (bf16[512,256]{1,0:T(8,128)(2,1)S(1)}, bf16[512,256]{1,0:T(8,128)(2,1)S(1)}, u32[]{:S(2)}, u32[]{:S(2)}) collective-permute-start(bf16[512,256]{1,0:T(8,128)(2,1)S(1)} %pad_maximum_fusion.5.kv_ref), channel_id=1, source_target_pairs={{0,2},{1,3},{2,0},{3,1},{4,6},{5,7},{6,4},{7,5},{8,10},{9,11},{10,... | collective-permute-start | bytes 786440 | tf_op jit(solution)/shard_map/ppermute | solution.py:453
  7.9 16.1 %collective-permute-start.1 = (bf16[256,1280]{1,0:T(8,128)(2,1)S(1)}, bf16[256,1280]{1,0:T(8,128)(2,1)S(1)}, u32[]{:S(2)}, u32[]{:S(2)}) collective-permute-start(bf16[256,1280]{1,0:T(8,128)(2,1)S(1)} %pad_maximum_fusion.4), channel_id=1, source_target_pairs={{0,1},{1,0},{2,3},{3,2},{4,5},{5,4},{6,7},{7,6},{8,9},{9,8},{10,11... | collective-permute-start | bytes 1966088 | tf_op jit(solution)/shard_map/ppermute | solution.py:453
  18.8 14.8 %collective-permute-start.5 = (bf16[512,256]{1,0:T(8,128)(2,1)S(1)}, bf16[512,256]{1,0:T(8,128)(2,1)S(1)}, u32[]{:S(2)}, u32[]{:S(2)}) collective-permute-start(bf16[512,256]{1,0:T(8,128)(2,1)S(1)} %collective-permute-done.4.kv_ref), channel_id=1, source_target_pairs={{4,6},{5,7},{6,4},{7,5},{12,14},{13,15},{14,12},{15,13},{20,22},{2... | collective-permute-start | bytes 786440 | tf_op jit(solution)/shard_map/ppermute | solution.py:474
  26.5 8.7 %collective-permute-start.7 = (f16[144,1024]{1,0:T(8,128)(2,1)S(1)}, f16[144,1024]{1,0:T(8,128)(2,1)S(1)}, u32[]{:S(2)}, u32[]{:S(2)}) collective-permute-start(f16[144,1024]{1,0:T(8,128)(2,1)S(1)} %convert_element_type.54), channel_id=1, source_target_pairs={{0,2},{1,3},{2,0},{3,1},{4,6},{5,7},{6,4},{7,5},{8,10},{9,11},{10,... | collective-permute-start | bytes 884744 | tf_op jit(solution)/shard_map/ppermute | solution.py:453
  35.5 23.3 %collective-permute-start.8 = (f16[144,1024]{1,0:T(8,128)(2,1)S(1)}, f16[144,1024]{1,0:T(8,128)(2,1)S(1)}, u32[]{:S(2)}, u32[]{:S(2)}) collective-permute-start(f16[144,1024]{1,0:T(8,128)(2,1)S(1)} %convert_element_type.56), channel_id=1, source_target_pairs={{0,4},{1,5},{2,6},{3,7},{4,0},{5,1},{6,2},{7,3},{8,12},{9,13},{10,... | collective-permute-start | bytes 884744 | tf_op jit(solution)/shard_map/ppermute | solution.py:453
  60.5 14.3 %collective-permute-start.10 = (f16[144,1024]{1,0:T(8,128)(2,1)S(1)}, f16[144,1024]{1,0:T(8,128)(2,1)S(1)}, u32[]{:S(2)}, u32[]{:S(2)}) collective-permute-start(f16[144,1024]{1,0:T(8,128)(2,1)S(1)} %convert_element_type.58), channel_id=1, source_target_pairs={{0,2},{1,3},{2,0},{3,1},{4,6},{5,7},{6,4},{7,5},{8,10},{9,11},{10,... | collective-permute-start | bytes 884744 | tf_op jit(solution)/shard_map/ppermute | solution.py:453
  62.8 21.3 %collective-permute-start.11 = (f16[144,1024]{1,0:T(8,128)(2,1)S(1)}, f16[144,1024]{1,0:T(8,128)(2,1)S(1)}, u32[]{:S(2)}, u32[]{:S(2)}) collective-permute-start(f16[144,1024]{1,0:T(8,128)(2,1)S(1)} %convert_element_type.58), channel_id=1, source_target_pairs={{0,4},{1,5},{2,6},{3,7},{4,0},{5,1},{6,2},{7,3},{8,12},{9,13},{10,... | collective-permute-start | bytes 884744 | tf_op jit(solution)/shard_map/ppermute | solution.py:453
  64.0 26.2 %collective-permute-start.12 = (f16[144,1024]{1,0:T(8,128)(2,1)S(1)}, f16[144,1024]{1,0:T(8,128)(2,1)S(1)}, u32[]{:S(2)}, u32[]{:S(2)}) collective-permute-start(f16[144,1024]{1,0:T(8,128)(2,1)S(1)} %convert_element_type.58), channel_id=1, source_target_pairs={{0,6},{1,7},{2,4},{3,5},{4,2},{5,3},{6,0},{7,1},{8,14},{9,15},{10,... | collective-permute-start | bytes 884744 | tf_op jit(solution)/shard_map/ppermute | solution.py:453
  72.7 17.8 %collective-permute-start.14 = (f32[256,256]{1,0:T(8,128)S(1)}, f32[256,256]{1,0:T(8,128)S(1)}, u32[]{:S(2)}, u32[]{:S(2)}) collective-permute-start(f32[256,256]{1,0:T(8,128)S(1)} %constant_dynamic-slice_fusion), channel_id=1, source_target_pairs={{0,1},{1,0},{2,3},{3,2},{4,5},{5,4},{6,7},{7,6},{8,9},{9,8},{10,11... | collective-permute-start | bytes 786440 | tf_op jit(solution)/shard_map/ppermute | solution.py:453
  72.8 19.4 %copy-start.2 = (f32[32,256]{1,0:T(8,128)S(1)}, f32[32,256]{1,0:T(8,128)}, u32[]{:S(2)}) copy-start(f32[32,256]{1,0:T(8,128)} %ld_ref.1) | copy-start | bytes 98308
  72.8 19.4 %copy-start.3 = (f32[32,256]{1,0:T(8,128)S(1)}, f32[32,256]{1,0:T(8,128)}, u32[]{:S(2)}) copy-start(f32[32,256]{1,0:T(8,128)} %ls_ref.1) | copy-start | bytes 98308
  72.9 31.8 %collective-permute-start.9 = (f32[256,1024]{1,0:T(8,128)S(1)}, f32[256,1024]{1,0:T(8,128)S(1)}, u32[]{:S(2)}, u32[]{:S(2)}) collective-permute-start(f32[256,1024]{1,0:T(8,128)S(1)} %constant_dynamic-slice_fusion.1), channel_id=1, source_target_pairs={{0,1},{1,0},{2,3},{3,2},{4,5},{5,4},{6,7},{7,6},{8,9},{9,8},{10,11... | collective-permute-start | bytes 3145736 | tf_op jit(solution)/shard_map/ppermute | solution.py:453
  90.4 7.7 %collective-permute-start.13 = (f32[128,1024]{1,0:T(8,128)S(1)}, f32[128,1024]{1,0:T(8,128)S(1)}, u32[]{:S(2)}, u32[]{:S(2)}) collective-permute-start(f32[128,1024]{1,0:T(8,128)S(1)} %multiply_add_fusion), channel_id=1, source_target_pairs={{0,1},{1,0},{2,3},{3,2},{4,5},{5,4},{6,7},{7,6},{8,9},{9,8},{10,11... | collective-permute-start | bytes 1572872 | tf_op jit(solution)/shard_map/ppermute | solution.py:453
  90.6 6.0 %collective-permute-start.17 = (f32[256,128]{1,0:T(8,128)S(1)}, f32[256,128]{1,0:T(8,128)S(1)}, u32[]{:S(2)}, u32[]{:S(2)}) collective-permute-start(f32[256,128]{1,0:T(8,128)S(1)} %slice.95), channel_id=1, source_target_pairs={{0,8},{8,0},{16,24},{24,16},{1,9},{9,1},{17,25},{25,17},{2,10},{10... | collective-permute-start | bytes 393224 | tf_op jit(solution)/shard_map/ppermute | solution.py:586
  96.6 5.1 %collective-permute-start.18 = (f32[256,128]{1,0:T(8,128)S(1)}, f32[256,128]{1,0:T(8,128)S(1)}, u32[]{:S(2)}, u32[]{:S(2)}) collective-permute-start(f32[256,128]{1,0:T(8,128)S(1)} %get-tuple-element.90), channel_id=1, source_target_pairs={{0,16},{8,24},{16,0},{24,8},{1,17},{9,25},{17,1},{25,9},{2,18},{10... | collective-permute-start | bytes 393224 | tf_op jit(solution)/shard_map/ppermute | solution.py:586
  99.1 5.0 %collective-permute-start.15 = (f32[256,128]{1,0:T(8,128)S(1)}, f32[256,128]{1,0:T(8,128)S(1)}, u32[]{:S(2)}, u32[]{:S(2)}) collective-permute-start(f32[256,128]{1,0:T(8,128)S(1)} %shard_map.122), channel_id=1, source_target_pairs={{0,8},{8,0},{16,24},{24,16},{1,9},{9,1},{17,25},{25,17},{2,10},{10... | collective-permute-start | bytes 393224 | tf_op jit(solution)/shard_map/ppermute | solution.py:586
  104.1 5.0 %collective-permute-start.16 = (f32[256,128]{1,0:T(8,128)S(1)}, f32[256,128]{1,0:T(8,128)S(1)}, u32[]{:S(2)}, u32[]{:S(2)}) collective-permute-start(f32[256,128]{1,0:T(8,128)S(1)} %add.130), channel_id=1, source_target_pairs={{0,16},{8,24},{16,0},{24,8},{1,17},{9,25},{17,1},{25,9},{2,18},{10... | collective-permute-start | bytes 393224 | tf_op jit(solution)/shard_map/ppermute | solution.py:586

commit v2 on v1

--- a/solution.py
+++ b/solution.py
@@ -425,7 +425,7 @@
         scratch_shapes=list(scratch),
         input_output_aliases=alias or {},
         cost_estimate=pl.CostEstimate(flops=flops, bytes_accessed=moved, transcendentals=0),
-        compiler_params=pltpu.CompilerParams(vmem_limit_bytes=16 * 2**20),
+        compiler_params=pltpu.CompilerParams(vmem_limit_bytes=8 * 2**20),
     )(*args)
 
 
@@ -461,7 +461,10 @@
         return jnp.concatenate([a, b], axis=axis)
 
     def near(a):
-        return {1 << b: swap(a, 2 << b) for b in range(chips.bit_length() - 1)}
+        got = {}
+        for b in range(chips.bit_length() - 1):
+            got[1 << b] = swap(a, 2 << b)
+        return got
 
     def relay(got, token):
         got = dict(got)

time: 110 us -> 110 us (level)
  no operation moved by 1% of the time
where the time goes in v2:
time: 110 us
  waiting for transfers between devices  46.4 us (42%)
  Pallas kernels  30.4 us (28%)
  starting transfers between devices  25.3 us (23%)
  other arithmetic  5.27 us (5%)
  local copies, waits for them, and re-layouts  1.29 us (1%)
  between operations  1.16 us (1%)
    ppermute x14, waiting for transfers between devices, swap(): return lax.ppermute(a, 'seq', [(i, i ^ bits) for i in range(count)])  38.4 us
    pallas_call x12, Pallas kernels, call(): pl.pallas_call(kernel, out_shape=shapes, in_specs=in_specs or [VM] * len(...  30.4 us
    ppermute x14, starting transfers between devices, swap(): return lax.ppermute(a, 'seq', [(i, i ^ bits) for i in range(count)])  19.4 us
    ppermute x4, waiting for transfers between devices, tp_sum(): a = a + lax.ppermute(a, 'tp', [(i, i ^ bit) for i in range(tp)])  7.98 us
    ppermute x4, starting transfers between devices, tp_sum(): a = a + lax.ppermute(a, 'tp', [(i, i ^ bit) for i in range(tp)])  5.26 us
  transfers between devices with their start and end apart: 19, of which 12 were waited for; matrix products, arithmetic and copies ran while one was open for 4% of the time, Pallas kernels for 26%

profile of v2, /device:TPU:8, one launch (start us, length us, event | category | flops | bytes accessed | tf_op | source)
XLA Modules:
  0.0 109.8 jit_solution(13290559464848571865)
XLA Ops:
  0.7 0.9 pad_maximum_fusion.10
  1.6 0.0 copy-start.1
  1.6 0.0 copy-start.5
  1.6 1.0 constant_dynamic-slice_fusion.6
  2.6 0.5 collective-permute-start
  3.2 0.1 slice_reduce_fusion.3
  3.3 0.8 dynamic-slice_select_fusion.3
  4.0 0.1 collective-permute-done
  4.2 0.1 broadcast_select_fusion.7
  4.3 0.4 collective-permute-start.3
  4.7 2.6 %collective-permute-start.4 = (bf16[512,256]{1,0:T(8,128)(2,1)S(1)}, bf16[512,256]{1,0:T(8,128)(2,1)S(1)}, u32[]{:S(2)}, u32[]{:S(2)}) collective-permute-start(bf16[512,256]{1,0:T(8,128)(2,1)S(1)} %pad_maximum_fusion.5.kv_ref), channel_id=1, source_target_pairs={{0,4},{1,5},{2,6},{3,7},{4,0},{5,1},{6,2},{7,3},{8,12},{9,13},{10,... | collective-permute-start | bytes 786440 | tf_op jit(solution)/shard_map/ppermute | solution.py:453
  7.3 0.4 collective-permute-start.6
  7.9 0.1 pad_maximum_fusion.4
  7.9 0.1 collective-permute-start.1
  8.0 0.3 broadcast_select_fusion.1
  8.3 0.1 pad_maximum_fusion.2.q_ref
  8.4 3.1 %shard_map.113 = (bf16[512,2048]{1,0:T(8,128)(2,1)S(1)}, f32[1024,512]{1,0:T(8,128)S(1)}, f32[8,512]{1,0:T(8,128)S(1)}, f32[8,512]{1,0:T(8,128)S(1)}) custom-call(bf16[512,1024]{1,0:T(8,128)(2,1)S(1)} %pad_maximum_fusion.2.q_ref, bf16[512,256]{1,0:T(8,128)(2,1)S(1)} %pad_maximum_fusion.5.kv_ref), custom_call_target="tpu_custom_call" | custom-call | flops 1073741824 | bytes 1310720 | tf_op jit(solution)/shard_map/pallas_call | solution.py:420
  11.5 7.3 %collective-permute-done.4.kv_ref = bf16[512,256]{1,0:T(8,128)(2,1)S(1)} collective-permute-done((bf16[512,256]{1,0:T(8,128)(2,1)S(1)}, bf16[512,256]{1,0:T(8,128)(2,1)S(1)}, u32[]{:S(2)}, u32[]{:S(2)}) %collective-permute-start.4) | collective-permute-done | bytes 262176 | tf_op jit(solution)/shard_map/ppermute | solution.py:453
  18.8 0.7 collective-permute-start.5
  19.4 0.4 collective-permute-done.6.kv_ref
  19.8 3.9 %shard_map.114 = (f32[1024,512]{1,0:T(8,128)S(1)}, f32[8,512]{1,0:T(8,128)S(1)}, f32[8,512]{1,0:T(8,128)S(1)}) custom-call(s32[1]{0:T(128)} %bitcast.2.flag, bf16[512,2048]{1,0:T(8,128)(2,1)S(1)} %get-tuple-element.45.qs_ref, bf16[512,256]{1,0:T(8,128)(2,1)S(1)} %collective-permute-done.6.kv_ref, ...), custom_call_target="tpu_custom_call", output_to_operand_aliasing={{0}: (3, {}), {1}: (4, {}), {2}: (5, {})} | custom-call | flops 1073741824 | bytes 4489220 | tf_op jit(solution)/shard_map/pallas_call | solution.py:420
  23.8 0.3 shard_map.115
  24.1 0.3 broadcast_select_fusion.3
  24.4 0.1 pad_maximum_fusion.1.x_ref
  24.5 2.0 %shard_map.111 = (f32[128,1024]{1,0:T(8,128)S(1)}, f32[144,1024]{1,0:T(8,128)S(1)}, f32[512,1024]{1,0:T(8,128)S(1)}) custom-call(bf16[512,1024]{1,0:T(8,128)(2,1)S(1)} %pad_maximum_fusion.1.x_ref, bf16[512,128]{1,0:T(8,128)(2,1)S(1)} %pad_maximum_fusion.8.w_ref, f32[16,512]{1,0:T(8,128)S(1)} %pad_maximum_fusion.11.ls_ref, ...), custom_call_target="tpu_custom_call" | custom-call | flops 536870912 | bytes 1245184 | tf_op jit(solution)/shard_map/pallas_call | solution.py:420
  26.5 0.1 collective-permute-start.7
  26.6 6.9 %shard_map.112 = (f32[512,1024]{1,0:T(8,128)S(1)}, f32[512,1024]{1,0:T(8,128)S(1)}, f32[512,1024]{1,0:T(8,128)S(1)}, f32[16,512]{1,0:T(8,128)S(1)}) custom-call(bf16[512,1024]{1,0:T(8,128)(2,1)S(1)} %pad_maximum_fusion.1.x_ref, bf16[512,128]{1,0:T(8,128)(2,1)S(1)} %pad_maximum_fusion.8.w_ref, bf16[512,128]{1,0:T(8,128)(2,1)S(1)} %pad_maximum_fusion.9.r_ref, ...), custom_call_target="tpu_custom_call" | custom-call | flops 1073741824 | bytes 1900544 | tf_op jit(solution)/shard_map/pallas_call | solution.py:420
  33.5 0.5 shard_map.116
  34.0 1.2 %collective-permute-done.7 = f16[144,1024]{1,0:T(8,128)(2,1)S(1)} collective-permute-done((f16[144,1024]{1,0:T(8,128)(2,1)S(1)}, f16[144,1024]{1,0:T(8,128)(2,1)S(1)}, u32[]{:S(2)}, u32[]{:S(2)}) %collective-permute-start.7) | collective-permute-done | bytes 294944 | tf_op jit(solution)/shard_map/ppermute | solution.py:453
  35.2 0.2 shard_map.117
  35.5 10.5 %collective-permute-start.8 = (f16[144,1024]{1,0:T(8,128)(2,1)S(1)}, f16[144,1024]{1,0:T(8,128)(2,1)S(1)}, u32[]{:S(2)}, u32[]{:S(2)}) collective-permute-start(f16[144,1024]{1,0:T(8,128)(2,1)S(1)} %convert_element_type.56), channel_id=1, source_target_pairs={{0,4},{1,5},{2,6},{3,7},{4,0},{5,1},{6,2},{7,3},{8,12},{9,13},{10,... | collective-permute-start | bytes 884744 | tf_op jit(solution)/shard_map/ppermute | solution.py:453
  46.1 12.7 %collective-permute-done.8 = f16[144,1024]{1,0:T(8,128)(2,1)S(1)} collective-permute-done((f16[144,1024]{1,0:T(8,128)(2,1)S(1)}, f16[144,1024]{1,0:T(8,128)(2,1)S(1)}, u32[]{:S(2)}, u32[]{:S(2)}) %collective-permute-start.8) | collective-permute-done | bytes 294944 | tf_op jit(solution)/shard_map/ppermute | solution.py:453
  58.9 0.1 fusion.sin_ref
  59.0 1.4 %shard_map.118 = (f32[512,1024]{1,0:T(8,128)S(1)}, f32[128,1024]{1,0:T(8,128)S(1)}, f32[144,1024]{1,0:T(8,128)S(1)}) custom-call(f32[512,1024]{1,0:T(8,128)S(1)} %get-tuple-element.43.y_ref, f32[1024,512]{1,0:T(8,128)S(1)} %get-tuple-element.56.acc_ref, f32[8,512]{1,0:T(8,128)S(1)} %get-tuple-element.57.l_ref, bf16[512,128]{1,0:T(8,128)(2,1)S(1)} %pad_maximum_fusion.9.r_ref, ...), custom_call_target="tpu_custom_call" | custom-call | flops 1073741824 | bytes 6963200 | tf_op jit(solution)/shard_map/pallas_call | solution.py:420
  60.5 2.3 %collective-permute-start.10 = (f16[144,1024]{1,0:T(8,128)(2,1)S(1)}, f16[144,1024]{1,0:T(8,128)(2,1)S(1)}, u32[]{:S(2)}, u32[]{:S(2)}) collective-permute-start(f16[144,1024]{1,0:T(8,128)(2,1)S(1)} %convert_element_type.58), channel_id=1, source_target_pairs={{0,2},{1,3},{2,0},{3,1},{4,6},{5,7},{6,4},{7,5},{8,10},{9,11},{10,... | collective-permute-start | bytes 884744 | tf_op jit(solution)/shard_map/ppermute | solution.py:453
  62.8 1.3 %collective-permute-start.11 = (f16[144,1024]{1,0:T(8,128)(2,1)S(1)}, f16[144,1024]{1,0:T(8,128)(2,1)S(1)}, u32[]{:S(2)}, u32[]{:S(2)}) collective-permute-start(f16[144,1024]{1,0:T(8,128)(2,1)S(1)} %convert_element_type.58), channel_id=1, source_target_pairs={{0,4},{1,5},{2,6},{3,7},{4,0},{5,1},{6,2},{7,3},{8,12},{9,13},{10,... | collective-permute-start | bytes 884744 | tf_op jit(solution)/shard_map/ppermute | solution.py:453
  64.0 0.5 collective-permute-start.12
  64.5 8.1 %shard_map.119 = (f32[512,1024]{1,0:T(8,128)S(1)}, f32[512,128]{1,0:T(8,128)S(1)}, f32[512,128]{1,0:T(8,128)S(1)}) custom-call(f32[512,1024]{1,0:T(8,128)S(1)} %get-tuple-element.60.res_ref, bf16[512,1024]{1,0:T(8,128)(2,1)S(1)} %pad_maximum_fusion.1.x_ref, bf16[512,128]{1,0:T(8,128)(2,1)S(1)} %pad_maximum_fusion.8.w_ref, ...), custom_call_target="tpu_custom_call" | custom-call | flops 2147483648 | bytes 11304960 | tf_op jit(solution)/shard_map/pallas_call | solution.py:420
  72.7 0.1 collective-permute-start.14
  72.8 0.0 copy-start.2
  72.8 0.1 constant_dynamic-slice_fusion.1
  72.9 0.5 collective-permute-start.9
  73.5 1.3 %collective-permute-done.10 = f16[144,1024]{1,0:T(8,128)(2,1)S(1)} collective-permute-done((f16[144,1024]{1,0:T(8,128)(2,1)S(1)}, f16[144,1024]{1,0:T(8,128)(2,1)S(1)}, u32[]{:S(2)}, u32[]{:S(2)}) %collective-permute-start.10) | collective-permute-done | bytes 294944 | tf_op jit(solution)/shard_map/ppermute | solution.py:453
  74.8 9.3 %collective-permute-done.11 = f16[144,1024]{1,0:T(8,128)(2,1)S(1)} collective-permute-done((f16[144,1024]{1,0:T(8,128)(2,1)S(1)}, f16[144,1024]{1,0:T(8,128)(2,1)S(1)}, u32[]{:S(2)}, u32[]{:S(2)}) %collective-permute-start.11) | collective-permute-done | bytes 294944 | tf_op jit(solution)/shard_map/ppermute | solution.py:453
  84.1 6.1 %collective-permute-done.12 = f16[144,1024]{1,0:T(8,128)(2,1)S(1)} collective-permute-done((f16[144,1024]{1,0:T(8,128)(2,1)S(1)}, f16[144,1024]{1,0:T(8,128)(2,1)S(1)}, u32[]{:S(2)}, u32[]{:S(2)}) %collective-permute-start.12) | collective-permute-done | bytes 294944 | tf_op jit(solution)/shard_map/ppermute | solution.py:453
  90.2 0.2 multiply_add_fusion
  90.4 0.1 collective-permute-start.13
  90.6 1.6 %collective-permute-start.17 = (f32[256,128]{1,0:T(8,128)S(1)}, f32[256,128]{1,0:T(8,128)S(1)}, u32[]{:S(2)}, u32[]{:S(2)}) collective-permute-start(f32[256,128]{1,0:T(8,128)S(1)} %slice.95), channel_id=1, source_target_pairs={{0,8},{8,0},{16,24},{24,16},{1,9},{9,1},{17,25},{25,17},{2,10},{10... | collective-permute-start | bytes 393224 | tf_op jit(solution)/shard_map/ppermute | solution.py:589
  92.1 1.0 shard_map.120
  93.1 3.4 %collective-permute-done.17 = f32[256,128]{1,0:T(8,128)S(1)} collective-permute-done((f32[256,128]{1,0:T(8,128)S(1)}, f32[256,128]{1,0:T(8,128)S(1)}, u32[]{:S(2)}, u32[]{:S(2)}) %collective-permute-start.17) | collective-permute-done | bytes 131104 | tf_op jit(solution)/shard_map/ppermute | solution.py:589
  96.5 1.6 %collective-permute-start.18 = (f32[256,128]{1,0:T(8,128)S(1)}, f32[256,128]{1,0:T(8,128)S(1)}, u32[]{:S(2)}, u32[]{:S(2)}) collective-permute-start(f32[256,128]{1,0:T(8,128)S(1)} %get-tuple-element.90), channel_id=1, source_target_pairs={{0,16},{8,24},{16,0},{24,8},{1,17},{9,25},{17,1},{25,9},{2,18},{10... | collective-permute-start | bytes 393224 | tf_op jit(solution)/shard_map/ppermute | solution.py:589
  98.1 0.1 broadcast_select_fusion.5
  98.2 0.1 pad_maximum_fusion.3.g_ref
  98.3 0.8 shard_map.122
  99.1 1.6 %collective-permute-start.15 = (f32[256,128]{1,0:T(8,128)S(1)}, f32[256,128]{1,0:T(8,128)S(1)}, u32[]{:S(2)}, u32[]{:S(2)}) collective-permute-start(f32[256,128]{1,0:T(8,128)S(1)} %shard_map.122), channel_id=1, source_target_pairs={{0,8},{8,0},{16,24},{24,16},{1,9},{9,1},{17,25},{25,17},{2,10},{10... | collective-permute-start | bytes 393224 | tf_op jit(solution)/shard_map/ppermute | solution.py:589
  100.6 1.0 collective-permute-done.18
  101.6 0.7 add.133
  102.3 1.8 %collective-permute-done.15 = f32[256,128]{1,0:T(8,128)S(1)} collective-permute-done((f32[256,128]{1,0:T(8,128)S(1)}, f32[256,128]{1,0:T(8,128)S(1)}, u32[]{:S(2)}, u32[]{:S(2)}) %collective-permute-start.15) | collective-permute-done | bytes 131104 | tf_op jit(solution)/shard_map/ppermute | solution.py:589
  104.1 0.6 collective-permute-start.16
  104.7 0.3 dynamic-slice_select_fusion.1
  105.0 0.1 pad_maximum_fusion.back_ref
  105.2 2.2 %shard_map.121 = (f32[256,2048]{1,0:T(8,128)}, f32[32,256]{1,0:T(8,128)}) custom-call(f32[256,2048]{1,0:T(8,128)S(1)} %pad_maximum_fusion.back_ref, f32[256,2048]{1,0:T(8,128)S(1)} %get-tuple-element.66.wexp_ref, bf16[256,2048]{1,0:T(8,128)(2,1)S(1)} %copy-done, bf16[256,128]{1,0:T(8,128)(2,1)S(1)} %copy-done.1, f32[128,2048]{1,0:T(8,128)S(1)} %pad_maximum_fusion.3.g_ref), custom_call_target="tpu_custom_call" | custom-call | flops 1073741824 | bytes 6356992 | tf_op jit(solution)/shard_map/pallas_call | solution.py:420
  107.4 1.8 %collective-permute-done.16 = f32[256,128]{1,0:T(8,128)S(1)} collective-permute-done((f32[256,128]{1,0:T(8,128)S(1)}, f32[256,128]{1,0:T(8,128)S(1)}, u32[]{:S(2)}, u32[]{:S(2)}) %collective-permute-start.16) | collective-permute-done | bytes 131104 | tf_op jit(solution)/shard_map/ppermute | solution.py:589
  109.1 0.7 add.131
  (47 shorter events, 0.7 us)
Async XLA Ops:
  0.6 7.2 %copy-start = (bf16[256,2048]{1,0:T(8,128)(2,1)S(1)}, bf16[256,2048]{1,0:T(8,128)(2,1)}, u32[]{:S(2)}) copy-start(bf16[256,2048]{1,0:T(8,128)(2,1)} %x_ref.3) | copy-start | bytes 3145732
  0.6 3.6 %copy-start.4 = (bf16[256,2048]{1,0:T(8,128)(2,1)S(1)}, bf16[256,2048]{1,0:T(8,128)(2,1)}, u32[]{:S(2)}) copy-start(bf16[256,2048]{1,0:T(8,128)(2,1)} %param.8) | copy-start | bytes 3145732
  1.6 1.6 %collective-permute-start.2 = (f32[64,256]{1,0:T(8,128)S(1)}, f32[64,256]{1,0:T(8,128)S(1)}, u32[]{:S(2)}, u32[]{:S(2)}) collective-permute-start(f32[64,256]{1,0:T(8,128)S(1)} %pad_maximum_fusion.10), channel_id=1, source_target_pairs={{0,1},{1,0},{2,3},{3,2},{4,5},{5,4},{6,7},{7,6},{8,9},{9,8},{10,11... | collective-permute-start | bytes 196616 | tf_op jit(solution)/shard_map/ppermute | solution.py:453
  1.6 6.2 %copy-start.1 = (bf16[256,128]{1,0:T(8,128)(2,1)S(1)}, bf16[256,128]{1,0:T(8,128)(2,1)}, u32[]{:S(2)}) copy-start(bf16[256,128]{1,0:T(8,128)(2,1)} %w_ref.1) | copy-start | bytes 196612
  1.6 6.2 %copy-start.5 = (bf16[256,128]{1,0:T(8,128)(2,1)S(1)}, bf16[256,128]{1,0:T(8,128)(2,1)}, u32[]{:S(2)}) copy-start(bf16[256,128]{1,0:T(8,128)(2,1)} %param.13) | copy-start | bytes 196612
  2.6 1.5 %collective-permute-start = (bf16[256,256]{1,0:T(8,128)(2,1)S(1)}, bf16[256,256]{1,0:T(8,128)(2,1)S(1)}, u32[]{:S(2)}, u32[]{:S(2)}) collective-permute-start(bf16[256,256]{1,0:T(8,128)(2,1)S(1)} %pad_maximum_fusion.7), channel_id=1, source_target_pairs={{0,1},{1,0},{2,3},{3,2},{4,5},{5,4},{6,7},{7,6},{8,9},{9,8},{10,11... | collective-permute-start | bytes 393224 | tf_op jit(solution)/shard_map/ppermute | solution.py:453
  4.3 3.7 %collective-permute-start.3 = (bf16[256,1024]{1,0:T(8,128)(2,1)S(1)}, bf16[256,1024]{1,0:T(8,128)(2,1)S(1)}, u32[]{:S(2)}, u32[]{:S(2)}) collective-permute-start(bf16[256,1024]{1,0:T(8,128)(2,1)S(1)} %constant_dynamic-slice_fusion.2), channel_id=1, source_target_pairs={{0,1},{1,0},{2,3},{3,2},{4,5},{5,4},{6,7},{7,6},{8,9},{9,8},{10,11... | collective-permute-start | bytes 1572872 | tf_op jit(solution)/shard_map/ppermute | solution.py:453
  4.7 14.0 %collective-permute-start.4 = (bf16[512,256]{1,0:T(8,128)(2,1)S(1)}, bf16[512,256]{1,0:T(8,128)(2,1)S(1)}, u32[]{:S(2)}, u32[]{:S(2)}) collective-permute-start(bf16[512,256]{1,0:T(8,128)(2,1)S(1)} %pad_maximum_fusion.5.kv_ref), channel_id=1, source_target_pairs={{0,4},{1,5},{2,6},{3,7},{4,0},{5,1},{6,2},{7,3},{8,12},{9,13},{10,... | collective-permute-start | bytes 786440 | tf_op jit(solution)/shard_map/ppermute | solution.py:453
  7.3 12.5 %collective-permute-start.6 = (bf16[512,256]{1,0:T(8,128)(2,1)S(1)}, bf16[512,256]{1,0:T(8,128)(2,1)S(1)}, u32[]{:S(2)}, u32[]{:S(2)}) collective-permute-start(bf16[512,256]{1,0:T(8,128)(2,1)S(1)} %pad_maximum_fusion.5.kv_ref), channel_id=1, source_target_pairs={{0,2},{1,3},{2,0},{3,1},{4,6},{5,7},{6,4},{7,5},{8,10},{9,11},{10,... | collective-permute-start | bytes 786440 | tf_op jit(solution)/shard_map/ppermute | solution.py:453
  7.9 16.2 %collective-permute-start.1 = (bf16[256,1280]{1,0:T(8,128)(2,1)S(1)}, bf16[256,1280]{1,0:T(8,128)(2,1)S(1)}, u32[]{:S(2)}, u32[]{:S(2)}) collective-permute-start(bf16[256,1280]{1,0:T(8,128)(2,1)S(1)} %pad_maximum_fusion.4), channel_id=1, source_target_pairs={{0,1},{1,0},{2,3},{3,2},{4,5},{5,4},{6,7},{7,6},{8,9},{9,8},{10,11... | collective-permute-start | bytes 1966088 | tf_op jit(solution)/shard_map/ppermute | solution.py:453
  18.8 14.8 %collective-permute-start.5 = (bf16[512,256]{1,0:T(8,128)(2,1)S(1)}, bf16[512,256]{1,0:T(8,128)(2,1)S(1)}, u32[]{:S(2)}, u32[]{:S(2)}) collective-permute-start(bf16[512,256]{1,0:T(8,128)(2,1)S(1)} %collective-permute-done.4.kv_ref), channel_id=1, source_target_pairs={{4,6},{5,7},{6,4},{7,5},{12,14},{13,15},{14,12},{15,13},{20,22},{2... | collective-permute-start | bytes 786440 | tf_op jit(solution)/shard_map/ppermute | solution.py:477
  26.5 8.7 %collective-permute-start.7 = (f16[144,1024]{1,0:T(8,128)(2,1)S(1)}, f16[144,1024]{1,0:T(8,128)(2,1)S(1)}, u32[]{:S(2)}, u32[]{:S(2)}) collective-permute-start(f16[144,1024]{1,0:T(8,128)(2,1)S(1)} %convert_element_type.54), channel_id=1, source_target_pairs={{0,2},{1,3},{2,0},{3,1},{4,6},{5,7},{6,4},{7,5},{8,10},{9,11},{10,... | collective-permute-start | bytes 884744 | tf_op jit(solution)/shard_map/ppermute | solution.py:453
  35.5 23.3 %collective-permute-start.8 = (f16[144,1024]{1,0:T(8,128)(2,1)S(1)}, f16[144,1024]{1,0:T(8,128)(2,1)S(1)}, u32[]{:S(2)}, u32[]{:S(2)}) collective-permute-start(f16[144,1024]{1,0:T(8,128)(2,1)S(1)} %convert_element_type.56), channel_id=1, source_target_pairs={{0,4},{1,5},{2,6},{3,7},{4,0},{5,1},{6,2},{7,3},{8,12},{9,13},{10,... | collective-permute-start | bytes 884744 | tf_op jit(solution)/shard_map/ppermute | solution.py:453
  60.5 14.3 %collective-permute-start.10 = (f16[144,1024]{1,0:T(8,128)(2,1)S(1)}, f16[144,1024]{1,0:T(8,128)(2,1)S(1)}, u32[]{:S(2)}, u32[]{:S(2)}) collective-permute-start(f16[144,1024]{1,0:T(8,128)(2,1)S(1)} %convert_element_type.58), channel_id=1, source_target_pairs={{0,2},{1,3},{2,0},{3,1},{4,6},{5,7},{6,4},{7,5},{8,10},{9,11},{10,... | collective-permute-start | bytes 884744 | tf_op jit(solution)/shard_map/ppermute | solution.py:453
  62.8 21.3 %collective-permute-start.11 = (f16[144,1024]{1,0:T(8,128)(2,1)S(1)}, f16[144,1024]{1,0:T(8,128)(2,1)S(1)}, u32[]{:S(2)}, u32[]{:S(2)}) collective-permute-start(f16[144,1024]{1,0:T(8,128)(2,1)S(1)} %convert_element_type.58), channel_id=1, source_target_pairs={{0,4},{1,5},{2,6},{3,7},{4,0},{5,1},{6,2},{7,3},{8,12},{9,13},{10,... | collective-permute-start | bytes 884744 | tf_op jit(solution)/shard_map/ppermute | solution.py:453
  64.0 26.2 %collective-permute-start.12 = (f16[144,1024]{1,0:T(8,128)(2,1)S(1)}, f16[144,1024]{1,0:T(8,128)(2,1)S(1)}, u32[]{:S(2)}, u32[]{:S(2)}) collective-permute-start(f16[144,1024]{1,0:T(8,128)(2,1)S(1)} %convert_element_type.58), channel_id=1, source_target_pairs={{0,6},{1,7},{2,4},{3,5},{4,2},{5,3},{6,0},{7,1},{8,14},{9,15},{10,... | collective-permute-start | bytes 884744 | tf_op jit(solution)/shard_map/ppermute | solution.py:453
  72.7 17.8 %collective-permute-start.14 = (f32[256,256]{1,0:T(8,128)S(1)}, f32[256,256]{1,0:T(8,128)S(1)}, u32[]{:S(2)}, u32[]{:S(2)}) collective-permute-start(f32[256,256]{1,0:T(8,128)S(1)} %constant_dynamic-slice_fusion), channel_id=1, source_target_pairs={{0,1},{1,0},{2,3},{3,2},{4,5},{5,4},{6,7},{7,6},{8,9},{9,8},{10,11... | collective-permute-start | bytes 786440 | tf_op jit(solution)/shard_map/ppermute | solution.py:453
  72.8 19.3 %copy-start.2 = (f32[32,256]{1,0:T(8,128)S(1)}, f32[32,256]{1,0:T(8,128)}, u32[]{:S(2)}) copy-start(f32[32,256]{1,0:T(8,128)} %ld_ref.1) | copy-start | bytes 98308
  72.8 19.3 %copy-start.3 = (f32[32,256]{1,0:T(8,128)S(1)}, f32[32,256]{1,0:T(8,128)}, u32[]{:S(2)}) copy-start(f32[32,256]{1,0:T(8,128)} %ls_ref.1) | copy-start | bytes 98308
  72.9 31.7 %collective-permute-start.9 = (f32[256,1024]{1,0:T(8,128)S(1)}, f32[256,1024]{1,0:T(8,128)S(1)}, u32[]{:S(2)}, u32[]{:S(2)}) collective-permute-start(f32[256,1024]{1,0:T(8,128)S(1)} %constant_dynamic-slice_fusion.1), channel_id=1, source_target_pairs={{0,1},{1,0},{2,3},{3,2},{4,5},{5,4},{6,7},{7,6},{8,9},{9,8},{10,11... | collective-permute-start | bytes 3145736 | tf_op jit(solution)/shard_map/ppermute | solution.py:453
  90.4 7.7 %collective-permute-start.13 = (f32[128,1024]{1,0:T(8,128)S(1)}, f32[128,1024]{1,0:T(8,128)S(1)}, u32[]{:S(2)}, u32[]{:S(2)}) collective-permute-start(f32[128,1024]{1,0:T(8,128)S(1)} %multiply_add_fusion), channel_id=1, source_target_pairs={{0,1},{1,0},{2,3},{3,2},{4,5},{5,4},{6,7},{7,6},{8,9},{9,8},{10,11... | collective-permute-start | bytes 1572872 | tf_op jit(solution)/shard_map/ppermute | solution.py:453
  90.6 5.9 %collective-permute-start.17 = (f32[256,128]{1,0:T(8,128)S(1)}, f32[256,128]{1,0:T(8,128)S(1)}, u32[]{:S(2)}, u32[]{:S(2)}) collective-permute-start(f32[256,128]{1,0:T(8,128)S(1)} %slice.95), channel_id=1, source_target_pairs={{0,8},{8,0},{16,24},{24,16},{1,9},{9,1},{17,25},{25,17},{2,10},{10... | collective-permute-start | bytes 393224 | tf_op jit(solution)/shard_map/ppermute | solution.py:589
  96.5 5.1 %collective-permute-start.18 = (f32[256,128]{1,0:T(8,128)S(1)}, f32[256,128]{1,0:T(8,128)S(1)}, u32[]{:S(2)}, u32[]{:S(2)}) collective-permute-start(f32[256,128]{1,0:T(8,128)S(1)} %get-tuple-element.90), channel_id=1, source_target_pairs={{0,16},{8,24},{16,0},{24,8},{1,17},{9,25},{17,1},{25,9},{2,18},{10... | collective-permute-start | bytes 393224 | tf_op jit(solution)/shard_map/ppermute | solution.py:589
  99.1 5.0 %collective-permute-start.15 = (f32[256,128]{1,0:T(8,128)S(1)}, f32[256,128]{1,0:T(8,128)S(1)}, u32[]{:S(2)}, u32[]{:S(2)}) collective-permute-start(f32[256,128]{1,0:T(8,128)S(1)} %shard_map.122), channel_id=1, source_target_pairs={{0,8},{8,0},{16,24},{24,16},{1,9},{9,1},{17,25},{25,17},{2,10},{10... | collective-permute-start | bytes 393224 | tf_op jit(solution)/shard_map/ppermute | solution.py:589
  104.1 5.0 %collective-permute-start.16 = (f32[256,128]{1,0:T(8,128)S(1)}, f32[256,128]{1,0:T(8,128)S(1)}, u32[]{:S(2)}, u32[]{:S(2)}) collective-permute-start(f32[256,128]{1,0:T(8,128)S(1)} %add.130), channel_id=1, source_target_pairs={{0,16},{8,24},{16,0},{24,8},{1,17},{9,25},{17,1},{25,9},{2,18},{10... | collective-permute-start | bytes 393224 | tf_op jit(solution)/shard_map/ppermute | solution.py:589

commit v3 on v2

--- a/solution.py
+++ b/solution.py
@@ -547,11 +547,14 @@
     far = relay(keys_near, soft[1])
 
     def combine(got):
-        out = 0.0
-        for d, g in enumerate(got, 1):
-            fade = jnp.exp(between(chip, chip ^ d, chips))
-            out += decode(g, n, jnp.where((chip ^ d) > chip, fade, 0.0))
-        return out
+        powers = jnp.concatenate([g[n : n + 1] for g in got], axis=0).astype(F32)
+        fades = [
+            jnp.where((chip ^ d) > chip, jnp.exp(between(chip, chip ^ d, chips)), 0.0)
+            for d in range(1, chips)
+        ]
+        fades, _ = lax.optimization_barrier((jnp.concatenate(fades, axis=0), soft[1]))
+        weights = lax.optimization_barrier(jnp.exp2(powers - 12.0) * fades)
+        return sum(g[:n].astype(F32) * weights[d : d + 1] for d, g in enumerate(got))
 
     for d, keys in enumerate(far, 1):
         flag = jnp.reshape((chip ^ d) < chip, (1,)).astype(jnp.int32)

time: 110 us -> 109 us (level)
  waiting for transfers between devices: 46.4 us -> 44.5 us
    ppermute x14, waiting for transfers between devices: 38.4 us -> 36.5 us  [swap(): return lax.ppermute(a, 'seq', [(i, i ^ bits) for i in range(count)])]
  transfers between devices with their start and end apart: 19 -> 19, of which waited for: 12 -> 11; matrix products, arithmetic and copies ran while one was open for 4% -> 4% of each run, Pallas kernels for 26% -> 26%
where the time goes in v3:
time: 109 us
  waiting for transfers between devices  44.5 us (41%)
  Pallas kernels  30.4 us (28%)
  starting transfers between devices  26.3 us (24%)
  other arithmetic  5.28 us (5%)
  local copies, waits for them, and re-layouts  1.33 us (1%)
  between operations  1.17 us (1%)
    ppermute x14, waiting for transfers between devices, swap(): return lax.ppermute(a, 'seq', [(i, i ^ bits) for i in range(count)])  36.5 us
    pallas_call x12, Pallas kernels, call(): pl.pallas_call(kernel, out_shape=shapes, in_specs=in_specs or [VM] * len(...  30.4 us
    ppermute x14, starting transfers between devices, swap(): return lax.ppermute(a, 'seq', [(i, i ^ bits) for i in range(count)])  20.4 us
    ppermute x4, waiting for transfers between devices, tp_sum(): a = a + lax.ppermute(a, 'tp', [(i, i ^ bit) for i in range(tp)])  7.99 us
    ppermute x4, starting transfers between devices, tp_sum(): a = a + lax.ppermute(a, 'tp', [(i, i ^ bit) for i in range(tp)])  5.26 us
  transfers between devices with their start and end apart: 19, of which 11 were waited for; matrix products, arithmetic and copies ran while one was open for 4% of the time, Pallas kernels for 26%

profile of v3, /device:TPU:8, one launch (start us, length us, event | category | flops | bytes accessed | tf_op | source)
XLA Modules:
  0.0 109.0 jit_solution(5721969383103185181)
XLA Ops:
  0.7 0.9 pad_maximum_fusion.10
  1.6 0.0 copy-start.1
  1.6 0.0 copy-start.5
  1.6 1.0 constant_dynamic-slice_fusion.6
  2.6 0.5 collective-permute-start
  3.2 0.1 slice_reduce_fusion.3
  3.3 0.8 dynamic-slice_select_fusion.3
  4.0 0.1 collective-permute-done
  4.2 0.1 broadcast_select_fusion.7
  4.3 0.4 collective-permute-start.3
  4.7 2.6 %collective-permute-start.4 = (bf16[512,256]{1,0:T(8,128)(2,1)S(1)}, bf16[512,256]{1,0:T(8,128)(2,1)S(1)}, u32[]{:S(2)}, u32[]{:S(2)}) collective-permute-start(bf16[512,256]{1,0:T(8,128)(2,1)S(1)} %pad_maximum_fusion.5.kv_ref), channel_id=1, source_target_pairs={{0,4},{1,5},{2,6},{3,7},{4,0},{5,1},{6,2},{7,3},{8,12},{9,13},{10,... | collective-permute-start | bytes 786440 | tf_op jit(solution)/shard_map/ppermute | solution.py:453
  7.3 0.4 collective-permute-start.6
  7.9 0.1 pad_maximum_fusion.4
  7.9 0.1 collective-permute-start.1
  8.0 0.3 broadcast_select_fusion.1
  8.3 0.1 pad_maximum_fusion.2.q_ref
  8.4 3.1 %shard_map.113 = (bf16[512,2048]{1,0:T(8,128)(2,1)S(1)}, f32[1024,512]{1,0:T(8,128)S(1)}, f32[8,512]{1,0:T(8,128)S(1)}, f32[8,512]{1,0:T(8,128)S(1)}) custom-call(bf16[512,1024]{1,0:T(8,128)(2,1)S(1)} %pad_maximum_fusion.2.q_ref, bf16[512,256]{1,0:T(8,128)(2,1)S(1)} %pad_maximum_fusion.5.kv_ref), custom_call_target="tpu_custom_call" | custom-call | flops 1073741824 | bytes 1310720 | tf_op jit(solution)/shard_map/pallas_call | solution.py:420
  11.5 7.3 %collective-permute-done.4.kv_ref = bf16[512,256]{1,0:T(8,128)(2,1)S(1)} collective-permute-done((bf16[512,256]{1,0:T(8,128)(2,1)S(1)}, bf16[512,256]{1,0:T(8,128)(2,1)S(1)}, u32[]{:S(2)}, u32[]{:S(2)}) %collective-permute-start.4) | collective-permute-done | bytes 262176 | tf_op jit(solution)/shard_map/ppermute | solution.py:453
  18.8 0.7 collective-permute-start.5
  19.4 0.4 collective-permute-done.6.kv_ref
  19.8 3.9 %shard_map.114 = (f32[1024,512]{1,0:T(8,128)S(1)}, f32[8,512]{1,0:T(8,128)S(1)}, f32[8,512]{1,0:T(8,128)S(1)}) custom-call(s32[1]{0:T(128)} %bitcast.2.flag, bf16[512,2048]{1,0:T(8,128)(2,1)S(1)} %get-tuple-element.45.qs_ref, bf16[512,256]{1,0:T(8,128)(2,1)S(1)} %collective-permute-done.6.kv_ref, ...), custom_call_target="tpu_custom_call", output_to_operand_aliasing={{0}: (3, {}), {1}: (4, {}), {2}: (5, {})} | custom-call | flops 1073741824 | bytes 4489220 | tf_op jit(solution)/shard_map/pallas_call | solution.py:420
  23.8 0.3 shard_map.115
  24.1 0.3 broadcast_select_fusion.3
  24.4 0.1 pad_maximum_fusion.1.x_ref
  24.5 2.0 %shard_map.111 = (f32[128,1024]{1,0:T(8,128)S(1)}, f32[144,1024]{1,0:T(8,128)S(1)}, f32[512,1024]{1,0:T(8,128)S(1)}) custom-call(bf16[512,1024]{1,0:T(8,128)(2,1)S(1)} %pad_maximum_fusion.1.x_ref, bf16[512,128]{1,0:T(8,128)(2,1)S(1)} %pad_maximum_fusion.8.w_ref, f32[16,512]{1,0:T(8,128)S(1)} %pad_maximum_fusion.11.ls_ref, ...), custom_call_target="tpu_custom_call" | custom-call | flops 536870912 | bytes 1245184 | tf_op jit(solution)/shard_map/pallas_call | solution.py:420
  26.5 0.1 collective-permute-start.7
  26.6 6.9 %shard_map.112 = (f32[512,1024]{1,0:T(8,128)S(1)}, f32[512,1024]{1,0:T(8,128)S(1)}, f32[512,1024]{1,0:T(8,128)S(1)}, f32[16,512]{1,0:T(8,128)S(1)}) custom-call(bf16[512,1024]{1,0:T(8,128)(2,1)S(1)} %pad_maximum_fusion.1.x_ref, bf16[512,128]{1,0:T(8,128)(2,1)S(1)} %pad_maximum_fusion.8.w_ref, bf16[512,128]{1,0:T(8,128)(2,1)S(1)} %pad_maximum_fusion.9.r_ref, ...), custom_call_target="tpu_custom_call" | custom-call | flops 1073741824 | bytes 1900544 | tf_op jit(solution)/shard_map/pallas_call | solution.py:420
  33.5 0.5 shard_map.116
  34.0 1.2 %collective-permute-done.7 = f16[144,1024]{1,0:T(8,128)(2,1)S(1)} collective-permute-done((f16[144,1024]{1,0:T(8,128)(2,1)S(1)}, f16[144,1024]{1,0:T(8,128)(2,1)S(1)}, u32[]{:S(2)}, u32[]{:S(2)}) %collective-permute-start.7) | collective-permute-done | bytes 294944 | tf_op jit(solution)/shard_map/ppermute | solution.py:453
  35.2 0.2 shard_map.117
  35.5 10.5 %collective-permute-start.8 = (f16[144,1024]{1,0:T(8,128)(2,1)S(1)}, f16[144,1024]{1,0:T(8,128)(2,1)S(1)}, u32[]{:S(2)}, u32[]{:S(2)}) collective-permute-start(f16[144,1024]{1,0:T(8,128)(2,1)S(1)} %convert_element_type.50), channel_id=1, source_target_pairs={{0,4},{1,5},{2,6},{3,7},{4,0},{5,1},{6,2},{7,3},{8,12},{9,13},{10,... | collective-permute-start | bytes 884744 | tf_op jit(solution)/shard_map/ppermute | solution.py:453
  46.1 12.7 %collective-permute-done.8 = f16[144,1024]{1,0:T(8,128)(2,1)S(1)} collective-permute-done((f16[144,1024]{1,0:T(8,128)(2,1)S(1)}, f16[144,1024]{1,0:T(8,128)(2,1)S(1)}, u32[]{:S(2)}, u32[]{:S(2)}) %collective-permute-start.8) | collective-permute-done | bytes 294944 | tf_op jit(solution)/shard_map/ppermute | solution.py:453
  58.9 0.1 fusion.sin_ref
  59.0 1.4 %shard_map.118 = (f32[512,1024]{1,0:T(8,128)S(1)}, f32[128,1024]{1,0:T(8,128)S(1)}, f32[144,1024]{1,0:T(8,128)S(1)}) custom-call(f32[512,1024]{1,0:T(8,128)S(1)} %get-tuple-element.43.y_ref, f32[1024,512]{1,0:T(8,128)S(1)} %get-tuple-element.56.acc_ref, f32[8,512]{1,0:T(8,128)S(1)} %get-tuple-element.57.l_ref, bf16[512,128]{1,0:T(8,128)(2,1)S(1)} %pad_maximum_fusion.9.r_ref, ...), custom_call_target="tpu_custom_call" | custom-call | flops 1073741824 | bytes 6963200 | tf_op jit(solution)/shard_map/pallas_call | solution.py:420
  60.5 3.5 %collective-permute-start.11 = (f16[144,1024]{1,0:T(8,128)(2,1)S(1)}, f16[144,1024]{1,0:T(8,128)(2,1)S(1)}, u32[]{:S(2)}, u32[]{:S(2)}) collective-permute-start(f16[144,1024]{1,0:T(8,128)(2,1)S(1)} %convert_element_type.52), channel_id=1, source_target_pairs={{0,4},{1,5},{2,6},{3,7},{4,0},{5,1},{6,2},{7,3},{8,12},{9,13},{10,... | collective-permute-start | bytes 884744 | tf_op jit(solution)/shard_map/ppermute | solution.py:453
  63.9 0.3 collective-permute-start.12
  64.2 1.3 %collective-permute-start.10 = (f16[144,1024]{1,0:T(8,128)(2,1)S(1)}, f16[144,1024]{1,0:T(8,128)(2,1)S(1)}, u32[]{:S(2)}, u32[]{:S(2)}) collective-permute-start(f16[144,1024]{1,0:T(8,128)(2,1)S(1)} %convert_element_type.52), channel_id=1, source_target_pairs={{0,2},{1,3},{2,0},{3,1},{4,6},{5,7},{6,4},{7,5},{8,10},{9,11},{10,... | collective-permute-start | bytes 884744 | tf_op jit(solution)/shard_map/ppermute | solution.py:453
  65.5 8.1 %shard_map.119 = (f32[512,1024]{1,0:T(8,128)S(1)}, f32[512,128]{1,0:T(8,128)S(1)}, f32[512,128]{1,0:T(8,128)S(1)}) custom-call(f32[512,1024]{1,0:T(8,128)S(1)} %get-tuple-element.60.res_ref, bf16[512,1024]{1,0:T(8,128)(2,1)S(1)} %pad_maximum_fusion.1.x_ref, bf16[512,128]{1,0:T(8,128)(2,1)S(1)} %pad_maximum_fusion.8.w_ref, ...), custom_call_target="tpu_custom_call" | custom-call | flops 2147483648 | bytes 11304960 | tf_op jit(solution)/shard_map/pallas_call | solution.py:420
  73.7 0.1 collective-permute-start.14
  73.8 0.0 copy-start.2
  73.8 0.0 copy-start.3
  73.8 0.1 constant_dynamic-slice_fusion.1
  73.9 0.6 collective-permute-start.9
  74.5 7.2 %collective-permute-done.11 = f16[144,1024]{1,0:T(8,128)(2,1)S(1)} collective-permute-done((f16[144,1024]{1,0:T(8,128)(2,1)S(1)}, f16[144,1024]{1,0:T(8,128)(2,1)S(1)}, u32[]{:S(2)}, u32[]{:S(2)}) %collective-permute-start.11) | collective-permute-done | bytes 294944 | tf_op jit(solution)/shard_map/ppermute | solution.py:453
  81.7 7.6 %collective-permute-done.12 = f16[144,1024]{1,0:T(8,128)(2,1)S(1)} collective-permute-done((f16[144,1024]{1,0:T(8,128)(2,1)S(1)}, f16[144,1024]{1,0:T(8,128)(2,1)S(1)}, u32[]{:S(2)}, u32[]{:S(2)}) %collective-permute-start.12) | collective-permute-done | bytes 294944 | tf_op jit(solution)/shard_map/ppermute | solution.py:453
  89.4 0.2 multiply_add_fusion
  89.6 0.1 collective-permute-start.13
  89.7 1.6 %collective-permute-start.17 = (f32[256,128]{1,0:T(8,128)S(1)}, f32[256,128]{1,0:T(8,128)S(1)}, u32[]{:S(2)}, u32[]{:S(2)}) collective-permute-start(f32[256,128]{1,0:T(8,128)S(1)} %slice.110), channel_id=1, source_target_pairs={{0,8},{8,0},{16,24},{24,16},{1,9},{9,1},{17,25},{25,17},{2,10},{10... | collective-permute-start | bytes 393224 | tf_op jit(solution)/shard_map/ppermute | solution.py:592
  91.3 1.0 shard_map.120
  92.3 3.4 %collective-permute-done.17 = f32[256,128]{1,0:T(8,128)S(1)} collective-permute-done((f32[256,128]{1,0:T(8,128)S(1)}, f32[256,128]{1,0:T(8,128)S(1)}, u32[]{:S(2)}, u32[]{:S(2)}) %collective-permute-start.17) | collective-permute-done | bytes 131104 | tf_op jit(solution)/shard_map/ppermute | solution.py:592
  95.7 1.6 %collective-permute-start.18 = (f32[256,128]{1,0:T(8,128)S(1)}, f32[256,128]{1,0:T(8,128)S(1)}, u32[]{:S(2)}, u32[]{:S(2)}) collective-permute-start(f32[256,128]{1,0:T(8,128)S(1)} %get-tuple-element.90), channel_id=1, source_target_pairs={{0,16},{8,24},{16,0},{24,8},{1,17},{9,25},{17,1},{25,9},{2,18},{10... | collective-permute-start | bytes 393224 | tf_op jit(solution)/shard_map/ppermute | solution.py:592
  97.3 0.1 broadcast_select_fusion.5
  97.4 0.1 pad_maximum_fusion.3.g_ref
  97.4 0.8 shard_map.122
  98.2 1.6 %collective-permute-start.15 = (f32[256,128]{1,0:T(8,128)S(1)}, f32[256,128]{1,0:T(8,128)S(1)}, u32[]{:S(2)}, u32[]{:S(2)}) collective-permute-start(f32[256,128]{1,0:T(8,128)S(1)} %shard_map.122), channel_id=1, source_target_pairs={{0,8},{8,0},{16,24},{24,16},{1,9},{9,1},{17,25},{25,17},{2,10},{10... | collective-permute-start | bytes 393224 | tf_op jit(solution)/shard_map/ppermute | solution.py:592
  99.8 1.0 collective-permute-done.18
  100.8 0.7 add.131
  101.5 1.8 %collective-permute-done.15 = f32[256,128]{1,0:T(8,128)S(1)} collective-permute-done((f32[256,128]{1,0:T(8,128)S(1)}, f32[256,128]{1,0:T(8,128)S(1)}, u32[]{:S(2)}, u32[]{:S(2)}) %collective-permute-start.15) | collective-permute-done | bytes 131104 | tf_op jit(solution)/shard_map/ppermute | solution.py:592
  103.3 0.6 collective-permute-start.16
  103.8 0.3 dynamic-slice_select_fusion.1
  104.1 0.1 pad_maximum_fusion.back_ref
  104.3 2.2 %shard_map.121 = (f32[256,2048]{1,0:T(8,128)}, f32[32,256]{1,0:T(8,128)}) custom-call(f32[256,2048]{1,0:T(8,128)S(1)} %pad_maximum_fusion.back_ref, f32[256,2048]{1,0:T(8,128)S(1)} %get-tuple-element.66.wexp_ref, bf16[256,2048]{1,0:T(8,128)(2,1)S(1)} %copy-done, bf16[256,128]{1,0:T(8,128)(2,1)S(1)} %copy-done.1, f32[128,2048]{1,0:T(8,128)S(1)} %pad_maximum_fusion.3.g_ref), custom_call_target="tpu_custom_call" | custom-call | flops 1073741824 | bytes 6356992 | tf_op jit(solution)/shard_map/pallas_call | solution.py:420
  106.5 1.8 %collective-permute-done.16 = f32[256,128]{1,0:T(8,128)S(1)} collective-permute-done((f32[256,128]{1,0:T(8,128)S(1)}, f32[256,128]{1,0:T(8,128)S(1)}, u32[]{:S(2)}, u32[]{:S(2)}) %collective-permute-start.16) | collective-permute-done | bytes 131104 | tf_op jit(solution)/shard_map/ppermute | solution.py:592
  108.3 0.7 add.129
  (50 shorter events, 0.8 us)
Async XLA Ops:
  0.6 7.2 %copy-start = (bf16[256,2048]{1,0:T(8,128)(2,1)S(1)}, bf16[256,2048]{1,0:T(8,128)(2,1)}, u32[]{:S(2)}) copy-start(bf16[256,2048]{1,0:T(8,128)(2,1)} %x_ref.3) | copy-start | bytes 3145732
  0.6 3.6 %copy-start.4 = (bf16[256,2048]{1,0:T(8,128)(2,1)S(1)}, bf16[256,2048]{1,0:T(8,128)(2,1)}, u32[]{:S(2)}) copy-start(bf16[256,2048]{1,0:T(8,128)(2,1)} %param.8) | copy-start | bytes 3145732
  1.6 1.6 %collective-permute-start.2 = (f32[64,256]{1,0:T(8,128)S(1)}, f32[64,256]{1,0:T(8,128)S(1)}, u32[]{:S(2)}, u32[]{:S(2)}) collective-permute-start(f32[64,256]{1,0:T(8,128)S(1)} %pad_maximum_fusion.10), channel_id=1, source_target_pairs={{0,1},{1,0},{2,3},{3,2},{4,5},{5,4},{6,7},{7,6},{8,9},{9,8},{10,11... | collective-permute-start | bytes 196616 | tf_op jit(solution)/shard_map/ppermute | solution.py:453
  1.6 6.2 %copy-start.1 = (bf16[256,128]{1,0:T(8,128)(2,1)S(1)}, bf16[256,128]{1,0:T(8,128)(2,1)}, u32[]{:S(2)}) copy-start(bf16[256,128]{1,0:T(8,128)(2,1)} %w_ref.1) | copy-start | bytes 196612
  1.6 6.2 %copy-start.5 = (bf16[256,128]{1,0:T(8,128)(2,1)S(1)}, bf16[256,128]{1,0:T(8,128)(2,1)}, u32[]{:S(2)}) copy-start(bf16[256,128]{1,0:T(8,128)(2,1)} %param.13) | copy-start | bytes 196612
  2.6 1.5 %collective-permute-start = (bf16[256,256]{1,0:T(8,128)(2,1)S(1)}, bf16[256,256]{1,0:T(8,128)(2,1)S(1)}, u32[]{:S(2)}, u32[]{:S(2)}) collective-permute-start(bf16[256,256]{1,0:T(8,128)(2,1)S(1)} %pad_maximum_fusion.7), channel_id=1, source_target_pairs={{0,1},{1,0},{2,3},{3,2},{4,5},{5,4},{6,7},{7,6},{8,9},{9,8},{10,11... | collective-permute-start | bytes 393224 | tf_op jit(solution)/shard_map/ppermute | solution.py:453
  4.3 3.7 %collective-permute-start.3 = (bf16[256,1024]{1,0:T(8,128)(2,1)S(1)}, bf16[256,1024]{1,0:T(8,128)(2,1)S(1)}, u32[]{:S(2)}, u32[]{:S(2)}) collective-permute-start(bf16[256,1024]{1,0:T(8,128)(2,1)S(1)} %constant_dynamic-slice_fusion.2), channel_id=1, source_target_pairs={{0,1},{1,0},{2,3},{3,2},{4,5},{5,4},{6,7},{7,6},{8,9},{9,8},{10,11... | collective-permute-start | bytes 1572872 | tf_op jit(solution)/shard_map/ppermute | solution.py:453
  4.7 14.0 %collective-permute-start.4 = (bf16[512,256]{1,0:T(8,128)(2,1)S(1)}, bf16[512,256]{1,0:T(8,128)(2,1)S(1)}, u32[]{:S(2)}, u32[]{:S(2)}) collective-permute-start(bf16[512,256]{1,0:T(8,128)(2,1)S(1)} %pad_maximum_fusion.5.kv_ref), channel_id=1, source_target_pairs={{0,4},{1,5},{2,6},{3,7},{4,0},{5,1},{6,2},{7,3},{8,12},{9,13},{10,... | collective-permute-start | bytes 786440 | tf_op jit(solution)/shard_map/ppermute | solution.py:453
  7.3 12.5 %collective-permute-start.6 = (bf16[512,256]{1,0:T(8,128)(2,1)S(1)}, bf16[512,256]{1,0:T(8,128)(2,1)S(1)}, u32[]{:S(2)}, u32[]{:S(2)}) collective-permute-start(bf16[512,256]{1,0:T(8,128)(2,1)S(1)} %pad_maximum_fusion.5.kv_ref), channel_id=1, source_target_pairs={{0,2},{1,3},{2,0},{3,1},{4,6},{5,7},{6,4},{7,5},{8,10},{9,11},{10,... | collective-permute-start | bytes 786440 | tf_op jit(solution)/shard_map/ppermute | solution.py:453
  7.9 16.2 %collective-permute-start.1 = (bf16[256,1280]{1,0:T(8,128)(2,1)S(1)}, bf16[256,1280]{1,0:T(8,128)(2,1)S(1)}, u32[]{:S(2)}, u32[]{:S(2)}) collective-permute-start(bf16[256,1280]{1,0:T(8,128)(2,1)S(1)} %pad_maximum_fusion.4), channel_id=1, source_target_pairs={{0,1},{1,0},{2,3},{3,2},{4,5},{5,4},{6,7},{7,6},{8,9},{9,8},{10,11... | collective-permute-start | bytes 1966088 | tf_op jit(solution)/shard_map/ppermute | solution.py:453
  18.8 14.8 %collective-permute-start.5 = (bf16[512,256]{1,0:T(8,128)(2,1)S(1)}, bf16[512,256]{1,0:T(8,128)(2,1)S(1)}, u32[]{:S(2)}, u32[]{:S(2)}) collective-permute-start(bf16[512,256]{1,0:T(8,128)(2,1)S(1)} %collective-permute-done.4.kv_ref), channel_id=1, source_target_pairs={{4,6},{5,7},{6,4},{7,5},{12,14},{13,15},{14,12},{15,13},{20,22},{2... | collective-permute-start | bytes 786440 | tf_op jit(solution)/shard_map/ppermute | solution.py:477
  26.5 8.7 %collective-permute-start.7 = (f16[144,1024]{1,0:T(8,128)(2,1)S(1)}, f16[144,1024]{1,0:T(8,128)(2,1)S(1)}, u32[]{:S(2)}, u32[]{:S(2)}) collective-permute-start(f16[144,1024]{1,0:T(8,128)(2,1)S(1)} %convert_element_type.48), channel_id=1, source_target_pairs={{0,2},{1,3},{2,0},{3,1},{4,6},{5,7},{6,4},{7,5},{8,10},{9,11},{10,... | collective-permute-start | bytes 884744 | tf_op jit(solution)/shard_map/ppermute | solution.py:453
  35.5 23.3 %collective-permute-start.8 = (f16[144,1024]{1,0:T(8,128)(2,1)S(1)}, f16[144,1024]{1,0:T(8,128)(2,1)S(1)}, u32[]{:S(2)}, u32[]{:S(2)}) collective-permute-start(f16[144,1024]{1,0:T(8,128)(2,1)S(1)} %convert_element_type.50), channel_id=1, source_target_pairs={{0,4},{1,5},{2,6},{3,7},{4,0},{5,1},{6,2},{7,3},{8,12},{9,13},{10,... | collective-permute-start | bytes 884744 | tf_op jit(solution)/shard_map/ppermute | solution.py:453
  60.5 21.2 %collective-permute-start.11 = (f16[144,1024]{1,0:T(8,128)(2,1)S(1)}, f16[144,1024]{1,0:T(8,128)(2,1)S(1)}, u32[]{:S(2)}, u32[]{:S(2)}) collective-permute-start(f16[144,1024]{1,0:T(8,128)(2,1)S(1)} %convert_element_type.52), channel_id=1, source_target_pairs={{0,4},{1,5},{2,6},{3,7},{4,0},{5,1},{6,2},{7,3},{8,12},{9,13},{10,... | collective-permute-start | bytes 884744 | tf_op jit(solution)/shard_map/ppermute | solution.py:453
  63.9 25.4 %collective-permute-start.12 = (f16[144,1024]{1,0:T(8,128)(2,1)S(1)}, f16[144,1024]{1,0:T(8,128)(2,1)S(1)}, u32[]{:S(2)}, u32[]{:S(2)}) collective-permute-start(f16[144,1024]{1,0:T(8,128)(2,1)S(1)} %convert_element_type.52), channel_id=1, source_target_pairs={{0,6},{1,7},{2,4},{3,5},{4,2},{5,3},{6,0},{7,1},{8,14},{9,15},{10,... | collective-permute-start | bytes 884744 | tf_op jit(solution)/shard_map/ppermute | solution.py:453
  64.2 25.1 %collective-permute-start.10 = (f16[144,1024]{1,0:T(8,128)(2,1)S(1)}, f16[144,1024]{1,0:T(8,128)(2,1)S(1)}, u32[]{:S(2)}, u32[]{:S(2)}) collective-permute-start(f16[144,1024]{1,0:T(8,128)(2,1)S(1)} %convert_element_type.52), channel_id=1, source_target_pairs={{0,2},{1,3},{2,0},{3,1},{4,6},{5,7},{6,4},{7,5},{8,10},{9,11},{10,... | collective-permute-start | bytes 884744 | tf_op jit(solution)/shard_map/ppermute | solution.py:453
  73.7 15.9 %collective-permute-start.14 = (f32[256,256]{1,0:T(8,128)S(1)}, f32[256,256]{1,0:T(8,128)S(1)}, u32[]{:S(2)}, u32[]{:S(2)}) collective-permute-start(f32[256,256]{1,0:T(8,128)S(1)} %constant_dynamic-slice_fusion), channel_id=1, source_target_pairs={{0,1},{1,0},{2,3},{3,2},{4,5},{5,4},{6,7},{7,6},{8,9},{9,8},{10,11... | collective-permute-start | bytes 786440 | tf_op jit(solution)/shard_map/ppermute | solution.py:453
  73.8 17.5 %copy-start.2 = (f32[32,256]{1,0:T(8,128)S(1)}, f32[32,256]{1,0:T(8,128)}, u32[]{:S(2)}) copy-start(f32[32,256]{1,0:T(8,128)} %ld_ref.1) | copy-start | bytes 98308
  73.8 17.5 %copy-start.3 = (f32[32,256]{1,0:T(8,128)S(1)}, f32[32,256]{1,0:T(8,128)}, u32[]{:S(2)}) copy-start(f32[32,256]{1,0:T(8,128)} %ls_ref.1) | copy-start | bytes 98308
  73.9 29.9 %collective-permute-start.9 = (f32[256,1024]{1,0:T(8,128)S(1)}, f32[256,1024]{1,0:T(8,128)S(1)}, u32[]{:S(2)}, u32[]{:S(2)}) collective-permute-start(f32[256,1024]{1,0:T(8,128)S(1)} %constant_dynamic-slice_fusion.1), channel_id=1, source_target_pairs={{0,1},{1,0},{2,3},{3,2},{4,5},{5,4},{6,7},{7,6},{8,9},{9,8},{10,11... | collective-permute-start | bytes 3145736 | tf_op jit(solution)/shard_map/ppermute | solution.py:453
  89.6 7.7 %collective-permute-start.13 = (f32[128,1024]{1,0:T(8,128)S(1)}, f32[128,1024]{1,0:T(8,128)S(1)}, u32[]{:S(2)}, u32[]{:S(2)}) collective-permute-start(f32[128,1024]{1,0:T(8,128)S(1)} %multiply_add_fusion), channel_id=1, source_target_pairs={{0,1},{1,0},{2,3},{3,2},{4,5},{5,4},{6,7},{7,6},{8,9},{9,8},{10,11... | collective-permute-start | bytes 1572872 | tf_op jit(solution)/shard_map/ppermute | solution.py:453
  89.7 5.9 %collective-permute-start.17 = (f32[256,128]{1,0:T(8,128)S(1)}, f32[256,128]{1,0:T(8,128)S(1)}, u32[]{:S(2)}, u32[]{:S(2)}) collective-permute-start(f32[256,128]{1,0:T(8,128)S(1)} %slice.110), channel_id=1, source_target_pairs={{0,8},{8,0},{16,24},{24,16},{1,9},{9,1},{17,25},{25,17},{2,10},{10... | collective-permute-start | bytes 393224 | tf_op jit(solution)/shard_map/ppermute | solution.py:592
  95.7 5.1 %collective-permute-start.18 = (f32[256,128]{1,0:T(8,128)S(1)}, f32[256,128]{1,0:T(8,128)S(1)}, u32[]{:S(2)}, u32[]{:S(2)}) collective-permute-start(f32[256,128]{1,0:T(8,128)S(1)} %get-tuple-element.90), channel_id=1, source_target_pairs={{0,16},{8,24},{16,0},{24,8},{1,17},{9,25},{17,1},{25,9},{2,18},{10... | collective-permute-start | bytes 393224 | tf_op jit(solution)/shard_map/ppermute | solution.py:592
  98.2 5.0 %collective-permute-start.15 = (f32[256,128]{1,0:T(8,128)S(1)}, f32[256,128]{1,0:T(8,128)S(1)}, u32[]{:S(2)}, u32[]{:S(2)}) collective-permute-start(f32[256,128]{1,0:T(8,128)S(1)} %shard_map.122), channel_id=1, source_target_pairs={{0,8},{8,0},{16,24},{24,16},{1,9},{9,1},{17,25},{25,17},{2,10},{10... | collective-permute-start | bytes 393224 | tf_op jit(solution)/shard_map/ppermute | solution.py:592
  103.3 5.0 %collective-permute-start.16 = (f32[256,128]{1,0:T(8,128)S(1)}, f32[256,128]{1,0:T(8,128)S(1)}, u32[]{:S(2)}, u32[]{:S(2)}) collective-permute-start(f32[256,128]{1,0:T(8,128)S(1)} %add.128), channel_id=1, source_target_pairs={{0,16},{8,24},{16,0},{24,8},{1,17},{9,25},{17,1},{25,9},{2,18},{10... | collective-permute-start | bytes 393224 | tf_op jit(solution)/shard_map/ppermute | solution.py:592

commit v4 on v2

--- a/solution.py
+++ b/solution.py
@@ -553,7 +553,9 @@
             out += decode(g, n, jnp.where((chip ^ d) > chip, fade, 0.0))
         return out
 
-    for d, keys in enumerate(far, 1):
+    nearer = [1 << b for b in reversed(range(chips.bit_length() - 1))]
+    for d in nearer + [d for d in range(1, chips) if d not in nearer]:
+        keys = far[d - 1]
         flag = jnp.reshape((chip ^ d) < chip, (1,)).astype(jnp.int32)
         soft = call(
             far_kernel, carry, (flag, qs, keys, *soft),
@@ -584,10 +586,8 @@
         return half(a, core, t, 0), swap(half(a, 1 - core, t, 0), 1)
 
     def tp_sum(a):
-        bit = 1
-        while bit < tp:
-            a = a + lax.ppermute(a, "tp", [(i, i ^ bit) for i in range(tp)])
-            bit *= 2
+        for bit in range(tp.bit_length() - 1):
+            a = a + lax.ppermute(a, "tp", [(i, i ^ (1 << bit)) for i in range(tp)])
         return a
 
     back_all = joined(*home(back), 1)

time: 110 us -> 110 us (level)
  no operation moved by 1% of the time
where the time goes in v4:
time: 110 us
  waiting for transfers between devices  46.4 us (42%)
  Pallas kernels  30.4 us (28%)
  starting transfers between devices  25.3 us (23%)
  other arithmetic  5.27 us (5%)
  local copies, waits for them, and re-layouts  1.29 us (1%)
  between operations  1.16 us (1%)
    ppermute x14, waiting for transfers between devices, swap(): return lax.ppermute(a, 'seq', [(i, i ^ bits) for i in range(count)])  38.4 us
    pallas_call x12, Pallas kernels, call(): pl.pallas_call(kernel, out_shape=shapes, in_specs=in_specs or [VM] * len(...  30.4 us
    ppermute x14, starting transfers between devices, swap(): return lax.ppermute(a, 'seq', [(i, i ^ bits) for i in range(count)])  19.4 us
    ppermute x4, waiting for transfers between devices, tp_sum(): a = a + lax.ppermute(a, 'tp', [(i, i ^ 1 << bit) for i in range(tp)])  7.98 us
    ppermute x4, starting transfers between devices, tp_sum(): a = a + lax.ppermute(a, 'tp', [(i, i ^ 1 << bit) for i in range(tp)])  5.26 us
  transfers between devices with their start and end apart: 19, of which 12 were waited for; matrix products, arithmetic and copies ran while one was open for 4% of the time, Pallas kernels for 26%

profile of v4, /device:TPU:8, one launch (start us, length us, event | category | flops | bytes accessed | tf_op | source)
XLA Modules:
  0.0 109.8 jit_solution(2205255148355737471)
XLA Ops:
  0.7 0.9 pad_maximum_fusion.10
  1.6 0.0 copy-start.1
  1.6 0.0 copy-start.5
  1.6 1.0 constant_dynamic-slice_fusion.6
  2.6 0.5 collective-permute-start
  3.2 0.1 slice_reduce_fusion.3
  3.3 0.8 dynamic-slice_select_fusion.3
  4.0 0.1 collective-permute-done
  4.2 0.1 broadcast_select_fusion.7
  4.3 0.4 collective-permute-start.3
  4.7 2.6 %collective-permute-start.4 = (bf16[512,256]{1,0:T(8,128)(2,1)S(1)}, bf16[512,256]{1,0:T(8,128)(2,1)S(1)}, u32[]{:S(2)}, u32[]{:S(2)}) collective-permute-start(bf16[512,256]{1,0:T(8,128)(2,1)S(1)} %pad_maximum_fusion.5.kv_ref), channel_id=1, source_target_pairs={{0,4},{1,5},{2,6},{3,7},{4,0},{5,1},{6,2},{7,3},{8,12},{9,13},{10,... | collective-permute-start | bytes 786440 | tf_op jit(solution)/shard_map/ppermute | solution.py:453
  7.3 0.4 collective-permute-start.6
  7.9 0.1 pad_maximum_fusion.4
  7.9 0.1 collective-permute-start.1
  8.0 0.3 broadcast_select_fusion.1
  8.3 0.1 pad_maximum_fusion.2.q_ref
  8.4 3.1 %shard_map.113 = (bf16[512,2048]{1,0:T(8,128)(2,1)S(1)}, f32[1024,512]{1,0:T(8,128)S(1)}, f32[8,512]{1,0:T(8,128)S(1)}, f32[8,512]{1,0:T(8,128)S(1)}) custom-call(bf16[512,1024]{1,0:T(8,128)(2,1)S(1)} %pad_maximum_fusion.2.q_ref, bf16[512,256]{1,0:T(8,128)(2,1)S(1)} %pad_maximum_fusion.5.kv_ref), custom_call_target="tpu_custom_call" | custom-call | flops 1073741824 | bytes 1310720 | tf_op jit(solution)/shard_map/pallas_call | solution.py:420
  11.5 7.3 %collective-permute-done.4.kv_ref = bf16[512,256]{1,0:T(8,128)(2,1)S(1)} collective-permute-done((bf16[512,256]{1,0:T(8,128)(2,1)S(1)}, bf16[512,256]{1,0:T(8,128)(2,1)S(1)}, u32[]{:S(2)}, u32[]{:S(2)}) %collective-permute-start.4) | collective-permute-done | bytes 262176 | tf_op jit(solution)/shard_map/ppermute | solution.py:453
  18.8 0.7 collective-permute-start.5
  19.4 0.3 shard_map.114
  19.7 0.1 collective-permute-done.6.kv_ref
  19.8 3.9 %shard_map.115 = (f32[1024,512]{1,0:T(8,128)S(1)}, f32[8,512]{1,0:T(8,128)S(1)}, f32[8,512]{1,0:T(8,128)S(1)}) custom-call(s32[1]{0:T(128)} %bitcast.1.flag, bf16[512,2048]{1,0:T(8,128)(2,1)S(1)} %get-tuple-element.45.qs_ref, bf16[512,256]{1,0:T(8,128)(2,1)S(1)} %collective-permute-done.6.kv_ref, ...), custom_call_target="tpu_custom_call", output_to_operand_aliasing={{0}: (3, {}), {1}: (4, {}), {2}: (5, {})} | custom-call | flops 1073741824 | bytes 4489220 | tf_op jit(solution)/shard_map/pallas_call | solution.py:420
  23.8 0.3 broadcast_select_fusion.3
  24.1 0.1 pad_maximum_fusion.1.x_ref
  24.2 2.0 %shard_map.111 = (f32[128,1024]{1,0:T(8,128)S(1)}, f32[144,1024]{1,0:T(8,128)S(1)}, f32[512,1024]{1,0:T(8,128)S(1)}) custom-call(bf16[512,1024]{1,0:T(8,128)(2,1)S(1)} %pad_maximum_fusion.1.x_ref, bf16[512,128]{1,0:T(8,128)(2,1)S(1)} %pad_maximum_fusion.8.w_ref, f32[16,512]{1,0:T(8,128)S(1)} %pad_maximum_fusion.11.ls_ref, ...), custom_call_target="tpu_custom_call" | custom-call | flops 536870912 | bytes 1245184 | tf_op jit(solution)/shard_map/pallas_call | solution.py:420
  26.2 0.1 collective-permute-start.7
  26.3 6.9 %shard_map.112 = (f32[512,1024]{1,0:T(8,128)S(1)}, f32[512,1024]{1,0:T(8,128)S(1)}, f32[512,1024]{1,0:T(8,128)S(1)}, f32[16,512]{1,0:T(8,128)S(1)}) custom-call(bf16[512,1024]{1,0:T(8,128)(2,1)S(1)} %pad_maximum_fusion.1.x_ref, bf16[512,128]{1,0:T(8,128)(2,1)S(1)} %pad_maximum_fusion.8.w_ref, bf16[512,128]{1,0:T(8,128)(2,1)S(1)} %pad_maximum_fusion.9.r_ref, ...), custom_call_target="tpu_custom_call" | custom-call | flops 1073741824 | bytes 1900544 | tf_op jit(solution)/shard_map/pallas_call | solution.py:420
  33.2 0.5 shard_map.116
  33.7 1.5 %collective-permute-done.7 = f16[144,1024]{1,0:T(8,128)(2,1)S(1)} collective-permute-done((f16[144,1024]{1,0:T(8,128)(2,1)S(1)}, f16[144,1024]{1,0:T(8,128)(2,1)S(1)}, u32[]{:S(2)}, u32[]{:S(2)}) %collective-permute-start.7) | collective-permute-done | bytes 294944 | tf_op jit(solution)/shard_map/ppermute | solution.py:453
  35.2 0.2 shard_map.117
  35.5 10.5 %collective-permute-start.8 = (f16[144,1024]{1,0:T(8,128)(2,1)S(1)}, f16[144,1024]{1,0:T(8,128)(2,1)S(1)}, u32[]{:S(2)}, u32[]{:S(2)}) collective-permute-start(f16[144,1024]{1,0:T(8,128)(2,1)S(1)} %convert_element_type.56), channel_id=1, source_target_pairs={{0,4},{1,5},{2,6},{3,7},{4,0},{5,1},{6,2},{7,3},{8,12},{9,13},{10,... | collective-permute-start | bytes 884744 | tf_op jit(solution)/shard_map/ppermute | solution.py:453
  46.1 12.8 %collective-permute-done.8 = f16[144,1024]{1,0:T(8,128)(2,1)S(1)} collective-permute-done((f16[144,1024]{1,0:T(8,128)(2,1)S(1)}, f16[144,1024]{1,0:T(8,128)(2,1)S(1)}, u32[]{:S(2)}, u32[]{:S(2)}) %collective-permute-start.8) | collective-permute-done | bytes 294944 | tf_op jit(solution)/shard_map/ppermute | solution.py:453
  58.9 0.1 fusion.sin_ref
  59.0 1.4 %shard_map.118 = (f32[512,1024]{1,0:T(8,128)S(1)}, f32[128,1024]{1,0:T(8,128)S(1)}, f32[144,1024]{1,0:T(8,128)S(1)}) custom-call(f32[512,1024]{1,0:T(8,128)S(1)} %get-tuple-element.43.y_ref, f32[1024,512]{1,0:T(8,128)S(1)} %get-tuple-element.56.acc_ref, f32[8,512]{1,0:T(8,128)S(1)} %get-tuple-element.57.l_ref, bf16[512,128]{1,0:T(8,128)(2,1)S(1)} %pad_maximum_fusion.9.r_ref, ...), custom_call_target="tpu_custom_call" | custom-call | flops 1073741824 | bytes 6963200 | tf_op jit(solution)/shard_map/pallas_call | solution.py:420
  60.5 2.3 %collective-permute-start.10 = (f16[144,1024]{1,0:T(8,128)(2,1)S(1)}, f16[144,1024]{1,0:T(8,128)(2,1)S(1)}, u32[]{:S(2)}, u32[]{:S(2)}) collective-permute-start(f16[144,1024]{1,0:T(8,128)(2,1)S(1)} %convert_element_type.58), channel_id=1, source_target_pairs={{0,2},{1,3},{2,0},{3,1},{4,6},{5,7},{6,4},{7,5},{8,10},{9,11},{10,... | collective-permute-start | bytes 884744 | tf_op jit(solution)/shard_map/ppermute | solution.py:453
  62.8 1.3 %collective-permute-start.11 = (f16[144,1024]{1,0:T(8,128)(2,1)S(1)}, f16[144,1024]{1,0:T(8,128)(2,1)S(1)}, u32[]{:S(2)}, u32[]{:S(2)}) collective-permute-start(f16[144,1024]{1,0:T(8,128)(2,1)S(1)} %convert_element_type.58), channel_id=1, source_target_pairs={{0,4},{1,5},{2,6},{3,7},{4,0},{5,1},{6,2},{7,3},{8,12},{9,13},{10,... | collective-permute-start | bytes 884744 | tf_op jit(solution)/shard_map/ppermute | solution.py:453
  64.0 0.5 collective-permute-start.12
  64.5 8.1 %shard_map.119 = (f32[512,1024]{1,0:T(8,128)S(1)}, f32[512,128]{1,0:T(8,128)S(1)}, f32[512,128]{1,0:T(8,128)S(1)}) custom-call(f32[512,1024]{1,0:T(8,128)S(1)} %get-tuple-element.60.res_ref, bf16[512,1024]{1,0:T(8,128)(2,1)S(1)} %pad_maximum_fusion.1.x_ref, bf16[512,128]{1,0:T(8,128)(2,1)S(1)} %pad_maximum_fusion.8.w_ref, ...), custom_call_target="tpu_custom_call" | custom-call | flops 2147483648 | bytes 11304960 | tf_op jit(solution)/shard_map/pallas_call | solution.py:420
  72.7 0.1 collective-permute-start.14
  72.8 0.0 copy-start.2
  72.8 0.1 constant_dynamic-slice_fusion.1
  72.9 0.5 collective-permute-start.9
  73.5 1.3 %collective-permute-done.10 = f16[144,1024]{1,0:T(8,128)(2,1)S(1)} collective-permute-done((f16[144,1024]{1,0:T(8,128)(2,1)S(1)}, f16[144,1024]{1,0:T(8,128)(2,1)S(1)}, u32[]{:S(2)}, u32[]{:S(2)}) %collective-permute-start.10) | collective-permute-done | bytes 294944 | tf_op jit(solution)/shard_map/ppermute | solution.py:453
  74.8 9.3 %collective-permute-done.11 = f16[144,1024]{1,0:T(8,128)(2,1)S(1)} collective-permute-done((f16[144,1024]{1,0:T(8,128)(2,1)S(1)}, f16[144,1024]{1,0:T(8,128)(2,1)S(1)}, u32[]{:S(2)}, u32[]{:S(2)}) %collective-permute-start.11) | collective-permute-done | bytes 294944 | tf_op jit(solution)/shard_map/ppermute | solution.py:453
  84.1 6.1 %collective-permute-done.12 = f16[144,1024]{1,0:T(8,128)(2,1)S(1)} collective-permute-done((f16[144,1024]{1,0:T(8,128)(2,1)S(1)}, f16[144,1024]{1,0:T(8,128)(2,1)S(1)}, u32[]{:S(2)}, u32[]{:S(2)}) %collective-permute-start.12) | collective-permute-done | bytes 294944 | tf_op jit(solution)/shard_map/ppermute | solution.py:453
  90.2 0.2 multiply_add_fusion
  90.4 0.1 collective-permute-start.13
  90.6 1.6 %collective-permute-start.17 = (f32[256,128]{1,0:T(8,128)S(1)}, f32[256,128]{1,0:T(8,128)S(1)}, u32[]{:S(2)}, u32[]{:S(2)}) collective-permute-start(f32[256,128]{1,0:T(8,128)S(1)} %slice.95), channel_id=1, source_target_pairs={{0,8},{8,0},{16,24},{24,16},{1,9},{9,1},{17,25},{25,17},{2,10},{10... | collective-permute-start | bytes 393224 | tf_op jit(solution)/shard_map/ppermute | solution.py:590
  92.1 1.0 shard_map.120
  93.1 3.4 %collective-permute-done.17 = f32[256,128]{1,0:T(8,128)S(1)} collective-permute-done((f32[256,128]{1,0:T(8,128)S(1)}, f32[256,128]{1,0:T(8,128)S(1)}, u32[]{:S(2)}, u32[]{:S(2)}) %collective-permute-start.17) | collective-permute-done | bytes 131104 | tf_op jit(solution)/shard_map/ppermute | solution.py:590
  96.5 1.6 %collective-permute-start.18 = (f32[256,128]{1,0:T(8,128)S(1)}, f32[256,128]{1,0:T(8,128)S(1)}, u32[]{:S(2)}, u32[]{:S(2)}) collective-permute-start(f32[256,128]{1,0:T(8,128)S(1)} %get-tuple-element.90), channel_id=1, source_target_pairs={{0,16},{8,24},{16,0},{24,8},{1,17},{9,25},{17,1},{25,9},{2,18},{10... | collective-permute-start | bytes 393224 | tf_op jit(solution)/shard_map/ppermute | solution.py:590
  98.1 0.1 broadcast_select_fusion.5
  98.2 0.1 pad_maximum_fusion.3.g_ref
  98.3 0.8 shard_map.122
  99.1 1.6 %collective-permute-start.15 = (f32[256,128]{1,0:T(8,128)S(1)}, f32[256,128]{1,0:T(8,128)S(1)}, u32[]{:S(2)}, u32[]{:S(2)}) collective-permute-start(f32[256,128]{1,0:T(8,128)S(1)} %shard_map.122), channel_id=1, source_target_pairs={{0,8},{8,0},{16,24},{24,16},{1,9},{9,1},{17,25},{25,17},{2,10},{10... | collective-permute-start | bytes 393224 | tf_op jit(solution)/shard_map/ppermute | solution.py:590
  100.6 1.0 collective-permute-done.18
  101.6 0.7 add.133
  102.3 1.8 %collective-permute-done.15 = f32[256,128]{1,0:T(8,128)S(1)} collective-permute-done((f32[256,128]{1,0:T(8,128)S(1)}, f32[256,128]{1,0:T(8,128)S(1)}, u32[]{:S(2)}, u32[]{:S(2)}) %collective-permute-start.15) | collective-permute-done | bytes 131104 | tf_op jit(solution)/shard_map/ppermute | solution.py:590
  104.1 0.6 collective-permute-start.16
  104.7 0.3 dynamic-slice_select_fusion.1
  105.0 0.1 pad_maximum_fusion.back_ref
  105.2 2.2 %shard_map.121 = (f32[256,2048]{1,0:T(8,128)}, f32[32,256]{1,0:T(8,128)}) custom-call(f32[256,2048]{1,0:T(8,128)S(1)} %pad_maximum_fusion.back_ref, f32[256,2048]{1,0:T(8,128)S(1)} %get-tuple-element.66.wexp_ref, bf16[256,2048]{1,0:T(8,128)(2,1)S(1)} %copy-done, bf16[256,128]{1,0:T(8,128)(2,1)S(1)} %copy-done.1, f32[128,2048]{1,0:T(8,128)S(1)} %pad_maximum_fusion.3.g_ref), custom_call_target="tpu_custom_call" | custom-call | flops 1073741824 | bytes 6356992 | tf_op jit(solution)/shard_map/pallas_call | solution.py:420
  107.4 1.8 %collective-permute-done.16 = f32[256,128]{1,0:T(8,128)S(1)} collective-permute-done((f32[256,128]{1,0:T(8,128)S(1)}, f32[256,128]{1,0:T(8,128)S(1)}, u32[]{:S(2)}, u32[]{:S(2)}) %collective-permute-start.16) | collective-permute-done | bytes 131104 | tf_op jit(solution)/shard_map/ppermute | solution.py:590
  109.1 0.7 add.131
  (47 shorter events, 0.7 us)
Async XLA Ops:
  0.6 7.2 %copy-start = (bf16[256,2048]{1,0:T(8,128)(2,1)S(1)}, bf16[256,2048]{1,0:T(8,128)(2,1)}, u32[]{:S(2)}) copy-start(bf16[256,2048]{1,0:T(8,128)(2,1)} %x_ref.3) | copy-start | bytes 3145732
  0.6 3.6 %copy-start.4 = (bf16[256,2048]{1,0:T(8,128)(2,1)S(1)}, bf16[256,2048]{1,0:T(8,128)(2,1)}, u32[]{:S(2)}) copy-start(bf16[256,2048]{1,0:T(8,128)(2,1)} %param.8) | copy-start | bytes 3145732
  1.6 1.6 %collective-permute-start.2 = (f32[64,256]{1,0:T(8,128)S(1)}, f32[64,256]{1,0:T(8,128)S(1)}, u32[]{:S(2)}, u32[]{:S(2)}) collective-permute-start(f32[64,256]{1,0:T(8,128)S(1)} %pad_maximum_fusion.10), channel_id=1, source_target_pairs={{0,1},{1,0},{2,3},{3,2},{4,5},{5,4},{6,7},{7,6},{8,9},{9,8},{10,11... | collective-permute-start | bytes 196616 | tf_op jit(solution)/shard_map/ppermute | solution.py:453
  1.6 6.2 %copy-start.1 = (bf16[256,128]{1,0:T(8,128)(2,1)S(1)}, bf16[256,128]{1,0:T(8,128)(2,1)}, u32[]{:S(2)}) copy-start(bf16[256,128]{1,0:T(8,128)(2,1)} %w_ref.1) | copy-start | bytes 196612
  1.6 6.2 %copy-start.5 = (bf16[256,128]{1,0:T(8,128)(2,1)S(1)}, bf16[256,128]{1,0:T(8,128)(2,1)}, u32[]{:S(2)}) copy-start(bf16[256,128]{1,0:T(8,128)(2,1)} %param.13) | copy-start | bytes 196612
  2.6 1.5 %collective-permute-start = (bf16[256,256]{1,0:T(8,128)(2,1)S(1)}, bf16[256,256]{1,0:T(8,128)(2,1)S(1)}, u32[]{:S(2)}, u32[]{:S(2)}) collective-permute-start(bf16[256,256]{1,0:T(8,128)(2,1)S(1)} %pad_maximum_fusion.7), channel_id=1, source_target_pairs={{0,1},{1,0},{2,3},{3,2},{4,5},{5,4},{6,7},{7,6},{8,9},{9,8},{10,11... | collective-permute-start | bytes 393224 | tf_op jit(solution)/shard_map/ppermute | solution.py:453
  4.3 3.7 %collective-permute-start.3 = (bf16[256,1024]{1,0:T(8,128)(2,1)S(1)}, bf16[256,1024]{1,0:T(8,128)(2,1)S(1)}, u32[]{:S(2)}, u32[]{:S(2)}) collective-permute-start(bf16[256,1024]{1,0:T(8,128)(2,1)S(1)} %constant_dynamic-slice_fusion.2), channel_id=1, source_target_pairs={{0,1},{1,0},{2,3},{3,2},{4,5},{5,4},{6,7},{7,6},{8,9},{9,8},{10,11... | collective-permute-start | bytes 1572872 | tf_op jit(solution)/shard_map/ppermute | solution.py:453
  4.7 14.0 %collective-permute-start.4 = (bf16[512,256]{1,0:T(8,128)(2,1)S(1)}, bf16[512,256]{1,0:T(8,128)(2,1)S(1)}, u32[]{:S(2)}, u32[]{:S(2)}) collective-permute-start(bf16[512,256]{1,0:T(8,128)(2,1)S(1)} %pad_maximum_fusion.5.kv_ref), channel_id=1, source_target_pairs={{0,4},{1,5},{2,6},{3,7},{4,0},{5,1},{6,2},{7,3},{8,12},{9,13},{10,... | collective-permute-start | bytes 786440 | tf_op jit(solution)/shard_map/ppermute | solution.py:453
  7.3 12.5 %collective-permute-start.6 = (bf16[512,256]{1,0:T(8,128)(2,1)S(1)}, bf16[512,256]{1,0:T(8,128)(2,1)S(1)}, u32[]{:S(2)}, u32[]{:S(2)}) collective-permute-start(bf16[512,256]{1,0:T(8,128)(2,1)S(1)} %pad_maximum_fusion.5.kv_ref), channel_id=1, source_target_pairs={{0,2},{1,3},{2,0},{3,1},{4,6},{5,7},{6,4},{7,5},{8,10},{9,11},{10,... | collective-permute-start | bytes 786440 | tf_op jit(solution)/shard_map/ppermute | solution.py:453
  7.9 15.9 %collective-permute-start.1 = (bf16[256,1280]{1,0:T(8,128)(2,1)S(1)}, bf16[256,1280]{1,0:T(8,128)(2,1)S(1)}, u32[]{:S(2)}, u32[]{:S(2)}) collective-permute-start(bf16[256,1280]{1,0:T(8,128)(2,1)S(1)} %pad_maximum_fusion.4), channel_id=1, source_target_pairs={{0,1},{1,0},{2,3},{3,2},{4,5},{5,4},{6,7},{7,6},{8,9},{9,8},{10,11... | collective-permute-start | bytes 1966088 | tf_op jit(solution)/shard_map/ppermute | solution.py:453
  18.8 14.5 %collective-permute-start.5 = (bf16[512,256]{1,0:T(8,128)(2,1)S(1)}, bf16[512,256]{1,0:T(8,128)(2,1)S(1)}, u32[]{:S(2)}, u32[]{:S(2)}) collective-permute-start(bf16[512,256]{1,0:T(8,128)(2,1)S(1)} %collective-permute-done.4.kv_ref), channel_id=1, source_target_pairs={{4,6},{5,7},{6,4},{7,5},{12,14},{13,15},{14,12},{15,13},{20,22},{2... | collective-permute-start | bytes 786440 | tf_op jit(solution)/shard_map/ppermute | solution.py:477
  26.2 9.0 %collective-permute-start.7 = (f16[144,1024]{1,0:T(8,128)(2,1)S(1)}, f16[144,1024]{1,0:T(8,128)(2,1)S(1)}, u32[]{:S(2)}, u32[]{:S(2)}) collective-permute-start(f16[144,1024]{1,0:T(8,128)(2,1)S(1)} %convert_element_type.54), channel_id=1, source_target_pairs={{0,2},{1,3},{2,0},{3,1},{4,6},{5,7},{6,4},{7,5},{8,10},{9,11},{10,... | collective-permute-start | bytes 884744 | tf_op jit(solution)/shard_map/ppermute | solution.py:453
  35.5 23.3 %collective-permute-start.8 = (f16[144,1024]{1,0:T(8,128)(2,1)S(1)}, f16[144,1024]{1,0:T(8,128)(2,1)S(1)}, u32[]{:S(2)}, u32[]{:S(2)}) collective-permute-start(f16[144,1024]{1,0:T(8,128)(2,1)S(1)} %convert_element_type.56), channel_id=1, source_target_pairs={{0,4},{1,5},{2,6},{3,7},{4,0},{5,1},{6,2},{7,3},{8,12},{9,13},{10,... | collective-permute-start | bytes 884744 | tf_op jit(solution)/shard_map/ppermute | solution.py:453
  60.5 14.3 %collective-permute-start.10 = (f16[144,1024]{1,0:T(8,128)(2,1)S(1)}, f16[144,1024]{1,0:T(8,128)(2,1)S(1)}, u32[]{:S(2)}, u32[]{:S(2)}) collective-permute-start(f16[144,1024]{1,0:T(8,128)(2,1)S(1)} %convert_element_type.58), channel_id=1, source_target_pairs={{0,2},{1,3},{2,0},{3,1},{4,6},{5,7},{6,4},{7,5},{8,10},{9,11},{10,... | collective-permute-start | bytes 884744 | tf_op jit(solution)/shard_map/ppermute | solution.py:453
  62.8 21.3 %collective-permute-start.11 = (f16[144,1024]{1,0:T(8,128)(2,1)S(1)}, f16[144,1024]{1,0:T(8,128)(2,1)S(1)}, u32[]{:S(2)}, u32[]{:S(2)}) collective-permute-start(f16[144,1024]{1,0:T(8,128)(2,1)S(1)} %convert_element_type.58), channel_id=1, source_target_pairs={{0,4},{1,5},{2,6},{3,7},{4,0},{5,1},{6,2},{7,3},{8,12},{9,13},{10,... | collective-permute-start | bytes 884744 | tf_op jit(solution)/shard_map/ppermute | solution.py:453
  64.0 26.2 %collective-permute-start.12 = (f16[144,1024]{1,0:T(8,128)(2,1)S(1)}, f16[144,1024]{1,0:T(8,128)(2,1)S(1)}, u32[]{:S(2)}, u32[]{:S(2)}) collective-permute-start(f16[144,1024]{1,0:T(8,128)(2,1)S(1)} %convert_element_type.58), channel_id=1, source_target_pairs={{0,6},{1,7},{2,4},{3,5},{4,2},{5,3},{6,0},{7,1},{8,14},{9,15},{10,... | collective-permute-start | bytes 884744 | tf_op jit(solution)/shard_map/ppermute | solution.py:453
  72.7 17.8 %collective-permute-start.14 = (f32[256,256]{1,0:T(8,128)S(1)}, f32[256,256]{1,0:T(8,128)S(1)}, u32[]{:S(2)}, u32[]{:S(2)}) collective-permute-start(f32[256,256]{1,0:T(8,128)S(1)} %constant_dynamic-slice_fusion), channel_id=1, source_target_pairs={{0,1},{1,0},{2,3},{3,2},{4,5},{5,4},{6,7},{7,6},{8,9},{9,8},{10,11... | collective-permute-start | bytes 786440 | tf_op jit(solution)/shard_map/ppermute | solution.py:453
  72.8 19.3 %copy-start.2 = (f32[32,256]{1,0:T(8,128)S(1)}, f32[32,256]{1,0:T(8,128)}, u32[]{:S(2)}) copy-start(f32[32,256]{1,0:T(8,128)} %ld_ref.1) | copy-start | bytes 98308
  72.8 19.3 %copy-start.3 = (f32[32,256]{1,0:T(8,128)S(1)}, f32[32,256]{1,0:T(8,128)}, u32[]{:S(2)}) copy-start(f32[32,256]{1,0:T(8,128)} %ls_ref.1) | copy-start | bytes 98308
  72.9 31.7 %collective-permute-start.9 = (f32[256,1024]{1,0:T(8,128)S(1)}, f32[256,1024]{1,0:T(8,128)S(1)}, u32[]{:S(2)}, u32[]{:S(2)}) collective-permute-start(f32[256,1024]{1,0:T(8,128)S(1)} %constant_dynamic-slice_fusion.1), channel_id=1, source_target_pairs={{0,1},{1,0},{2,3},{3,2},{4,5},{5,4},{6,7},{7,6},{8,9},{9,8},{10,11... | collective-permute-start | bytes 3145736 | tf_op jit(solution)/shard_map/ppermute | solution.py:453
  90.4 7.7 %collective-permute-start.13 = (f32[128,1024]{1,0:T(8,128)S(1)}, f32[128,1024]{1,0:T(8,128)S(1)}, u32[]{:S(2)}, u32[]{:S(2)}) collective-permute-start(f32[128,1024]{1,0:T(8,128)S(1)} %multiply_add_fusion), channel_id=1, source_target_pairs={{0,1},{1,0},{2,3},{3,2},{4,5},{5,4},{6,7},{7,6},{8,9},{9,8},{10,11... | collective-permute-start | bytes 1572872 | tf_op jit(solution)/shard_map/ppermute | solution.py:453
  90.6 5.9 %collective-permute-start.17 = (f32[256,128]{1,0:T(8,128)S(1)}, f32[256,128]{1,0:T(8,128)S(1)}, u32[]{:S(2)}, u32[]{:S(2)}) collective-permute-start(f32[256,128]{1,0:T(8,128)S(1)} %slice.95), channel_id=1, source_target_pairs={{0,8},{8,0},{16,24},{24,16},{1,9},{9,1},{17,25},{25,17},{2,10},{10... | collective-permute-start | bytes 393224 | tf_op jit(solution)/shard_map/ppermute | solution.py:590
  96.5 5.1 %collective-permute-start.18 = (f32[256,128]{1,0:T(8,128)S(1)}, f32[256,128]{1,0:T(8,128)S(1)}, u32[]{:S(2)}, u32[]{:S(2)}) collective-permute-start(f32[256,128]{1,0:T(8,128)S(1)} %get-tuple-element.90), channel_id=1, source_target_pairs={{0,16},{8,24},{16,0},{24,8},{1,17},{9,25},{17,1},{25,9},{2,18},{10... | collective-permute-start | bytes 393224 | tf_op jit(solution)/shard_map/ppermute | solution.py:590
  99.1 5.0 %collective-permute-start.15 = (f32[256,128]{1,0:T(8,128)S(1)}, f32[256,128]{1,0:T(8,128)S(1)}, u32[]{:S(2)}, u32[]{:S(2)}) collective-permute-start(f32[256,128]{1,0:T(8,128)S(1)} %shard_map.122), channel_id=1, source_target_pairs={{0,8},{8,0},{16,24},{24,16},{1,9},{9,1},{17,25},{25,17},{2,10},{10... | collective-permute-start | bytes 393224 | tf_op jit(solution)/shard_map/ppermute | solution.py:590
  104.1 5.0 %collective-permute-start.16 = (f32[256,128]{1,0:T(8,128)S(1)}, f32[256,128]{1,0:T(8,128)S(1)}, u32[]{:S(2)}, u32[]{:S(2)}) collective-permute-start(f32[256,128]{1,0:T(8,128)S(1)} %add.130), channel_id=1, source_target_pairs={{0,16},{8,24},{16,0},{24,8},{1,17},{9,25},{17,1},{25,9},{2,18},{10... | collective-permute-start | bytes 393224 | tf_op jit(solution)/shard_map/ppermute | solution.py:590

commit v5 on v2

--- a/solution.py
+++ b/solution.py
@@ -394,11 +394,14 @@
     xh_ref[...], xl_ref[...] = split2(x_ref[...].astype(F32) * wexp)
 
 
-def write_kernel(xh_ref, xl_ref, g_ref, gw0_ref, gw_ref):
+def write_kernel(xh_ref, xl_ref, g_ref, gw0_ref, top_ref, low_ref):
     gh, gl = split2(g_ref[...])
     n = gh.shape[0]
+    half = top_ref.shape[0]
     both = nt(xh_ref[...], jnp.concatenate([gh, gl], axis=0))
-    gw_ref[...] = gw0_ref[...] + both[:, :n] + both[:, n:] + nt(xl_ref[...], gh)
+    out = gw0_ref[...] + both[:, :n] + both[:, n:] + nt(xl_ref[...], gh)
+    top_ref[...] = out[:half]
+    low_ref[...] = out[half:]
 
 
 def final_kernel(back_ref, wexp_ref, x_ref, w_ref, g_ref, gi_ref, gls_ref):
@@ -583,22 +586,26 @@
     def home(a):
         return half(a, core, t, 0), swap(half(a, 1 - core, t, 0), 1)
 
-    def tp_sum(a):
-        bit = 1
-        while bit < tp:
-            a = a + lax.ppermute(a, "tp", [(i, i ^ bit) for i in range(tp)])
-            bit *= 2
-        return a
+    def tp_sum(parts):
+        bits = tp.bit_length() - 1
+        parts = list(parts)
+        for step in range(bits):
+            sent = [
+                lax.ppermute(a, "tp", [(i, i ^ (1 << ((step + k) % bits))) for i in range(tp)])
+                for k, a in enumerate(parts)
+            ]
+            parts = [a + b for a, b in zip(parts, sent)]
+        return parts
 
     back_all = joined(*home(back), 1)
     own, other = home(jnp.concatenate([gw, gr], axis=1))
     grads = own + other
     gw0, gr0 = grads[:, :n], grads[:, n:]
-    grad_read = tp_sum(gr0)
+    grad_read = jnp.concatenate(tp_sum([gr0[: t // 2], gr0[t // 2 :]]), axis=0)
     arriving = combine(coming)
     arrived = joined(arriving, swap(arriving, 1), 1)
-    (gwp,) = call(write_kernel, [((t, n), F32)], (xh, xl, arrived, gw0), flops=4 * mm)
-    grad_write = tp_sum(gwp)
+    gwp = call(write_kernel, [((t // 2, n), F32)] * 2, (xh, xl, arrived, gw0), flops=4 * mm)
+    grad_write = jnp.concatenate(tp_sum(gwp), axis=0)
     gi, gls = call(
         final_kernel, [((t, 2 * hc), F32), ((heads, t), F32)], (back_all, wexp, x, wr, arrived),
         flops=8 * mm,

time: 110 us -> 127 us (1.15)
  waiting for transfers between devices: 46.4 us -> 56.9 us
  starting transfers between devices: 25.3 us -> 27.6 us
  other arithmetic: 5.27 us -> 7.33 us
  local copies, waits for them, and re-layouts: 1.29 us -> 2.86 us
    ppermute x14, waiting for transfers between devices: 38.4 us -> 47 us  [swap(): return lax.ppermute(a, 'seq', [(i, i ^ bits) for i in range(count)])]
    ppermute x4 -> x8, starting transfers between devices: 5.26 us -> 7.91 us  [tp_sum(): lax.ppermute(a, 'tp', [(i, i ^ 1 << (step + k) % bits) for i in range(tp)])]
    ppermute x4 -> x8, waiting for transfers between devices: 7.98 us -> 9.87 us  [tp_sum(): lax.ppermute(a, 'tp', [(i, i ^ 1 << (step + k) % bits) for i in range(tp)])]
    unnamed x13 -> x19, local copies, waits for them, and re-layouts: 0.05 us -> 1.66 us
    concatenate x0 -> x2, other arithmetic: none -> 1.33 us  [the longest x1 0.67 us: on_device(): grad_write = jnp.concatenate(tp_sum(gwp), axis=0)]
    add x4 -> x7, other arithmetic: 1.39 us -> 0.07 us  [tp_sum(): parts = [a + b for a, b in zip(parts, sent)]]
  transfers between devices with their start and end apart: 19 -> 23, of which waited for: 12 -> 15; matrix products, arithmetic and copies ran while one was open for 4% -> 5% of each run, Pallas kernels for 26% -> 15%
where the time goes in v5:
time: 127 us; the launch traced here: 126 us
  waiting for transfers between devices  56.9 us (45%)
  Pallas kernels  30.5 us (24%)
  starting transfers between devices  27.6 us (22%)
  other arithmetic  7.33 us (6%)
  local copies, waits for them, and re-layouts  2.86 us (2%)
    ppermute x14, waiting for transfers between devices, swap(): return lax.ppermute(a, 'seq', [(i, i ^ bits) for i in range(count)])  47 us
    pallas_call x12, Pallas kernels, call(): pl.pallas_call(kernel, out_shape=shapes, in_specs=in_specs or [VM] * len(...  30.5 us
    ppermute x14, starting transfers between devices, swap(): return lax.ppermute(a, 'seq', [(i, i ^ bits) for i in range(count)])  19 us
    ppermute x8, waiting for transfers between devices, tp_sum(): lax.ppermute(a, 'tp', [(i, i ^ 1 << (step + k) % bits) for i in range(tp)])  9.87 us
    ppermute x8, starting transfers between devices, tp_sum(): lax.ppermute(a, 'tp', [(i, i ^ 1 << (step + k) % bits) for i in range(tp)])  7.91 us
  transfers between devices with their start and end apart: 23, of which 15 were waited for; matrix products, arithmetic and copies ran while one was open for 5% of the time, Pallas kernels for 15%

profile of v5, /device:TPU:8, one launch (start us, length us, event | category | flops | bytes accessed | tf_op | source)
XLA Modules:
  0.0 126.4 jit_solution(8418398079333401482)
XLA Ops:
  0.7 0.9 pad_maximum_fusion.12
  1.6 1.0 constant_dynamic-slice_fusion.6
  2.6 0.5 collective-permute-start
  3.2 0.1 slice_reduce_fusion.3
  3.3 0.8 dynamic-slice_select_fusion.3
  4.0 0.1 collective-permute-done
  4.3 0.4 collective-permute-start.3
  4.7 2.6 %collective-permute-start.4 = (bf16[512,256]{1,0:T(8,128)(2,1)S(1)}, bf16[512,256]{1,0:T(8,128)(2,1)S(1)}, u32[]{:S(2)}, u32[]{:S(2)}) collective-permute-start(bf16[512,256]{1,0:T(8,128)(2,1)S(1)} %pad_maximum_fusion.5.kv_ref), channel_id=1, source_target_pairs={{0,4},{1,5},{2,6},{3,7},{4,0},{5,1},{6,2},{7,3},{8,12},{9,13},{10,... | collective-permute-start | bytes 786440 | tf_op jit(solution)/shard_map/ppermute | solution.py:456
  7.3 0.4 collective-permute-start.6
  7.9 0.1 collective-permute-start.1
  8.0 0.3 broadcast_select_fusion.1
  8.4 3.1 %shard_map.113 = (bf16[512,2048]{1,0:T(8,128)(2,1)S(1)}, f32[1024,512]{1,0:T(8,128)S(1)}, f32[8,512]{1,0:T(8,128)S(1)}, f32[8,512]{1,0:T(8,128)S(1)}) custom-call(bf16[512,1024]{1,0:T(8,128)(2,1)S(1)} %pad_maximum_fusion.2.q_ref, bf16[512,256]{1,0:T(8,128)(2,1)S(1)} %pad_maximum_fusion.5.kv_ref), custom_call_target="tpu_custom_call" | custom-call | flops 1073741824 | bytes 1310720 | tf_op jit(solution)/shard_map/pallas_call | solution.py:423
  11.5 7.3 %collective-permute-done.4.kv_ref = bf16[512,256]{1,0:T(8,128)(2,1)S(1)} collective-permute-done((bf16[512,256]{1,0:T(8,128)(2,1)S(1)}, bf16[512,256]{1,0:T(8,128)(2,1)S(1)}, u32[]{:S(2)}, u32[]{:S(2)}) %collective-permute-start.4) | collective-permute-done | bytes 262176 | tf_op jit(solution)/shard_map/ppermute | solution.py:456
  18.8 0.7 collective-permute-start.5
  19.4 0.4 collective-permute-done.6.kv_ref
  19.8 4.0 %shard_map.114 = (f32[1024,512]{1,0:T(8,128)S(1)}, f32[8,512]{1,0:T(8,128)S(1)}, f32[8,512]{1,0:T(8,128)S(1)}) custom-call(s32[1]{0:T(128)} %bitcast.2.flag, bf16[512,2048]{1,0:T(8,128)(2,1)S(1)} %get-tuple-element.47.qs_ref, bf16[512,256]{1,0:T(8,128)(2,1)S(1)} %collective-permute-done.6.kv_ref, ...), custom_call_target="tpu_custom_call", output_to_operand_aliasing={{0}: (3, {}), {1}: (4, {}), {2}: (5, {})} | custom-call | flops 1073741824 | bytes 4489220 | tf_op jit(solution)/shard_map/pallas_call | solution.py:423
  23.8 0.3 shard_map.115
  24.1 0.3 broadcast_select_fusion.3
  24.5 2.0 %shard_map.111 = (f32[128,1024]{1,0:T(8,128)S(1)}, f32[144,1024]{1,0:T(8,128)S(1)}, f32[512,1024]{1,0:T(8,128)S(1)}) custom-call(bf16[512,1024]{1,0:T(8,128)(2,1)S(1)} %pad_maximum_fusion.1.x_ref, bf16[512,128]{1,0:T(8,128)(2,1)S(1)} %pad_maximum_fusion.8.w_ref, f32[16,512]{1,0:T(8,128)S(1)} %pad_maximum_fusion.13.ls_ref, ...), custom_call_target="tpu_custom_call" | custom-call | flops 536870912 | bytes 1245184 | tf_op jit(solution)/shard_map/pallas_call | solution.py:423
  26.7 6.9 %shard_map.112 = (f32[512,1024]{1,0:T(8,128)S(1)}, f32[512,1024]{1,0:T(8,128)S(1)}, f32[512,1024]{1,0:T(8,128)S(1)}, f32[16,512]{1,0:T(8,128)S(1)}) custom-call(bf16[512,1024]{1,0:T(8,128)(2,1)S(1)} %pad_maximum_fusion.1.x_ref, bf16[512,128]{1,0:T(8,128)(2,1)S(1)} %pad_maximum_fusion.8.w_ref, bf16[512,128]{1,0:T(8,128)(2,1)S(1)} %pad_maximum_fusion.9.r_ref, ...), custom_call_target="tpu_custom_call" | custom-call | flops 1073741824 | bytes 1900544 | tf_op jit(solution)/shard_map/pallas_call | solution.py:423
  33.6 0.5 shard_map.116
  34.0 1.2 collective-permute-done.7
  35.3 0.2 shard_map.117
  35.5 10.5 %collective-permute-start.8 = (f16[144,1024]{1,0:T(8,128)(2,1)S(1)}, f16[144,1024]{1,0:T(8,128)(2,1)S(1)}, u32[]{:S(2)}, u32[]{:S(2)}) collective-permute-start(f16[144,1024]{1,0:T(8,128)(2,1)S(1)} %convert_element_type.56), channel_id=1, source_target_pairs={{0,4},{1,5},{2,6},{3,7},{4,0},{5,1},{6,2},{7,3},{8,12},{9,13},{10,... | collective-permute-start | bytes 884744 | tf_op jit(solution)/shard_map/ppermute | solution.py:456
  46.1 12.7 %collective-permute-done.8 = f16[144,1024]{1,0:T(8,128)(2,1)S(1)} collective-permute-done((f16[144,1024]{1,0:T(8,128)(2,1)S(1)}, f16[144,1024]{1,0:T(8,128)(2,1)S(1)}, u32[]{:S(2)}, u32[]{:S(2)}) %collective-permute-start.8) | collective-permute-done | bytes 294944 | tf_op jit(solution)/shard_map/ppermute | solution.py:456
  59.0 0.1 fusion.sin_ref
  59.1 1.5 %shard_map.118 = (f32[512,1024]{1,0:T(8,128)S(1)}, f32[128,1024]{1,0:T(8,128)S(1)}, f32[144,1024]{1,0:T(8,128)S(1)}) custom-call(f32[512,1024]{1,0:T(8,128)S(1)} %get-tuple-element.45.y_ref, f32[1024,512]{1,0:T(8,128)S(1)} %get-tuple-element.58.acc_ref, f32[8,512]{1,0:T(8,128)S(1)} %get-tuple-element.59.l_ref, bf16[512,128]{1,0:T(8,128)(2,1)S(1)} %pad_maximum_fusion.9.r_ref, ...), custom_call_target="tpu_custom_call" | custom-call | flops 1073741824 | bytes 6963200 | tf_op jit(solution)/shard_map/pallas_call | solution.py:423
  60.6 0.8 copy-done.2
  61.4 8.2 %shard_map.119 = (f32[512,1024]{1,0:T(8,128)S(1)}, f32[512,128]{1,0:T(8,128)S(1)}, f32[512,128]{1,0:T(8,128)S(1)}) custom-call(f32[512,1024]{1,0:T(8,128)S(1)} %get-tuple-element.62.res_ref, bf16[512,1024]{1,0:T(8,128)(2,1)S(1)} %pad_maximum_fusion.1.x_ref, bf16[512,128]{1,0:T(8,128)(2,1)S(1)} %pad_maximum_fusion.8.w_ref, ...), custom_call_target="tpu_custom_call" | custom-call | flops 2147483648 | bytes 11304960 | tf_op jit(solution)/shard_map/pallas_call | solution.py:423
  69.6 0.8 copy-done.5
  70.5 0.1 collective-permute-start.14
  70.6 1.2 convert_element_type.58
  71.7 2.3 %collective-permute-start.10 = (f16[144,1024]{1,0:T(8,128)(2,1)S(1)}, f16[144,1024]{1,0:T(8,128)(2,1)S(1)}, u32[]{:S(2)}, u32[]{:S(2)}) collective-permute-start(f16[144,1024]{1,0:T(8,128)(2,1)S(1)} %convert_element_type.58), channel_id=1, source_target_pairs={{0,2},{1,3},{2,0},{3,1},{4,6},{5,7},{6,4},{7,5},{8,10},{9,11},{10,... | collective-permute-start | bytes 884744 | tf_op jit(solution)/shard_map/ppermute | solution.py:456
  74.0 1.0 shard_map.120
  75.0 1.3 %collective-permute-start.11 = (f16[144,1024]{1,0:T(8,128)(2,1)S(1)}, f16[144,1024]{1,0:T(8,128)(2,1)S(1)}, u32[]{:S(2)}, u32[]{:S(2)}) collective-permute-start(f16[144,1024]{1,0:T(8,128)(2,1)S(1)} %convert_element_type.58), channel_id=1, source_target_pairs={{0,4},{1,5},{2,6},{3,7},{4,0},{5,1},{6,2},{7,3},{8,12},{9,13},{10,... | collective-permute-start | bytes 884744 | tf_op jit(solution)/shard_map/ppermute | solution.py:456
  76.3 0.6 collective-permute-start.12
  76.9 1.0 dynamic-slice_add_fusion
  77.9 8.1 %collective-permute-done.10 = f16[144,1024]{1,0:T(8,128)(2,1)S(1)} collective-permute-done((f16[144,1024]{1,0:T(8,128)(2,1)S(1)}, f16[144,1024]{1,0:T(8,128)(2,1)S(1)}, u32[]{:S(2)}, u32[]{:S(2)}) %collective-permute-start.10) | collective-permute-done | bytes 294944 | tf_op jit(solution)/shard_map/ppermute | solution.py:456
  85.9 10.4 %collective-permute-done.11 = f16[144,1024]{1,0:T(8,128)(2,1)S(1)} collective-permute-done((f16[144,1024]{1,0:T(8,128)(2,1)S(1)}, f16[144,1024]{1,0:T(8,128)(2,1)S(1)}, u32[]{:S(2)}, u32[]{:S(2)}) %collective-permute-start.11) | collective-permute-done | bytes 294944 | tf_op jit(solution)/shard_map/ppermute | solution.py:456
  96.4 6.8 %collective-permute-done.12 = f16[144,1024]{1,0:T(8,128)(2,1)S(1)} collective-permute-done((f16[144,1024]{1,0:T(8,128)(2,1)S(1)}, f16[144,1024]{1,0:T(8,128)(2,1)S(1)}, u32[]{:S(2)}, u32[]{:S(2)}) %collective-permute-start.12) | collective-permute-done | bytes 294944 | tf_op jit(solution)/shard_map/ppermute | solution.py:456
  103.2 0.2 multiply_add_fusion
  103.4 1.6 %collective-permute-start.19 = (f32[128,128]{1,0:T(8,128)S(1)}, f32[128,128]{1,0:T(8,128)S(1)}, u32[]{:S(2)}, u32[]{:S(2)}) collective-permute-start(f32[128,128]{1,0:T(8,128)S(1)} %get-tuple-element.96), channel_id=1, source_target_pairs={{0,8},{8,0},{16,24},{24,16},{1,9},{9,1},{17,25},{25,17},{2,10},{10... | collective-permute-start | bytes 196616 | tf_op jit(solution)/shard_map/ppermute | solution.py:594
  105.0 1.5 %collective-permute-start.21 = (f32[128,128]{1,0:T(8,128)S(1)}, f32[128,128]{1,0:T(8,128)S(1)}, u32[]{:S(2)}, u32[]{:S(2)}) collective-permute-start(f32[128,128]{1,0:T(8,128)S(1)} %get-tuple-element.97), channel_id=1, source_target_pairs={{0,16},{8,24},{16,0},{24,8},{1,17},{9,25},{17,1},{25,9},{2,18},{10... | collective-permute-start | bytes 196616 | tf_op jit(solution)/shard_map/ppermute | solution.py:594
  106.7 1.3 %collective-permute-done.19 = f32[128,128]{1,0:T(8,128)S(1)} collective-permute-done((f32[128,128]{1,0:T(8,128)S(1)}, f32[128,128]{1,0:T(8,128)S(1)}, u32[]{:S(2)}, u32[]{:S(2)}) %collective-permute-start.19) | collective-permute-done | bytes 65568 | tf_op jit(solution)/shard_map/ppermute | solution.py:594
  108.0 1.3 %collective-permute-done.21 = f32[128,128]{1,0:T(8,128)S(1)} collective-permute-done((f32[128,128]{1,0:T(8,128)S(1)}, f32[128,128]{1,0:T(8,128)S(1)}, u32[]{:S(2)}, u32[]{:S(2)}) %collective-permute-start.21) | collective-permute-done | bytes 65568 | tf_op jit(solution)/shard_map/ppermute | solution.py:594
  109.3 1.6 %collective-permute-start.20 = (f32[128,128]{1,0:T(8,128)S(1)}, f32[128,128]{1,0:T(8,128)S(1)}, u32[]{:S(2)}, u32[]{:S(2)}) collective-permute-start(f32[128,128]{1,0:T(8,128)S(1)} %get-tuple-element.94), channel_id=1, source_target_pairs={{0,16},{8,24},{16,0},{24,8},{1,17},{9,25},{17,1},{25,9},{2,18},{10... | collective-permute-start | bytes 196616 | tf_op jit(solution)/shard_map/ppermute | solution.py:594
  110.9 0.5 collective-permute-start.22
  111.4 0.1 broadcast_select_fusion.5
  111.5 0.1 pad_maximum_fusion.3.g_ref
  111.6 0.8 shard_map.122
  112.3 1.6 %collective-permute-start.15 = (f32[128,128]{1,0:T(8,128)S(1)}, f32[128,128]{1,0:T(8,128)S(1)}, u32[]{:S(2)}, u32[]{:S(2)}) collective-permute-start(f32[128,128]{1,0:T(8,128)S(1)} %get-tuple-element.75), channel_id=1, source_target_pairs={{0,8},{8,0},{16,24},{24,16},{1,9},{9,1},{17,25},{25,17},{2,10},{10... | collective-permute-start | bytes 196616 | tf_op jit(solution)/shard_map/ppermute | solution.py:594
  113.9 0.5 collective-permute-start.17
  114.4 0.8 collective-permute-done.22
  115.2 1.5 %collective-permute-done.15 = f32[128,128]{1,0:T(8,128)S(1)} collective-permute-done((f32[128,128]{1,0:T(8,128)S(1)}, f32[128,128]{1,0:T(8,128)S(1)}, u32[]{:S(2)}, u32[]{:S(2)}) %collective-permute-start.15) | collective-permute-done | bytes 65568 | tf_op jit(solution)/shard_map/ppermute | solution.py:594
  116.7 0.6 collective-permute-start.16
  117.3 1.5 %collective-permute-done.17 = f32[128,128]{1,0:T(8,128)S(1)} collective-permute-done((f32[128,128]{1,0:T(8,128)S(1)}, f32[128,128]{1,0:T(8,128)S(1)}, u32[]{:S(2)}, u32[]{:S(2)}) %collective-permute-start.17) | collective-permute-done | bytes 65568 | tf_op jit(solution)/shard_map/ppermute | solution.py:594
  118.7 0.1 collective-permute-start.18
  118.8 0.7 pad_maximum_fusion.11
  119.5 1.5 %collective-permute-done.16 = f32[128,128]{1,0:T(8,128)S(1)} collective-permute-done((f32[128,128]{1,0:T(8,128)S(1)}, f32[128,128]{1,0:T(8,128)S(1)}, u32[]{:S(2)}, u32[]{:S(2)}) %collective-permute-start.16) | collective-permute-done | bytes 65568 | tf_op jit(solution)/shard_map/ppermute | solution.py:594
  121.0 2.1 %collective-permute-done.18 = f32[128,128]{1,0:T(8,128)S(1)} collective-permute-done((f32[128,128]{1,0:T(8,128)S(1)}, f32[128,128]{1,0:T(8,128)S(1)}, u32[]{:S(2)}, u32[]{:S(2)}) %collective-permute-start.18) | collective-permute-done | bytes 65568 | tf_op jit(solution)/shard_map/ppermute | solution.py:594
  123.1 0.7 pad_maximum_fusion.10
  123.8 0.2 dynamic-slice_select_fusion.1
  124.0 0.2 pad_maximum_fusion.back_ref
  124.2 2.2 %shard_map.121 = (f32[256,2048]{1,0:T(8,128)}, f32[32,256]{1,0:T(8,128)}) custom-call(f32[256,2048]{1,0:T(8,128)S(1)} %pad_maximum_fusion.back_ref, f32[256,2048]{1,0:T(8,128)S(1)} %get-tuple-element.68.wexp_ref, bf16[256,2048]{1,0:T(8,128)(2,1)S(1)} %copy-done, bf16[256,128]{1,0:T(8,128)(2,1)S(1)} %copy-done.1, f32[128,2048]{1,0:T(8,128)S(1)} %pad_maximum_fusion.3.g_ref), custom_call_target="tpu_custom_call" | custom-call | flops 1073741824 | bytes 6356992 | tf_op jit(solution)/shard_map/pallas_call | solution.py:423
  (67 shorter events, 1.2 us)
Async XLA Ops:
  0.6 7.2 %copy-start = (bf16[256,2048]{1,0:T(8,128)(2,1)S(1)}, bf16[256,2048]{1,0:T(8,128)(2,1)}, u32[]{:S(2)}) copy-start(bf16[256,2048]{1,0:T(8,128)(2,1)} %x_ref.3) | copy-start | bytes 3145732
  0.6 3.6 %copy-start.7 = (bf16[256,2048]{1,0:T(8,128)(2,1)S(1)}, bf16[256,2048]{1,0:T(8,128)(2,1)}, u32[]{:S(2)}) copy-start(bf16[256,2048]{1,0:T(8,128)(2,1)} %param.8) | copy-start | bytes 3145732
  1.6 1.6 %collective-permute-start.2 = (f32[64,256]{1,0:T(8,128)S(1)}, f32[64,256]{1,0:T(8,128)S(1)}, u32[]{:S(2)}, u32[]{:S(2)}) collective-permute-start(f32[64,256]{1,0:T(8,128)S(1)} %pad_maximum_fusion.12), channel_id=1, source_target_pairs={{0,1},{1,0},{2,3},{3,2},{4,5},{5,4},{6,7},{7,6},{8,9},{9,8},{10,11... | collective-permute-start | bytes 196616 | tf_op jit(solution)/shard_map/ppermute | solution.py:456
  1.6 6.2 %copy-start.1 = (bf16[256,128]{1,0:T(8,128)(2,1)S(1)}, bf16[256,128]{1,0:T(8,128)(2,1)}, u32[]{:S(2)}) copy-start(bf16[256,128]{1,0:T(8,128)(2,1)} %w_ref.1) | copy-start | bytes 196612
  1.6 6.2 %copy-start.8 = (bf16[256,128]{1,0:T(8,128)(2,1)S(1)}, bf16[256,128]{1,0:T(8,128)(2,1)}, u32[]{:S(2)}) copy-start(bf16[256,128]{1,0:T(8,128)(2,1)} %param.13) | copy-start | bytes 196612
  2.6 1.5 %collective-permute-start = (bf16[256,256]{1,0:T(8,128)(2,1)S(1)}, bf16[256,256]{1,0:T(8,128)(2,1)S(1)}, u32[]{:S(2)}, u32[]{:S(2)}) collective-permute-start(bf16[256,256]{1,0:T(8,128)(2,1)S(1)} %pad_maximum_fusion.7), channel_id=1, source_target_pairs={{0,1},{1,0},{2,3},{3,2},{4,5},{5,4},{6,7},{7,6},{8,9},{9,8},{10,11... | collective-permute-start | bytes 393224 | tf_op jit(solution)/shard_map/ppermute | solution.py:456
  4.3 3.7 %collective-permute-start.3 = (bf16[256,1024]{1,0:T(8,128)(2,1)S(1)}, bf16[256,1024]{1,0:T(8,128)(2,1)S(1)}, u32[]{:S(2)}, u32[]{:S(2)}) collective-permute-start(bf16[256,1024]{1,0:T(8,128)(2,1)S(1)} %constant_dynamic-slice_fusion.2), channel_id=1, source_target_pairs={{0,1},{1,0},{2,3},{3,2},{4,5},{5,4},{6,7},{7,6},{8,9},{9,8},{10,11... | collective-permute-start | bytes 1572872 | tf_op jit(solution)/shard_map/ppermute | solution.py:456
  4.7 14.0 %collective-permute-start.4 = (bf16[512,256]{1,0:T(8,128)(2,1)S(1)}, bf16[512,256]{1,0:T(8,128)(2,1)S(1)}, u32[]{:S(2)}, u32[]{:S(2)}) collective-permute-start(bf16[512,256]{1,0:T(8,128)(2,1)S(1)} %pad_maximum_fusion.5.kv_ref), channel_id=1, source_target_pairs={{0,4},{1,5},{2,6},{3,7},{4,0},{5,1},{6,2},{7,3},{8,12},{9,13},{10,... | collective-permute-start | bytes 786440 | tf_op jit(solution)/shard_map/ppermute | solution.py:456
  7.3 12.5 %collective-permute-start.6 = (bf16[512,256]{1,0:T(8,128)(2,1)S(1)}, bf16[512,256]{1,0:T(8,128)(2,1)S(1)}, u32[]{:S(2)}, u32[]{:S(2)}) collective-permute-start(bf16[512,256]{1,0:T(8,128)(2,1)S(1)} %pad_maximum_fusion.5.kv_ref), channel_id=1, source_target_pairs={{0,2},{1,3},{2,0},{3,1},{4,6},{5,7},{6,4},{7,5},{8,10},{9,11},{10,... | collective-permute-start | bytes 786440 | tf_op jit(solution)/shard_map/ppermute | solution.py:456
  7.9 16.2 %collective-permute-start.1 = (bf16[256,1280]{1,0:T(8,128)(2,1)S(1)}, bf16[256,1280]{1,0:T(8,128)(2,1)S(1)}, u32[]{:S(2)}, u32[]{:S(2)}) collective-permute-start(bf16[256,1280]{1,0:T(8,128)(2,1)S(1)} %pad_maximum_fusion.4), channel_id=1, source_target_pairs={{0,1},{1,0},{2,3},{3,2},{4,5},{5,4},{6,7},{7,6},{8,9},{9,8},{10,11... | collective-permute-start | bytes 1966088 | tf_op jit(solution)/shard_map/ppermute | solution.py:456
  18.8 14.8 %collective-permute-start.5 = (bf16[512,256]{1,0:T(8,128)(2,1)S(1)}, bf16[512,256]{1,0:T(8,128)(2,1)S(1)}, u32[]{:S(2)}, u32[]{:S(2)}) collective-permute-start(bf16[512,256]{1,0:T(8,128)(2,1)S(1)} %collective-permute-done.4.kv_ref), channel_id=1, source_target_pairs={{4,6},{5,7},{6,4},{7,5},{12,14},{13,15},{14,12},{15,13},{20,22},{2... | collective-permute-start | bytes 786440 | tf_op jit(solution)/shard_map/ppermute | solution.py:480
  26.6 8.7 %collective-permute-start.7 = (f16[144,1024]{1,0:T(8,128)(2,1)S(1)}, f16[144,1024]{1,0:T(8,128)(2,1)S(1)}, u32[]{:S(2)}, u32[]{:S(2)}) collective-permute-start(f16[144,1024]{1,0:T(8,128)(2,1)S(1)} %convert_element_type.54), channel_id=1, source_target_pairs={{0,2},{1,3},{2,0},{3,1},{4,6},{5,7},{6,4},{7,5},{8,10},{9,11},{10,... | collective-permute-start | bytes 884744 | tf_op jit(solution)/shard_map/ppermute | solution.py:456
  35.5 23.3 %collective-permute-start.8 = (f16[144,1024]{1,0:T(8,128)(2,1)S(1)}, f16[144,1024]{1,0:T(8,128)(2,1)S(1)}, u32[]{:S(2)}, u32[]{:S(2)}) collective-permute-start(f16[144,1024]{1,0:T(8,128)(2,1)S(1)} %convert_element_type.56), channel_id=1, source_target_pairs={{0,4},{1,5},{2,6},{3,7},{4,0},{5,1},{6,2},{7,3},{8,12},{9,13},{10,... | collective-permute-start | bytes 884744 | tf_op jit(solution)/shard_map/ppermute | solution.py:456
  60.6 0.8 copy-start.2
  69.6 4.4 %copy-start.3 = (f32[32,256]{1,0:T(8,128)S(1)}, f32[32,256]{1,0:T(8,128)}, u32[]{:S(2)}) copy-start(f32[32,256]{1,0:T(8,128)} %ld_ref.1) | copy-start | bytes 98308
  69.6 4.4 %copy-start.4 = (f32[32,256]{1,0:T(8,128)S(1)}, f32[32,256]{1,0:T(8,128)}, u32[]{:S(2)}) copy-start(f32[32,256]{1,0:T(8,128)} %ls_ref.1) | copy-start | bytes 98308
  69.6 0.8 copy-start.5
  70.5 6.4 %collective-permute-start.14 = (f32[256,256]{1,0:T(8,128)S(1)}, f32[256,256]{1,0:T(8,128)}, u32[]{:S(2)}, u32[]{:S(2)}) collective-permute-start(f32[256,256]{1,0:T(8,128)S(1)} %constant_dynamic-slice_fusion), channel_id=1, source_target_pairs={{0,1},{1,0},{2,3},{3,2},{4,5},{5,4},{6,7},{7,6},{8,9},{9,8},{10,11... | collective-permute-start | bytes 786440 | tf_op jit(solution)/shard_map/ppermute | solution.py:456
  70.5 6.3 %copy-start.6 = (f32[512,256]{1,0:T(8,128)S(1)}, f32[512,256]{1,0:T(8,128)}, u32[]{:S(2)}) copy-start(f32[512,256]{1,0:T(8,128)} %copy-done.5) | copy-start | bytes 1572868
  71.7 14.2 %collective-permute-start.10 = (f16[144,1024]{1,0:T(8,128)(2,1)S(1)}, f16[144,1024]{1,0:T(8,128)(2,1)S(1)}, u32[]{:S(2)}, u32[]{:S(2)}) collective-permute-start(f16[144,1024]{1,0:T(8,128)(2,1)S(1)} %convert_element_type.58), channel_id=1, source_target_pairs={{0,2},{1,3},{2,0},{3,1},{4,6},{5,7},{6,4},{7,5},{8,10},{9,11},{10,... | collective-permute-start | bytes 884744 | tf_op jit(solution)/shard_map/ppermute | solution.py:456
  75.0 21.4 %collective-permute-start.11 = (f16[144,1024]{1,0:T(8,128)(2,1)S(1)}, f16[144,1024]{1,0:T(8,128)(2,1)S(1)}, u32[]{:S(2)}, u32[]{:S(2)}) collective-permute-start(f16[144,1024]{1,0:T(8,128)(2,1)S(1)} %convert_element_type.58), channel_id=1, source_target_pairs={{0,4},{1,5},{2,6},{3,7},{4,0},{5,1},{6,2},{7,3},{8,12},{9,13},{10,... | collective-permute-start | bytes 884744 | tf_op jit(solution)/shard_map/ppermute | solution.py:456
  76.3 26.9 %collective-permute-start.12 = (f16[144,1024]{1,0:T(8,128)(2,1)S(1)}, f16[144,1024]{1,0:T(8,128)(2,1)S(1)}, u32[]{:S(2)}, u32[]{:S(2)}) collective-permute-start(f16[144,1024]{1,0:T(8,128)(2,1)S(1)} %convert_element_type.58), channel_id=1, source_target_pairs={{0,6},{1,7},{2,4},{3,5},{4,2},{5,3},{6,0},{7,1},{8,14},{9,15},{10,... | collective-permute-start | bytes 884744 | tf_op jit(solution)/shard_map/ppermute | solution.py:456
  103.4 8.1 %collective-permute-start.13 = (f32[128,1024]{1,0:T(8,128)S(1)}, f32[128,1024]{1,0:T(8,128)S(1)}, u32[]{:S(2)}, u32[]{:S(2)}) collective-permute-start(f32[128,1024]{1,0:T(8,128)S(1)} %multiply_add_fusion), channel_id=1, source_target_pairs={{0,1},{1,0},{2,3},{3,2},{4,5},{5,4},{6,7},{7,6},{8,9},{9,8},{10,11... | collective-permute-start | bytes 1572872 | tf_op jit(solution)/shard_map/ppermute | solution.py:456
  103.4 4.6 %collective-permute-start.19 = (f32[128,128]{1,0:T(8,128)S(1)}, f32[128,128]{1,0:T(8,128)S(1)}, u32[]{:S(2)}, u32[]{:S(2)}) collective-permute-start(f32[128,128]{1,0:T(8,128)S(1)} %get-tuple-element.96), channel_id=1, source_target_pairs={{0,8},{8,0},{16,24},{24,16},{1,9},{9,1},{17,25},{25,17},{2,10},{10... | collective-permute-start | bytes 196616 | tf_op jit(solution)/shard_map/ppermute | solution.py:594
  105.0 4.3 %collective-permute-start.21 = (f32[128,128]{1,0:T(8,128)S(1)}, f32[128,128]{1,0:T(8,128)S(1)}, u32[]{:S(2)}, u32[]{:S(2)}) collective-permute-start(f32[128,128]{1,0:T(8,128)S(1)} %get-tuple-element.97), channel_id=1, source_target_pairs={{0,16},{8,24},{16,0},{24,8},{1,17},{9,25},{17,1},{25,9},{2,18},{10... | collective-permute-start | bytes 196616 | tf_op jit(solution)/shard_map/ppermute | solution.py:594
  106.6 17.2 %collective-permute-start.9 = (f32[256,1024]{1,0:T(8,128)S(1)}, f32[256,1024]{1,0:T(8,128)S(1)}, u32[]{:S(2)}, u32[]{:S(2)}) collective-permute-start(f32[256,1024]{1,0:T(8,128)S(1)} %constant_dynamic-slice_fusion.1), channel_id=1, source_target_pairs={{0,1},{1,0},{2,3},{3,2},{4,5},{5,4},{6,7},{7,6},{8,9},{9,8},{10,11... | collective-permute-start | bytes 3145736 | tf_op jit(solution)/shard_map/ppermute | solution.py:456
  109.3 5.1 %collective-permute-start.20 = (f32[128,128]{1,0:T(8,128)S(1)}, f32[128,128]{1,0:T(8,128)S(1)}, u32[]{:S(2)}, u32[]{:S(2)}) collective-permute-start(f32[128,128]{1,0:T(8,128)S(1)} %get-tuple-element.94), channel_id=1, source_target_pairs={{0,16},{8,24},{16,0},{24,8},{1,17},{9,25},{17,1},{25,9},{2,18},{10... | collective-permute-start | bytes 196616 | tf_op jit(solution)/shard_map/ppermute | solution.py:594
  110.9 4.3 %collective-permute-start.22 = (f32[128,128]{1,0:T(8,128)S(1)}, f32[128,128]{1,0:T(8,128)S(1)}, u32[]{:S(2)}, u32[]{:S(2)}) collective-permute-start(f32[128,128]{1,0:T(8,128)S(1)} %get-tuple-element.95), channel_id=1, source_target_pairs={{0,8},{8,0},{16,24},{24,16},{1,9},{9,1},{17,25},{25,17},{2,10},{10... | collective-permute-start | bytes 196616 | tf_op jit(solution)/shard_map/ppermute | solution.py:594
  112.3 4.3 %collective-permute-start.15 = (f32[128,128]{1,0:T(8,128)S(1)}, f32[128,128]{1,0:T(8,128)S(1)}, u32[]{:S(2)}, u32[]{:S(2)}) collective-permute-start(f32[128,128]{1,0:T(8,128)S(1)} %get-tuple-element.75), channel_id=1, source_target_pairs={{0,8},{8,0},{16,24},{24,16},{1,9},{9,1},{17,25},{25,17},{2,10},{10... | collective-permute-start | bytes 196616 | tf_op jit(solution)/shard_map/ppermute | solution.py:594
  113.9 4.8 %collective-permute-start.17 = (f32[128,128]{1,0:T(8,128)S(1)}, f32[128,128]{1,0:T(8,128)S(1)}, u32[]{:S(2)}, u32[]{:S(2)}) collective-permute-start(f32[128,128]{1,0:T(8,128)S(1)} %get-tuple-element.76), channel_id=1, source_target_pairs={{0,16},{8,24},{16,0},{24,8},{1,17},{9,25},{17,1},{25,9},{2,18},{10... | collective-permute-start | bytes 196616 | tf_op jit(solution)/shard_map/ppermute | solution.py:594
  116.7 4.3 %collective-permute-start.16 = (f32[128,128]{1,0:T(8,128)S(1)}, f32[128,128]{1,0:T(8,128)S(1)}, u32[]{:S(2)}, u32[]{:S(2)}) collective-permute-start(f32[128,128]{1,0:T(8,128)S(1)} %add.142), channel_id=1, source_target_pairs={{0,16},{8,24},{16,0},{24,8},{1,17},{9,25},{17,1},{25,9},{2,18},{10... | collective-permute-start | bytes 196616 | tf_op jit(solution)/shard_map/ppermute | solution.py:594
  118.7 4.3 %collective-permute-start.18 = (f32[128,128]{1,0:T(8,128)S(1)}, f32[128,128]{1,0:T(8,128)S(1)}, u32[]{:S(2)}, u32[]{:S(2)}) collective-permute-start(f32[128,128]{1,0:T(8,128)S(1)} %add.144), channel_id=1, source_target_pairs={{0,8},{8,0},{16,24},{24,16},{1,9},{9,1},{17,25},{25,17},{2,10},{10... | collective-permute-start | bytes 196616 | tf_op jit(solution)/shard_map/ppermute | solution.py:594

commit v6 on v5

--- a/solution.py
+++ b/solution.py
@@ -314,7 +314,7 @@
 
 def back_kernel(
     res_ref, x_ref, w_ref, r_ref, clsx_ref, crow_ref, fs_ref, wexp_ref, sin_ref, st0_ref, d1_ref,
-    back_ref, gw_ref, gr_ref, a_ref, pair,
+    back_ref, shared_ref, a_ref, pair,
 ):
     t = x_ref.shape[0] // 2
     th = t // 2
@@ -379,9 +379,10 @@
 
         lax.fori_loop(0, width // 256, two, 0)
         ph, plo = split2(jnp.where(keep, pair[...], 0.0))
-        gr_ref[rows, :] = gr + tn(ph, w) + tn(plo, w)
+        n = w.shape[1]
         mixed = nn(ph, r) + nn(plo, r)
-        gw_ref[rows, :] = mixed if gw is None else mixed + gw
+        shared_ref[rows, :n] = mixed if gw is None else mixed + gw
+        shared_ref[rows, n:] = gr + tn(ph, w) + tn(plo, w)
 
 
 def ready_kernel(x_ref, ls_ref, ld_ref, extra_ref, wexp_ref, xh_ref, xl_ref):
@@ -487,10 +488,10 @@
 
     kv = joined(kv_half(core), swap(kv_half(1 - core), 1))
     keys_near = near(kv)
-    x1, q1, wr1, rd1, _ = lax.optimization_barrier((x, q, wr, rd, kv))
-    rates = swap(jnp.concatenate([ls, ld], axis=0), 1)
-    lsc = joined(half(ls, core, hh, 0), half(rates, core, hh, 0), 1)
-    ldc = joined(half(ld, core, hh, 0), half(rates[heads:], core, hh, 0), 1)
+    x1, q1, wr1, rd1, ls1, ld1, _ = lax.optimization_barrier((x, q, wr, rd, ls, ld, kv))
+    rates = swap(jnp.concatenate([ls1, ld1], axis=0), 1)
+    lsc = joined(half(ls1, core, hh, 0), half(rates, core, hh, 0), 1)
+    ldc = joined(half(ld1, core, hh, 0), half(rates[heads:], core, hh, 0), 1)
     mates = swap(jnp.concatenate([half(x1, 1 - core, hc), wr1, rd1], axis=1), 1)
     xc = joined(half(x1, core, hc), mates[:, :hc])
     wc = joined(wr1, mates[:, hc : hc + n])
@@ -550,10 +551,13 @@
     far = relay(keys_near, soft[1])
 
     def combine(got):
+        flat = jnp.concatenate([g.astype(F32) for g in got], axis=0)
+        flat = lax.optimization_barrier(flat)
         out = 0.0
-        for d, g in enumerate(got, 1):
+        for d in range(1, chips):
             fade = jnp.exp(between(chip, chip ^ d, chips))
-            out += decode(g, n, jnp.where((chip ^ d) > chip, fade, 0.0))
+            at = (d - 1) * (n + 16)
+            out += decode(flat[at : at + n + 16], n, jnp.where((chip ^ d) > chip, fade, 0.0))
         return out
 
     for d, keys in enumerate(far, 1):
@@ -569,9 +573,11 @@
         (ybase, soft[0], soft[2], rc, fs, incoming), flops=8 * mm,
     )
     sent = dcode.astype(F16)
-    coming = [swap(sent, 2 * d) for d in range(1, chips)]
-    back, gw, gr = call(
-        back_kernel, [((2 * t, hc), F32), ((2 * t, n), F32), ((2 * t, n), F32)],
+    coming = []
+    for d in range(1, chips):
+        coming.append(swap(sent, 2 * d))
+    back, shared = call(
+        back_kernel, [((2 * t, hc), F32), ((2 * t, 2 * n), F32)],
         (res, xc, wc, rc, clsx, crow, fs, wexpc, incoming, st0, d1),
         scratch=[pltpu.VMEM((t, t), F32), pltpu.VMEM((t, t), F32)],
         flops=16 * mm,
@@ -598,7 +604,7 @@
         return parts
 
     back_all = joined(*home(back), 1)
-    own, other = home(jnp.concatenate([gw, gr], axis=1))
+    own, other = home(shared)
     grads = own + other
     gw0, gr0 = grads[:, :n], grads[:, n:]
     grad_read = jnp.concatenate(tp_sum([gr0[: t // 2], gr0[t // 2 :]]), axis=0)

time: 127 us -> 125 us (0.984)
  waiting for transfers between devices: 56.9 us -> 55.5 us
    ppermute x14, waiting for transfers between devices: 47 us -> 45.6 us  [swap(): return lax.ppermute(a, 'seq', [(i, i ^ bits) for i in range(count)])]
  transfers between devices with their start and end apart: 23 -> 23, of which waited for: 15 -> 17; matrix products, arithmetic and copies ran while one was open for 5% -> 5% of each run, Pallas kernels for 15% -> 15%
where the time goes in v6:
time: 125 us
  waiting for transfers between devices  55.5 us (44%)
  Pallas kernels  30.4 us (24%)
  starting transfers between devices  27.2 us (22%)
  other arithmetic  6.86 us (5%)
  local copies, waits for them, and re-layouts  3.78 us (3%)
  between operations  1.39 us (1%)
    ppermute x14, waiting for transfers between devices, swap(): return lax.ppermute(a, 'seq', [(i, i ^ bits) for i in range(count)])  45.6 us
    pallas_call x12, Pallas kernels, call(): pl.pallas_call(kernel, out_shape=shapes, in_specs=in_specs or [VM] * len(...  30.4 us
    ppermute x14, starting transfers between devices, swap(): return lax.ppermute(a, 'seq', [(i, i ^ bits) for i in range(count)])  18.6 us
    ppermute x8, waiting for transfers between devices, tp_sum(): lax.ppermute(a, 'tp', [(i, i ^ 1 << (step + k) % bits) for i in range(tp)])  9.95 us
    ppermute x8, starting transfers between devices, tp_sum(): lax.ppermute(a, 'tp', [(i, i ^ 1 << (step + k) % bits) for i in range(tp)])  7.91 us
  transfers between devices with their start and end apart: 23, of which 17 were waited for; matrix products, arithmetic and copies ran while one was open for 5% of the time, Pallas kernels for 15%

profile of v6, /device:TPU:8, one launch (start us, length us, event | category | flops | bytes accessed | tf_op | source)
XLA Modules:
  0.0 125.2 jit_solution(6153645918531334300)
XLA Ops:
  0.7 1.0 constant_dynamic-slice_fusion.7
  1.7 1.0 constant_dynamic-slice_fusion.6
  2.9 1.2 collective-permute-done
  4.2 2.7 %collective-permute-start.4 = (bf16[512,256]{1,0:T(8,128)(2,1)S(1)}, bf16[512,256]{1,0:T(8,128)(2,1)S(1)}, u32[]{:S(2)}, u32[]{:S(2)}) collective-permute-start(bf16[512,256]{1,0:T(8,128)(2,1)S(1)} %pad_maximum_fusion.5.kv_ref), channel_id=1, source_target_pairs={{0,4},{1,5},{2,6},{3,7},{4,0},{5,1},{6,2},{7,3},{8,12},{9,13},{10,... | collective-permute-start | bytes 786440 | tf_op jit(solution)/shard_map/ppermute | solution.py:457
  6.9 0.4 collective-permute-start.6
  7.3 0.8 pad_maximum_fusion.12
  8.2 0.6 collective-permute-start.1
  8.8 0.1 collective-permute-start.3
  8.9 0.4 collective-permute-done.2
  9.3 0.1 slice_reduce_fusion.3
  9.5 1.7 %collective-permute-done.3 = bf16[256,1024]{1,0:T(8,128)(2,1)S(1)} collective-permute-done((bf16[256,1024]{1,0:T(8,128)(2,1)S(1)}, bf16[256,1024]{1,0:T(8,128)(2,1)S(1)}, u32[]{:S(2)}, u32[]{:S(2)}) %collective-permute-start.3) | collective-permute-done | bytes 524320 | tf_op jit(solution)/shard_map/ppermute | solution.py:457
  11.3 0.3 broadcast_select_fusion.1
  11.6 3.1 %shard_map.113 = (bf16[512,2048]{1,0:T(8,128)(2,1)S(1)}, f32[1024,512]{1,0:T(8,128)S(1)}, f32[8,512]{1,0:T(8,128)S(1)}, f32[8,512]{1,0:T(8,128)S(1)}) custom-call(bf16[512,1024]{1,0:T(8,128)(2,1)S(1)} %pad_maximum_fusion.2.q_ref, bf16[512,256]{1,0:T(8,128)(2,1)S(1)} %pad_maximum_fusion.5.kv_ref), custom_call_target="tpu_custom_call" | custom-call | flops 1073741824 | bytes 1310720 | tf_op jit(solution)/shard_map/pallas_call | solution.py:424
  14.7 3.5 %collective-permute-done.4.kv_ref = bf16[512,256]{1,0:T(8,128)(2,1)S(1)} collective-permute-done((bf16[512,256]{1,0:T(8,128)(2,1)S(1)}, bf16[512,256]{1,0:T(8,128)(2,1)S(1)}, u32[]{:S(2)}, u32[]{:S(2)}) %collective-permute-start.4) | collective-permute-done | bytes 262176 | tf_op jit(solution)/shard_map/ppermute | solution.py:457
  18.3 0.7 collective-permute-start.5
  18.9 0.4 collective-permute-done.6.kv_ref
  19.3 4.0 %shard_map.114 = (f32[1024,512]{1,0:T(8,128)S(1)}, f32[8,512]{1,0:T(8,128)S(1)}, f32[8,512]{1,0:T(8,128)S(1)}) custom-call(s32[1]{0:T(128)} %bitcast.2.flag, bf16[512,2048]{1,0:T(8,128)(2,1)S(1)} %get-tuple-element.50.qs_ref, bf16[512,256]{1,0:T(8,128)(2,1)S(1)} %collective-permute-done.6.kv_ref, ...), custom_call_target="tpu_custom_call", output_to_operand_aliasing={{0}: (3, {}), {1}: (4, {}), {2}: (5, {})} | custom-call | flops 1073741824 | bytes 4489220 | tf_op jit(solution)/shard_map/pallas_call | solution.py:424
  23.3 0.3 shard_map.115
  23.6 0.3 broadcast_select_fusion.3
  24.0 2.0 %shard_map.111 = (f32[128,1024]{1,0:T(8,128)S(1)}, f32[144,1024]{1,0:T(8,128)S(1)}, f32[512,1024]{1,0:T(8,128)S(1)}) custom-call(bf16[512,1024]{1,0:T(8,128)(2,1)S(1)} %pad_maximum_fusion.1.x_ref, bf16[512,128]{1,0:T(8,128)(2,1)S(1)} %pad_maximum_fusion.8.w_ref, f32[16,512]{1,0:T(8,128)S(1)} %pad_maximum_fusion.13.ls_ref, ...), custom_call_target="tpu_custom_call" | custom-call | flops 536870912 | bytes 1245184 | tf_op jit(solution)/shard_map/pallas_call | solution.py:424
  26.1 6.9 %shard_map.112 = (f32[512,1024]{1,0:T(8,128)S(1)}, f32[512,1024]{1,0:T(8,128)S(1)}, f32[512,1024]{1,0:T(8,128)S(1)}, f32[16,512]{1,0:T(8,128)S(1)}) custom-call(bf16[512,1024]{1,0:T(8,128)(2,1)S(1)} %pad_maximum_fusion.1.x_ref, bf16[512,128]{1,0:T(8,128)(2,1)S(1)} %pad_maximum_fusion.8.w_ref, bf16[512,128]{1,0:T(8,128)(2,1)S(1)} %pad_maximum_fusion.9.r_ref, ...), custom_call_target="tpu_custom_call" | custom-call | flops 1073741824 | bytes 1900544 | tf_op jit(solution)/shard_map/pallas_call | solution.py:424
  33.0 0.5 shard_map.116
  33.5 1.2 collective-permute-done.7
  34.7 0.2 shard_map.117
  35.0 10.5 %collective-permute-start.8 = (f16[144,1024]{1,0:T(8,128)(2,1)S(1)}, f16[144,1024]{1,0:T(8,128)(2,1)S(1)}, u32[]{:S(2)}, u32[]{:S(2)}) collective-permute-start(f16[144,1024]{1,0:T(8,128)(2,1)S(1)} %convert_element_type.41), channel_id=1, source_target_pairs={{0,4},{1,5},{2,6},{3,7},{4,0},{5,1},{6,2},{7,3},{8,12},{9,13},{10,... | collective-permute-start | bytes 884744 | tf_op jit(solution)/shard_map/ppermute | solution.py:457
  45.6 12.7 %collective-permute-done.8 = f16[144,1024]{1,0:T(8,128)(2,1)S(1)} collective-permute-done((f16[144,1024]{1,0:T(8,128)(2,1)S(1)}, f16[144,1024]{1,0:T(8,128)(2,1)S(1)}, u32[]{:S(2)}, u32[]{:S(2)}) %collective-permute-start.8) | collective-permute-done | bytes 294944 | tf_op jit(solution)/shard_map/ppermute | solution.py:457
  58.4 0.1 fusion.2.sin_ref
  58.6 1.5 %shard_map.118 = (f32[512,1024]{1,0:T(8,128)S(1)}, f32[128,1024]{1,0:T(8,128)S(1)}, f32[144,1024]{1,0:T(8,128)S(1)}) custom-call(f32[512,1024]{1,0:T(8,128)S(1)} %get-tuple-element.48.y_ref, f32[1024,512]{1,0:T(8,128)S(1)} %get-tuple-element.61.acc_ref, f32[8,512]{1,0:T(8,128)S(1)} %get-tuple-element.62.l_ref, bf16[512,128]{1,0:T(8,128)(2,1)S(1)} %pad_maximum_fusion.9.r_ref, ...), custom_call_target="tpu_custom_call" | custom-call | flops 1073741824 | bytes 6963200 | tf_op jit(solution)/shard_map/pallas_call | solution.py:424
  60.1 0.8 copy-done.2
  60.9 8.0 %shard_map.119 = (f32[512,1024]{1,0:T(8,128)S(1)}, f32[512,256]{1,0:T(8,128)S(1)}) custom-call(f32[512,1024]{1,0:T(8,128)S(1)} %get-tuple-element.65.res_ref, bf16[512,1024]{1,0:T(8,128)(2,1)S(1)} %pad_maximum_fusion.1.x_ref, bf16[512,128]{1,0:T(8,128)(2,1)S(1)} %pad_maximum_fusion.8.w_ref, bf16[512,128]{1,0:T(8,128)(2,1)S(1)} %pad_maximum_fusion.9.r_ref, ...), custom_call_target="tpu_custom_call" | custom-call | flops 2147483648 | bytes 11304960 | tf_op jit(solution)/shard_map/pallas_call | solution.py:424
  68.9 0.8 copy-done.3
  69.9 1.2 convert_element_type.43
  71.0 2.3 %collective-permute-start.10 = (f16[144,1024]{1,0:T(8,128)(2,1)S(1)}, f16[144,1024]{1,0:T(8,128)(2,1)S(1)}, u32[]{:S(2)}, u32[]{:S(2)}) collective-permute-start(f16[144,1024]{1,0:T(8,128)(2,1)S(1)} %convert_element_type.43), channel_id=1, source_target_pairs={{0,2},{1,3},{2,0},{3,1},{4,6},{5,7},{6,4},{7,5},{8,10},{9,11},{10,... | collective-permute-start | bytes 884744 | tf_op jit(solution)/shard_map/ppermute | solution.py:457
  73.3 1.3 collective-permute-start.11
  74.5 0.5 collective-permute-start.12
  75.0 1.0 shard_map.120
  76.0 1.0 dynamic-slice_add_fusion
  77.0 9.1 %collective-permute-done.10 = f16[144,1024]{1,0:T(8,128)(2,1)S(1)} collective-permute-done((f16[144,1024]{1,0:T(8,128)(2,1)S(1)}, f16[144,1024]{1,0:T(8,128)(2,1)S(1)}, u32[]{:S(2)}, u32[]{:S(2)}) %collective-permute-start.10) | collective-permute-done | bytes 294944 | tf_op jit(solution)/shard_map/ppermute | solution.py:457
  86.2 8.5 %collective-permute-done.11 = f16[144,1024]{1,0:T(8,128)(2,1)S(1)} collective-permute-done((f16[144,1024]{1,0:T(8,128)(2,1)S(1)}, f16[144,1024]{1,0:T(8,128)(2,1)S(1)}, u32[]{:S(2)}, u32[]{:S(2)}) %collective-permute-start.11) | collective-permute-done | bytes 294944 | tf_op jit(solution)/shard_map/ppermute | solution.py:457
  94.6 6.8 %collective-permute-done.12 = f16[144,1024]{1,0:T(8,128)(2,1)S(1)} collective-permute-done((f16[144,1024]{1,0:T(8,128)(2,1)S(1)}, f16[144,1024]{1,0:T(8,128)(2,1)S(1)}, u32[]{:S(2)}, u32[]{:S(2)}) %collective-permute-start.12) | collective-permute-done | bytes 294944 | tf_op jit(solution)/shard_map/ppermute | solution.py:457
  101.4 0.2 maximum_convert_fusion
  101.7 0.1 fusion
  101.9 1.6 %collective-permute-start.19 = (f32[128,128]{1,0:T(8,128)S(1)}, f32[128,128]{1,0:T(8,128)S(1)}, u32[]{:S(2)}, u32[]{:S(2)}) collective-permute-start(f32[128,128]{1,0:T(8,128)S(1)} %get-tuple-element.101), channel_id=1, source_target_pairs={{0,8},{8,0},{16,24},{24,16},{1,9},{9,1},{17,25},{25,17},{2,10},{10... | collective-permute-start | bytes 196616 | tf_op jit(solution)/shard_map/ppermute | solution.py:600
  103.5 1.5 %collective-permute-start.21 = (f32[128,128]{1,0:T(8,128)S(1)}, f32[128,128]{1,0:T(8,128)S(1)}, u32[]{:S(2)}, u32[]{:S(2)}) collective-permute-start(f32[128,128]{1,0:T(8,128)S(1)} %get-tuple-element.102), channel_id=1, source_target_pairs={{0,16},{8,24},{16,0},{24,8},{1,17},{9,25},{17,1},{25,9},{2,18},{10... | collective-permute-start | bytes 196616 | tf_op jit(solution)/shard_map/ppermute | solution.py:600
  105.2 1.3 %collective-permute-done.19 = f32[128,128]{1,0:T(8,128)S(1)} collective-permute-done((f32[128,128]{1,0:T(8,128)S(1)}, f32[128,128]{1,0:T(8,128)S(1)}, u32[]{:S(2)}, u32[]{:S(2)}) %collective-permute-start.19) | collective-permute-done | bytes 65568 | tf_op jit(solution)/shard_map/ppermute | solution.py:600
  106.5 1.3 %collective-permute-done.21 = f32[128,128]{1,0:T(8,128)S(1)} collective-permute-done((f32[128,128]{1,0:T(8,128)S(1)}, f32[128,128]{1,0:T(8,128)S(1)}, u32[]{:S(2)}, u32[]{:S(2)}) %collective-permute-start.21) | collective-permute-done | bytes 65568 | tf_op jit(solution)/shard_map/ppermute | solution.py:600
  107.8 1.6 %collective-permute-start.20 = (f32[128,128]{1,0:T(8,128)S(1)}, f32[128,128]{1,0:T(8,128)S(1)}, u32[]{:S(2)}, u32[]{:S(2)}) collective-permute-start(f32[128,128]{1,0:T(8,128)S(1)} %get-tuple-element.99), channel_id=1, source_target_pairs={{0,16},{8,24},{16,0},{24,8},{1,17},{9,25},{17,1},{25,9},{2,18},{10... | collective-permute-start | bytes 196616 | tf_op jit(solution)/shard_map/ppermute | solution.py:600
  109.3 0.5 collective-permute-start.22
  109.9 0.2 broadcast_select_fusion.5
  110.1 0.1 pad_maximum_fusion.3.g_ref
  110.2 0.8 shard_map.122
  111.0 1.6 %collective-permute-start.15 = (f32[128,128]{1,0:T(8,128)S(1)}, f32[128,128]{1,0:T(8,128)S(1)}, u32[]{:S(2)}, u32[]{:S(2)}) collective-permute-start(f32[128,128]{1,0:T(8,128)S(1)} %get-tuple-element.77), channel_id=1, source_target_pairs={{0,8},{8,0},{16,24},{24,16},{1,9},{9,1},{17,25},{25,17},{2,10},{10... | collective-permute-start | bytes 196616 | tf_op jit(solution)/shard_map/ppermute | solution.py:600
  112.5 0.5 collective-permute-start.17
  113.0 0.8 collective-permute-done.22
  113.8 1.5 %collective-permute-done.15 = f32[128,128]{1,0:T(8,128)S(1)} collective-permute-done((f32[128,128]{1,0:T(8,128)S(1)}, f32[128,128]{1,0:T(8,128)S(1)}, u32[]{:S(2)}, u32[]{:S(2)}) %collective-permute-start.15) | collective-permute-done | bytes 65568 | tf_op jit(solution)/shard_map/ppermute | solution.py:600
  115.3 0.6 collective-permute-start.16
  115.9 1.6 %collective-permute-done.17 = f32[128,128]{1,0:T(8,128)S(1)} collective-permute-done((f32[128,128]{1,0:T(8,128)S(1)}, f32[128,128]{1,0:T(8,128)S(1)}, u32[]{:S(2)}, u32[]{:S(2)}) %collective-permute-start.17) | collective-permute-done | bytes 65568 | tf_op jit(solution)/shard_map/ppermute | solution.py:600
  117.5 0.7 pad_maximum_fusion.11
  118.2 1.4 %collective-permute-done.16 = f32[128,128]{1,0:T(8,128)S(1)} collective-permute-done((f32[128,128]{1,0:T(8,128)S(1)}, f32[128,128]{1,0:T(8,128)S(1)}, u32[]{:S(2)}, u32[]{:S(2)}) %collective-permute-start.16) | collective-permute-done | bytes 65568 | tf_op jit(solution)/shard_map/ppermute | solution.py:600
  119.7 2.1 %collective-permute-done.18 = f32[128,128]{1,0:T(8,128)S(1)} collective-permute-done((f32[128,128]{1,0:T(8,128)S(1)}, f32[128,128]{1,0:T(8,128)S(1)}, u32[]{:S(2)}, u32[]{:S(2)}) %collective-permute-start.18) | collective-permute-done | bytes 65568 | tf_op jit(solution)/shard_map/ppermute | solution.py:600
  121.8 0.7 pad_maximum_fusion.10
  122.5 0.2 dynamic-slice_select_fusion.1
  122.7 0.2 pad_maximum_fusion.back_ref
  123.0 2.2 %shard_map.121 = (f32[256,2048]{1,0:T(8,128)}, f32[32,256]{1,0:T(8,128)}) custom-call(f32[256,2048]{1,0:T(8,128)S(1)} %pad_maximum_fusion.back_ref, f32[256,2048]{1,0:T(8,128)S(1)} %get-tuple-element.71.wexp_ref, bf16[256,2048]{1,0:T(8,128)(2,1)S(1)} %copy-done, bf16[256,128]{1,0:T(8,128)(2,1)S(1)} %copy-done.1, f32[128,2048]{1,0:T(8,128)S(1)} %pad_maximum_fusion.3.g_ref), custom_call_target="tpu_custom_call" | custom-call | flops 1073741824 | bytes 6356992 | tf_op jit(solution)/shard_map/pallas_call | solution.py:424
  (65 shorter events, 1.4 us)
Async XLA Ops:
  0.6 7.5 %copy-start = (bf16[256,2048]{1,0:T(8,128)(2,1)S(1)}, bf16[256,2048]{1,0:T(8,128)(2,1)}, u32[]{:S(2)}) copy-start(bf16[256,2048]{1,0:T(8,128)(2,1)} %x_ref.3) | copy-start | bytes 3145732
  0.6 7.5 %copy-start.1 = (bf16[256,128]{1,0:T(8,128)(2,1)S(1)}, bf16[256,128]{1,0:T(8,128)(2,1)}, u32[]{:S(2)}) copy-start(bf16[256,128]{1,0:T(8,128)(2,1)} %w_ref.1) | copy-start | bytes 196612
  0.7 7.5 %copy-start.8 = (bf16[256,128]{1,0:T(8,128)(2,1)S(1)}, bf16[256,128]{1,0:T(8,128)(2,1)}, u32[]{:S(2)}) copy-start(bf16[256,128]{1,0:T(8,128)(2,1)} %param.13) | copy-start | bytes 196612
  1.7 7.1 %copy-start.7 = (bf16[256,2048]{1,0:T(8,128)(2,1)S(1)}, bf16[256,2048]{1,0:T(8,128)(2,1)}, u32[]{:S(2)}) copy-start(bf16[256,2048]{1,0:T(8,128)(2,1)} %param.8) | copy-start | bytes 3145732
  2.7 1.4 %collective-permute-start = (bf16[256,256]{1,0:T(8,128)(2,1)S(1)}, bf16[256,256]{1,0:T(8,128)(2,1)S(1)}, u32[]{:S(2)}, u32[]{:S(2)}) collective-permute-start(bf16[256,256]{1,0:T(8,128)(2,1)S(1)} %pad_maximum_fusion.7), channel_id=1, source_target_pairs={{0,1},{1,0},{2,3},{3,2},{4,5},{5,4},{6,7},{7,6},{8,9},{9,8},{10,11... | collective-permute-start | bytes 393224 | tf_op jit(solution)/shard_map/ppermute | solution.py:457
  4.2 5.3 %copy-start.5 = (f32[32,256]{1,0:T(8,128)S(1)}, f32[32,256]{1,0:T(8,128)}, u32[]{:S(2)}) copy-start(f32[32,256]{1,0:T(8,128)} %ld_ref.1) | copy-start | bytes 98308
  4.2 5.3 %copy-start.6 = (f32[32,256]{1,0:T(8,128)S(1)}, f32[32,256]{1,0:T(8,128)}, u32[]{:S(2)}) copy-start(f32[32,256]{1,0:T(8,128)} %ls_ref.1) | copy-start | bytes 98308
  4.2 14.1 %collective-permute-start.4 = (bf16[512,256]{1,0:T(8,128)(2,1)S(1)}, bf16[512,256]{1,0:T(8,128)(2,1)S(1)}, u32[]{:S(2)}, u32[]{:S(2)}) collective-permute-start(bf16[512,256]{1,0:T(8,128)(2,1)S(1)} %pad_maximum_fusion.5.kv_ref), channel_id=1, source_target_pairs={{0,4},{1,5},{2,6},{3,7},{4,0},{5,1},{6,2},{7,3},{8,12},{9,13},{10,... | collective-permute-start | bytes 786440 | tf_op jit(solution)/shard_map/ppermute | solution.py:457
  6.9 12.4 %collective-permute-start.6 = (bf16[512,256]{1,0:T(8,128)(2,1)S(1)}, bf16[512,256]{1,0:T(8,128)(2,1)S(1)}, u32[]{:S(2)}, u32[]{:S(2)}) collective-permute-start(bf16[512,256]{1,0:T(8,128)(2,1)S(1)} %pad_maximum_fusion.5.kv_ref), channel_id=1, source_target_pairs={{0,2},{1,3},{2,0},{3,1},{4,6},{5,7},{6,4},{7,5},{8,10},{9,11},{10,... | collective-permute-start | bytes 786440 | tf_op jit(solution)/shard_map/ppermute | solution.py:457
  8.1 1.3 %collective-permute-start.2 = (f32[64,256]{1,0:T(8,128)S(1)}, f32[64,256]{1,0:T(8,128)S(1)}, u32[]{:S(2)}, u32[]{:S(2)}) collective-permute-start(f32[64,256]{1,0:T(8,128)S(1)} %pad_maximum_fusion.12), channel_id=1, source_target_pairs={{0,1},{1,0},{2,3},{3,2},{4,5},{5,4},{6,7},{7,6},{8,9},{9,8},{10,11... | collective-permute-start | bytes 196616 | tf_op jit(solution)/shard_map/ppermute | solution.py:457
  8.2 15.3 %collective-permute-start.1 = (bf16[256,1280]{1,0:T(8,128)(2,1)S(1)}, bf16[256,1280]{1,0:T(8,128)(2,1)S(1)}, u32[]{:S(2)}, u32[]{:S(2)}) collective-permute-start(bf16[256,1280]{1,0:T(8,128)(2,1)S(1)} %pad_maximum_fusion.4), channel_id=1, source_target_pairs={{0,1},{1,0},{2,3},{3,2},{4,5},{5,4},{6,7},{7,6},{8,9},{9,8},{10,11... | collective-permute-start | bytes 1966088 | tf_op jit(solution)/shard_map/ppermute | solution.py:457
  8.8 2.4 %collective-permute-start.3 = (bf16[256,1024]{1,0:T(8,128)(2,1)S(1)}, bf16[256,1024]{1,0:T(8,128)(2,1)S(1)}, u32[]{:S(2)}, u32[]{:S(2)}) collective-permute-start(bf16[256,1024]{1,0:T(8,128)(2,1)S(1)} %constant_dynamic-slice_fusion.2), channel_id=1, source_target_pairs={{0,1},{1,0},{2,3},{3,2},{4,5},{5,4},{6,7},{7,6},{8,9},{9,8},{10,11... | collective-permute-start | bytes 1572872 | tf_op jit(solution)/shard_map/ppermute | solution.py:457
  18.3 14.8 %collective-permute-start.5 = (bf16[512,256]{1,0:T(8,128)(2,1)S(1)}, bf16[512,256]{1,0:T(8,128)(2,1)S(1)}, u32[]{:S(2)}, u32[]{:S(2)}) collective-permute-start(bf16[512,256]{1,0:T(8,128)(2,1)S(1)} %collective-permute-done.4.kv_ref), channel_id=1, source_target_pairs={{4,6},{5,7},{6,4},{7,5},{12,14},{13,15},{14,12},{15,13},{20,22},{2... | collective-permute-start | bytes 786440 | tf_op jit(solution)/shard_map/ppermute | solution.py:481
  26.0 8.7 %collective-permute-start.7 = (f16[144,1024]{1,0:T(8,128)(2,1)S(1)}, f16[144,1024]{1,0:T(8,128)(2,1)S(1)}, u32[]{:S(2)}, u32[]{:S(2)}) collective-permute-start(f16[144,1024]{1,0:T(8,128)(2,1)S(1)} %convert_element_type.39), channel_id=1, source_target_pairs={{0,2},{1,3},{2,0},{3,1},{4,6},{5,7},{6,4},{7,5},{8,10},{9,11},{10,... | collective-permute-start | bytes 884744 | tf_op jit(solution)/shard_map/ppermute | solution.py:457
  35.0 23.3 %collective-permute-start.8 = (f16[144,1024]{1,0:T(8,128)(2,1)S(1)}, f16[144,1024]{1,0:T(8,128)(2,1)S(1)}, u32[]{:S(2)}, u32[]{:S(2)}) collective-permute-start(f16[144,1024]{1,0:T(8,128)(2,1)S(1)} %convert_element_type.41), channel_id=1, source_target_pairs={{0,4},{1,5},{2,6},{3,7},{4,0},{5,1},{6,2},{7,3},{8,12},{9,13},{10,... | collective-permute-start | bytes 884744 | tf_op jit(solution)/shard_map/ppermute | solution.py:457
  60.1 0.8 copy-start.2
  68.9 0.8 copy-start.3
  69.8 6.3 %collective-permute-start.14 = (f32[256,256]{1,0:T(8,128)S(1)}, f32[256,256]{1,0:T(8,128)}, u32[]{:S(2)}, u32[]{:S(2)}) collective-permute-start(f32[256,256]{1,0:T(8,128)S(1)} %constant_dynamic-slice_fusion), channel_id=1, source_target_pairs={{0,1},{1,0},{2,3},{3,2},{4,5},{5,4},{6,7},{7,6},{8,9},{9,8},{10,11... | collective-permute-start | bytes 786440 | tf_op jit(solution)/shard_map/ppermute | solution.py:457
  69.8 6.2 %copy-start.4 = (f32[512,256]{1,0:T(8,128)S(1)}, f32[512,256]{1,0:T(8,128)}, u32[]{:S(2)}) copy-start(f32[512,256]{1,0:T(8,128)} %copy-done.3) | copy-start | bytes 1572868
  71.0 15.1 %collective-permute-start.10 = (f16[144,1024]{1,0:T(8,128)(2,1)S(1)}, f16[144,1024]{1,0:T(8,128)(2,1)S(1)}, u32[]{:S(2)}, u32[]{:S(2)}) collective-permute-start(f16[144,1024]{1,0:T(8,128)(2,1)S(1)} %convert_element_type.43), channel_id=1, source_target_pairs={{0,2},{1,3},{2,0},{3,1},{4,6},{5,7},{6,4},{7,5},{8,10},{9,11},{10,... | collective-permute-start | bytes 884744 | tf_op jit(solution)/shard_map/ppermute | solution.py:457
  73.3 21.3 %collective-permute-start.11 = (f16[144,1024]{1,0:T(8,128)(2,1)S(1)}, f16[144,1024]{1,0:T(8,128)(2,1)S(1)}, u32[]{:S(2)}, u32[]{:S(2)}) collective-permute-start(f16[144,1024]{1,0:T(8,128)(2,1)S(1)} %convert_element_type.43), channel_id=1, source_target_pairs={{0,4},{1,5},{2,6},{3,7},{4,0},{5,1},{6,2},{7,3},{8,12},{9,13},{10,... | collective-permute-start | bytes 884744 | tf_op jit(solution)/shard_map/ppermute | solution.py:457
  74.5 26.9 %collective-permute-start.12 = (f16[144,1024]{1,0:T(8,128)(2,1)S(1)}, f16[144,1024]{1,0:T(8,128)(2,1)S(1)}, u32[]{:S(2)}, u32[]{:S(2)}) collective-permute-start(f16[144,1024]{1,0:T(8,128)(2,1)S(1)} %convert_element_type.43), channel_id=1, source_target_pairs={{0,6},{1,7},{2,4},{3,5},{4,2},{5,3},{6,0},{7,1},{8,14},{9,15},{10,... | collective-permute-start | bytes 884744 | tf_op jit(solution)/shard_map/ppermute | solution.py:457
  101.8 8.1 %collective-permute-start.13 = (f32[128,1024]{1,0:T(8,128)S(1)}, f32[128,1024]{1,0:T(8,128)S(1)}, u32[]{:S(2)}, u32[]{:S(2)}) collective-permute-start(f32[128,1024]{1,0:T(8,128)S(1)} %fusion), channel_id=1, source_target_pairs={{0,1},{1,0},{2,3},{3,2},{4,5},{5,4},{6,7},{7,6},{8,9},{9,8},{10,11... | collective-permute-start | bytes 1572872 | tf_op jit(solution)/shard_map/ppermute | solution.py:457
  101.9 4.6 %collective-permute-start.19 = (f32[128,128]{1,0:T(8,128)S(1)}, f32[128,128]{1,0:T(8,128)S(1)}, u32[]{:S(2)}, u32[]{:S(2)}) collective-permute-start(f32[128,128]{1,0:T(8,128)S(1)} %get-tuple-element.101), channel_id=1, source_target_pairs={{0,8},{8,0},{16,24},{24,16},{1,9},{9,1},{17,25},{25,17},{2,10},{10... | collective-permute-start | bytes 196616 | tf_op jit(solution)/shard_map/ppermute | solution.py:600
  103.5 4.3 %collective-permute-start.21 = (f32[128,128]{1,0:T(8,128)S(1)}, f32[128,128]{1,0:T(8,128)S(1)}, u32[]{:S(2)}, u32[]{:S(2)}) collective-permute-start(f32[128,128]{1,0:T(8,128)S(1)} %get-tuple-element.102), channel_id=1, source_target_pairs={{0,16},{8,24},{16,0},{24,8},{1,17},{9,25},{17,1},{25,9},{2,18},{10... | collective-permute-start | bytes 196616 | tf_op jit(solution)/shard_map/ppermute | solution.py:600
  105.1 17.4 %collective-permute-start.9 = (f32[256,1024]{1,0:T(8,128)S(1)}, f32[256,1024]{1,0:T(8,128)S(1)}, u32[]{:S(2)}, u32[]{:S(2)}) collective-permute-start(f32[256,1024]{1,0:T(8,128)S(1)} %constant_dynamic-slice_fusion.1), channel_id=1, source_target_pairs={{0,1},{1,0},{2,3},{3,2},{4,5},{5,4},{6,7},{7,6},{8,9},{9,8},{10,11... | collective-permute-start | bytes 3145736 | tf_op jit(solution)/shard_map/ppermute | solution.py:457
  107.8 5.3 %collective-permute-start.20 = (f32[128,128]{1,0:T(8,128)S(1)}, f32[128,128]{1,0:T(8,128)S(1)}, u32[]{:S(2)}, u32[]{:S(2)}) collective-permute-start(f32[128,128]{1,0:T(8,128)S(1)} %get-tuple-element.99), channel_id=1, source_target_pairs={{0,16},{8,24},{16,0},{24,8},{1,17},{9,25},{17,1},{25,9},{2,18},{10... | collective-permute-start | bytes 196616 | tf_op jit(solution)/shard_map/ppermute | solution.py:600
  109.3 4.5 %collective-permute-start.22 = (f32[128,128]{1,0:T(8,128)S(1)}, f32[128,128]{1,0:T(8,128)S(1)}, u32[]{:S(2)}, u32[]{:S(2)}) collective-permute-start(f32[128,128]{1,0:T(8,128)S(1)} %get-tuple-element.100), channel_id=1, source_target_pairs={{0,8},{8,0},{16,24},{24,16},{1,9},{9,1},{17,25},{25,17},{2,10},{10... | collective-permute-start | bytes 196616 | tf_op jit(solution)/shard_map/ppermute | solution.py:600
  111.0 4.3 %collective-permute-start.15 = (f32[128,128]{1,0:T(8,128)S(1)}, f32[128,128]{1,0:T(8,128)S(1)}, u32[]{:S(2)}, u32[]{:S(2)}) collective-permute-start(f32[128,128]{1,0:T(8,128)S(1)} %get-tuple-element.77), channel_id=1, source_target_pairs={{0,8},{8,0},{16,24},{24,16},{1,9},{9,1},{17,25},{25,17},{2,10},{10... | collective-permute-start | bytes 196616 | tf_op jit(solution)/shard_map/ppermute | solution.py:600
  112.5 4.9 %collective-permute-start.17 = (f32[128,128]{1,0:T(8,128)S(1)}, f32[128,128]{1,0:T(8,128)S(1)}, u32[]{:S(2)}, u32[]{:S(2)}) collective-permute-start(f32[128,128]{1,0:T(8,128)S(1)} %get-tuple-element.78), channel_id=1, source_target_pairs={{0,16},{8,24},{16,0},{24,8},{1,17},{9,25},{17,1},{25,9},{2,18},{10... | collective-permute-start | bytes 196616 | tf_op jit(solution)/shard_map/ppermute | solution.py:600
  115.3 4.3 %collective-permute-start.16 = (f32[128,128]{1,0:T(8,128)S(1)}, f32[128,128]{1,0:T(8,128)S(1)}, u32[]{:S(2)}, u32[]{:S(2)}) collective-permute-start(f32[128,128]{1,0:T(8,128)S(1)} %add.142), channel_id=1, source_target_pairs={{0,16},{8,24},{16,0},{24,8},{1,17},{9,25},{17,1},{25,9},{2,18},{10... | collective-permute-start | bytes 196616 | tf_op jit(solution)/shard_map/ppermute | solution.py:600
  117.5 4.3 %collective-permute-start.18 = (f32[128,128]{1,0:T(8,128)S(1)}, f32[128,128]{1,0:T(8,128)S(1)}, u32[]{:S(2)}, u32[]{:S(2)}) collective-permute-start(f32[128,128]{1,0:T(8,128)S(1)} %add.144), channel_id=1, source_target_pairs={{0,8},{8,0},{16,24},{24,16},{1,9},{9,1},{17,25},{25,17},{2,10},{10... | collective-permute-start | bytes 196616 | tf_op jit(solution)/shard_map/ppermute | solution.py:600

commit v7 on v6

--- a/solution.py
+++ b/solution.py
@@ -488,10 +488,10 @@
 
     kv = joined(kv_half(core), swap(kv_half(1 - core), 1))
     keys_near = near(kv)
-    x1, q1, wr1, rd1, ls1, ld1, _ = lax.optimization_barrier((x, q, wr, rd, ls, ld, kv))
-    rates = swap(jnp.concatenate([ls1, ld1], axis=0), 1)
-    lsc = joined(half(ls1, core, hh, 0), half(rates, core, hh, 0), 1)
-    ldc = joined(half(ld1, core, hh, 0), half(rates[heads:], core, hh, 0), 1)
+    x1, q1, wr1, rd1, _ = lax.optimization_barrier((x, q, wr, rd, kv))
+    rates = swap(jnp.concatenate([ls, ld], axis=0), 1)
+    lsc = joined(half(ls, core, hh, 0), half(rates, core, hh, 0), 1)
+    ldc = joined(half(ld, core, hh, 0), half(rates[heads:], core, hh, 0), 1)
     mates = swap(jnp.concatenate([half(x1, 1 - core, hc), wr1, rd1], axis=1), 1)
     xc = joined(half(x1, core, hc), mates[:, :hc])
     wc = joined(wr1, mates[:, hc : hc + n])

time: 125 us -> 126 us (level)
  transfers between devices with their start and end apart: 23 -> 23, of which waited for: 17 -> 15; matrix products, arithmetic and copies ran while one was open for 5% -> 5% of each run, Pallas kernels for 15% -> 15%
where the time goes in v7:
time: 126 us
  waiting for transfers between devices  56 us (44%)
  Pallas kernels  30.4 us (24%)
  starting transfers between devices  27.4 us (22%)
  other arithmetic  7.75 us (6%)
  local copies, waits for them, and re-layouts  2.81 us (2%)
    ppermute x14, waiting for transfers between devices, swap(): return lax.ppermute(a, 'seq', [(i, i ^ bits) for i in range(count)])  46.1 us
    pallas_call x12, Pallas kernels, call(): pl.pallas_call(kernel, out_shape=shapes, in_specs=in_specs or [VM] * len(...  30.4 us
    ppermute x14, starting transfers between devices, swap(): return lax.ppermute(a, 'seq', [(i, i ^ bits) for i in range(count)])  18.9 us
    ppermute x8, waiting for transfers between devices, tp_sum(): lax.ppermute(a, 'tp', [(i, i ^ 1 << (step + k) % bits) for i in range(tp)])  9.93 us
    ppermute x8, starting transfers between devices, tp_sum(): lax.ppermute(a, 'tp', [(i, i ^ 1 << (step + k) % bits) for i in range(tp)])  7.9 us
  transfers between devices with their start and end apart: 23, of which 15 were waited for; matrix products, arithmetic and copies ran while one was open for 5% of the time, Pallas kernels for 15%

profile of v7, /device:TPU:8, one launch (start us, length us, event | category | flops | bytes accessed | tf_op | source)
XLA Modules:
  0.0 125.7 jit_solution(12833143979825259262)
XLA Ops:
  0.7 0.9 pad_maximum_fusion.12
  1.6 1.0 constant_dynamic-slice_fusion.6
  2.6 0.5 collective-permute-start
  3.2 0.1 slice_reduce_fusion.3
  3.3 0.8 dynamic-slice_select_fusion.3
  4.0 0.1 collective-permute-done
  4.3 0.4 collective-permute-start.3
  4.7 2.6 %collective-permute-start.4 = (bf16[512,256]{1,0:T(8,128)(2,1)S(1)}, bf16[512,256]{1,0:T(8,128)(2,1)S(1)}, u32[]{:S(2)}, u32[]{:S(2)}) collective-permute-start(bf16[512,256]{1,0:T(8,128)(2,1)S(1)} %pad_maximum_fusion.5.kv_ref), channel_id=1, source_target_pairs={{0,4},{1,5},{2,6},{3,7},{4,0},{5,1},{6,2},{7,3},{8,12},{9,13},{10,... | collective-permute-start | bytes 786440 | tf_op jit(solution)/shard_map/ppermute | solution.py:457
  7.3 0.4 collective-permute-start.6
  7.9 0.1 collective-permute-start.1
  8.0 0.3 broadcast_select_fusion.1
  8.4 3.1 %shard_map.113 = (bf16[512,2048]{1,0:T(8,128)(2,1)S(1)}, f32[1024,512]{1,0:T(8,128)S(1)}, f32[8,512]{1,0:T(8,128)S(1)}, f32[8,512]{1,0:T(8,128)S(1)}) custom-call(bf16[512,1024]{1,0:T(8,128)(2,1)S(1)} %pad_maximum_fusion.2.q_ref, bf16[512,256]{1,0:T(8,128)(2,1)S(1)} %pad_maximum_fusion.5.kv_ref), custom_call_target="tpu_custom_call" | custom-call | flops 1073741824 | bytes 1310720 | tf_op jit(solution)/shard_map/pallas_call | solution.py:424
  11.5 7.3 %collective-permute-done.4.kv_ref = bf16[512,256]{1,0:T(8,128)(2,1)S(1)} collective-permute-done((bf16[512,256]{1,0:T(8,128)(2,1)S(1)}, bf16[512,256]{1,0:T(8,128)(2,1)S(1)}, u32[]{:S(2)}, u32[]{:S(2)}) %collective-permute-start.4) | collective-permute-done | bytes 262176 | tf_op jit(solution)/shard_map/ppermute | solution.py:457
  18.8 0.7 collective-permute-start.5
  19.4 0.4 collective-permute-done.6.kv_ref
  19.8 4.0 %shard_map.114 = (f32[1024,512]{1,0:T(8,128)S(1)}, f32[8,512]{1,0:T(8,128)S(1)}, f32[8,512]{1,0:T(8,128)S(1)}) custom-call(s32[1]{0:T(128)} %bitcast.2.flag, bf16[512,2048]{1,0:T(8,128)(2,1)S(1)} %get-tuple-element.46.qs_ref, bf16[512,256]{1,0:T(8,128)(2,1)S(1)} %collective-permute-done.6.kv_ref, ...), custom_call_target="tpu_custom_call", output_to_operand_aliasing={{0}: (3, {}), {1}: (4, {}), {2}: (5, {})} | custom-call | flops 1073741824 | bytes 4489220 | tf_op jit(solution)/shard_map/pallas_call | solution.py:424
  23.8 0.3 shard_map.115
  24.1 0.3 broadcast_select_fusion.3
  24.5 2.0 %shard_map.111 = (f32[128,1024]{1,0:T(8,128)S(1)}, f32[144,1024]{1,0:T(8,128)S(1)}, f32[512,1024]{1,0:T(8,128)S(1)}) custom-call(bf16[512,1024]{1,0:T(8,128)(2,1)S(1)} %pad_maximum_fusion.1.x_ref, bf16[512,128]{1,0:T(8,128)(2,1)S(1)} %pad_maximum_fusion.8.w_ref, f32[16,512]{1,0:T(8,128)S(1)} %pad_maximum_fusion.13.ls_ref, ...), custom_call_target="tpu_custom_call" | custom-call | flops 536870912 | bytes 1245184 | tf_op jit(solution)/shard_map/pallas_call | solution.py:424
  26.7 6.9 %shard_map.112 = (f32[512,1024]{1,0:T(8,128)S(1)}, f32[512,1024]{1,0:T(8,128)S(1)}, f32[512,1024]{1,0:T(8,128)S(1)}, f32[16,512]{1,0:T(8,128)S(1)}) custom-call(bf16[512,1024]{1,0:T(8,128)(2,1)S(1)} %pad_maximum_fusion.1.x_ref, bf16[512,128]{1,0:T(8,128)(2,1)S(1)} %pad_maximum_fusion.8.w_ref, bf16[512,128]{1,0:T(8,128)(2,1)S(1)} %pad_maximum_fusion.9.r_ref, ...), custom_call_target="tpu_custom_call" | custom-call | flops 1073741824 | bytes 1900544 | tf_op jit(solution)/shard_map/pallas_call | solution.py:424
  33.6 0.5 shard_map.116
  34.0 1.2 collective-permute-done.7
  35.3 0.2 shard_map.117
  35.5 10.5 %collective-permute-start.8 = (f16[144,1024]{1,0:T(8,128)(2,1)S(1)}, f16[144,1024]{1,0:T(8,128)(2,1)S(1)}, u32[]{:S(2)}, u32[]{:S(2)}) collective-permute-start(f16[144,1024]{1,0:T(8,128)(2,1)S(1)} %convert_element_type.41), channel_id=1, source_target_pairs={{0,4},{1,5},{2,6},{3,7},{4,0},{5,1},{6,2},{7,3},{8,12},{9,13},{10,... | collective-permute-start | bytes 884744 | tf_op jit(solution)/shard_map/ppermute | solution.py:457
  46.1 12.7 %collective-permute-done.8 = f16[144,1024]{1,0:T(8,128)(2,1)S(1)} collective-permute-done((f16[144,1024]{1,0:T(8,128)(2,1)S(1)}, f16[144,1024]{1,0:T(8,128)(2,1)S(1)}, u32[]{:S(2)}, u32[]{:S(2)}) %collective-permute-start.8) | collective-permute-done | bytes 294944 | tf_op jit(solution)/shard_map/ppermute | solution.py:457
  59.0 0.1 fusion.2.sin_ref
  59.1 1.5 %shard_map.118 = (f32[512,1024]{1,0:T(8,128)S(1)}, f32[128,1024]{1,0:T(8,128)S(1)}, f32[144,1024]{1,0:T(8,128)S(1)}) custom-call(f32[512,1024]{1,0:T(8,128)S(1)} %get-tuple-element.44.y_ref, f32[1024,512]{1,0:T(8,128)S(1)} %get-tuple-element.57.acc_ref, f32[8,512]{1,0:T(8,128)S(1)} %get-tuple-element.58.l_ref, bf16[512,128]{1,0:T(8,128)(2,1)S(1)} %pad_maximum_fusion.9.r_ref, ...), custom_call_target="tpu_custom_call" | custom-call | flops 1073741824 | bytes 6963200 | tf_op jit(solution)/shard_map/pallas_call | solution.py:424
  60.6 0.8 copy-done.2
  61.4 8.0 %shard_map.119 = (f32[512,1024]{1,0:T(8,128)S(1)}, f32[512,256]{1,0:T(8,128)S(1)}) custom-call(f32[512,1024]{1,0:T(8,128)S(1)} %get-tuple-element.61.res_ref, bf16[512,1024]{1,0:T(8,128)(2,1)S(1)} %pad_maximum_fusion.1.x_ref, bf16[512,128]{1,0:T(8,128)(2,1)S(1)} %pad_maximum_fusion.8.w_ref, bf16[512,128]{1,0:T(8,128)(2,1)S(1)} %pad_maximum_fusion.9.r_ref, ...), custom_call_target="tpu_custom_call" | custom-call | flops 2147483648 | bytes 11304960 | tf_op jit(solution)/shard_map/pallas_call | solution.py:424
  69.5 0.8 copy-done.3
  70.3 0.1 collective-permute-start.14
  70.4 1.2 convert_element_type.43
  71.5 2.3 %collective-permute-start.10 = (f16[144,1024]{1,0:T(8,128)(2,1)S(1)}, f16[144,1024]{1,0:T(8,128)(2,1)S(1)}, u32[]{:S(2)}, u32[]{:S(2)}) collective-permute-start(f16[144,1024]{1,0:T(8,128)(2,1)S(1)} %convert_element_type.43), channel_id=1, source_target_pairs={{0,2},{1,3},{2,0},{3,1},{4,6},{5,7},{6,4},{7,5},{8,10},{9,11},{10,... | collective-permute-start | bytes 884744 | tf_op jit(solution)/shard_map/ppermute | solution.py:457
  73.8 1.3 collective-permute-start.11
  75.0 0.5 collective-permute-start.12
  75.5 1.0 shard_map.120
  76.5 1.0 dynamic-slice_add_fusion
  77.5 9.1 %collective-permute-done.10 = f16[144,1024]{1,0:T(8,128)(2,1)S(1)} collective-permute-done((f16[144,1024]{1,0:T(8,128)(2,1)S(1)}, f16[144,1024]{1,0:T(8,128)(2,1)S(1)}, u32[]{:S(2)}, u32[]{:S(2)}) %collective-permute-start.10) | collective-permute-done | bytes 294944 | tf_op jit(solution)/shard_map/ppermute | solution.py:457
  86.7 8.5 %collective-permute-done.11 = f16[144,1024]{1,0:T(8,128)(2,1)S(1)} collective-permute-done((f16[144,1024]{1,0:T(8,128)(2,1)S(1)}, f16[144,1024]{1,0:T(8,128)(2,1)S(1)}, u32[]{:S(2)}, u32[]{:S(2)}) %collective-permute-start.11) | collective-permute-done | bytes 294944 | tf_op jit(solution)/shard_map/ppermute | solution.py:457
  95.1 6.8 %collective-permute-done.12 = f16[144,1024]{1,0:T(8,128)(2,1)S(1)} collective-permute-done((f16[144,1024]{1,0:T(8,128)(2,1)S(1)}, f16[144,1024]{1,0:T(8,128)(2,1)S(1)}, u32[]{:S(2)}, u32[]{:S(2)}) %collective-permute-start.12) | collective-permute-done | bytes 294944 | tf_op jit(solution)/shard_map/ppermute | solution.py:457
  101.9 0.2 maximum_convert_fusion
  102.2 0.1 fusion
  102.4 1.6 %collective-permute-start.19 = (f32[128,128]{1,0:T(8,128)S(1)}, f32[128,128]{1,0:T(8,128)S(1)}, u32[]{:S(2)}, u32[]{:S(2)}) collective-permute-start(f32[128,128]{1,0:T(8,128)S(1)} %get-tuple-element.97), channel_id=1, source_target_pairs={{0,8},{8,0},{16,24},{24,16},{1,9},{9,1},{17,25},{25,17},{2,10},{10... | collective-permute-start | bytes 196616 | tf_op jit(solution)/shard_map/ppermute | solution.py:600
  104.0 1.5 %collective-permute-start.21 = (f32[128,128]{1,0:T(8,128)S(1)}, f32[128,128]{1,0:T(8,128)S(1)}, u32[]{:S(2)}, u32[]{:S(2)}) collective-permute-start(f32[128,128]{1,0:T(8,128)S(1)} %get-tuple-element.98), channel_id=1, source_target_pairs={{0,16},{8,24},{16,0},{24,8},{1,17},{9,25},{17,1},{25,9},{2,18},{10... | collective-permute-start | bytes 196616 | tf_op jit(solution)/shard_map/ppermute | solution.py:600
  105.7 1.3 %collective-permute-done.19 = f32[128,128]{1,0:T(8,128)S(1)} collective-permute-done((f32[128,128]{1,0:T(8,128)S(1)}, f32[128,128]{1,0:T(8,128)S(1)}, u32[]{:S(2)}, u32[]{:S(2)}) %collective-permute-start.19) | collective-permute-done | bytes 65568 | tf_op jit(solution)/shard_map/ppermute | solution.py:600
  107.0 1.3 %collective-permute-done.21 = f32[128,128]{1,0:T(8,128)S(1)} collective-permute-done((f32[128,128]{1,0:T(8,128)S(1)}, f32[128,128]{1,0:T(8,128)S(1)}, u32[]{:S(2)}, u32[]{:S(2)}) %collective-permute-start.21) | collective-permute-done | bytes 65568 | tf_op jit(solution)/shard_map/ppermute | solution.py:600
  108.3 1.6 %collective-permute-start.20 = (f32[128,128]{1,0:T(8,128)S(1)}, f32[128,128]{1,0:T(8,128)S(1)}, u32[]{:S(2)}, u32[]{:S(2)}) collective-permute-start(f32[128,128]{1,0:T(8,128)S(1)} %get-tuple-element.95), channel_id=1, source_target_pairs={{0,16},{8,24},{16,0},{24,8},{1,17},{9,25},{17,1},{25,9},{2,18},{10... | collective-permute-start | bytes 196616 | tf_op jit(solution)/shard_map/ppermute | solution.py:600
  109.8 0.5 collective-permute-start.22
  110.4 0.2 broadcast_select_fusion.5
  110.6 0.1 pad_maximum_fusion.3.g_ref
  110.7 0.8 shard_map.122
  111.5 1.6 %collective-permute-start.15 = (f32[128,128]{1,0:T(8,128)S(1)}, f32[128,128]{1,0:T(8,128)S(1)}, u32[]{:S(2)}, u32[]{:S(2)}) collective-permute-start(f32[128,128]{1,0:T(8,128)S(1)} %get-tuple-element.73), channel_id=1, source_target_pairs={{0,8},{8,0},{16,24},{24,16},{1,9},{9,1},{17,25},{25,17},{2,10},{10... | collective-permute-start | bytes 196616 | tf_op jit(solution)/shard_map/ppermute | solution.py:600
  113.0 0.5 collective-permute-start.17
  113.6 0.8 collective-permute-done.22
  114.4 1.5 %collective-permute-done.15 = f32[128,128]{1,0:T(8,128)S(1)} collective-permute-done((f32[128,128]{1,0:T(8,128)S(1)}, f32[128,128]{1,0:T(8,128)S(1)}, u32[]{:S(2)}, u32[]{:S(2)}) %collective-permute-start.15) | collective-permute-done | bytes 65568 | tf_op jit(solution)/shard_map/ppermute | solution.py:600
  115.8 0.6 collective-permute-start.16
  116.4 1.5 %collective-permute-done.17 = f32[128,128]{1,0:T(8,128)S(1)} collective-permute-done((f32[128,128]{1,0:T(8,128)S(1)}, f32[128,128]{1,0:T(8,128)S(1)}, u32[]{:S(2)}, u32[]{:S(2)}) %collective-permute-start.17) | collective-permute-done | bytes 65568 | tf_op jit(solution)/shard_map/ppermute | solution.py:600
  118.0 0.7 pad_maximum_fusion.11
  118.7 1.5 %collective-permute-done.16 = f32[128,128]{1,0:T(8,128)S(1)} collective-permute-done((f32[128,128]{1,0:T(8,128)S(1)}, f32[128,128]{1,0:T(8,128)S(1)}, u32[]{:S(2)}, u32[]{:S(2)}) %collective-permute-start.16) | collective-permute-done | bytes 65568 | tf_op jit(solution)/shard_map/ppermute | solution.py:600
  120.2 2.1 %collective-permute-done.18 = f32[128,128]{1,0:T(8,128)S(1)} collective-permute-done((f32[128,128]{1,0:T(8,128)S(1)}, f32[128,128]{1,0:T(8,128)S(1)}, u32[]{:S(2)}, u32[]{:S(2)}) %collective-permute-start.18) | collective-permute-done | bytes 65568 | tf_op jit(solution)/shard_map/ppermute | solution.py:600
  122.3 0.7 pad_maximum_fusion.10
  123.0 0.2 dynamic-slice_select_fusion.1
  123.2 0.2 pad_maximum_fusion.back_ref
  123.4 2.2 %shard_map.121 = (f32[256,2048]{1,0:T(8,128)}, f32[32,256]{1,0:T(8,128)}) custom-call(f32[256,2048]{1,0:T(8,128)S(1)} %pad_maximum_fusion.back_ref, f32[256,2048]{1,0:T(8,128)S(1)} %get-tuple-element.67.wexp_ref, bf16[256,2048]{1,0:T(8,128)(2,1)S(1)} %copy-done, bf16[256,128]{1,0:T(8,128)(2,1)S(1)} %copy-done.1, f32[128,2048]{1,0:T(8,128)S(1)} %pad_maximum_fusion.3.g_ref), custom_call_target="tpu_custom_call" | custom-call | flops 1073741824 | bytes 6356992 | tf_op jit(solution)/shard_map/pallas_call | solution.py:424
  (64 shorter events, 1.2 us)
Async XLA Ops:
  0.6 7.2 %copy-start = (bf16[256,2048]{1,0:T(8,128)(2,1)S(1)}, bf16[256,2048]{1,0:T(8,128)(2,1)}, u32[]{:S(2)}) copy-start(bf16[256,2048]{1,0:T(8,128)(2,1)} %x_ref.3) | copy-start | bytes 3145732
  0.6 3.6 %copy-start.7 = (bf16[256,2048]{1,0:T(8,128)(2,1)S(1)}, bf16[256,2048]{1,0:T(8,128)(2,1)}, u32[]{:S(2)}) copy-start(bf16[256,2048]{1,0:T(8,128)(2,1)} %param.8) | copy-start | bytes 3145732
  1.6 1.6 %collective-permute-start.2 = (f32[64,256]{1,0:T(8,128)S(1)}, f32[64,256]{1,0:T(8,128)S(1)}, u32[]{:S(2)}, u32[]{:S(2)}) collective-permute-start(f32[64,256]{1,0:T(8,128)S(1)} %pad_maximum_fusion.12), channel_id=1, source_target_pairs={{0,1},{1,0},{2,3},{3,2},{4,5},{5,4},{6,7},{7,6},{8,9},{9,8},{10,11... | collective-permute-start | bytes 196616 | tf_op jit(solution)/shard_map/ppermute | solution.py:457
  1.6 6.2 %copy-start.1 = (bf16[256,128]{1,0:T(8,128)(2,1)S(1)}, bf16[256,128]{1,0:T(8,128)(2,1)}, u32[]{:S(2)}) copy-start(bf16[256,128]{1,0:T(8,128)(2,1)} %w_ref.1) | copy-start | bytes 196612
  1.6 6.2 %copy-start.8 = (bf16[256,128]{1,0:T(8,128)(2,1)S(1)}, bf16[256,128]{1,0:T(8,128)(2,1)}, u32[]{:S(2)}) copy-start(bf16[256,128]{1,0:T(8,128)(2,1)} %param.13) | copy-start | bytes 196612
  2.6 1.5 %collective-permute-start = (bf16[256,256]{1,0:T(8,128)(2,1)S(1)}, bf16[256,256]{1,0:T(8,128)(2,1)S(1)}, u32[]{:S(2)}, u32[]{:S(2)}) collective-permute-start(bf16[256,256]{1,0:T(8,128)(2,1)S(1)} %pad_maximum_fusion.7), channel_id=1, source_target_pairs={{0,1},{1,0},{2,3},{3,2},{4,5},{5,4},{6,7},{7,6},{8,9},{9,8},{10,11... | collective-permute-start | bytes 393224 | tf_op jit(solution)/shard_map/ppermute | solution.py:457
  4.3 3.7 %collective-permute-start.3 = (bf16[256,1024]{1,0:T(8,128)(2,1)S(1)}, bf16[256,1024]{1,0:T(8,128)(2,1)S(1)}, u32[]{:S(2)}, u32[]{:S(2)}) collective-permute-start(bf16[256,1024]{1,0:T(8,128)(2,1)S(1)} %constant_dynamic-slice_fusion.2), channel_id=1, source_target_pairs={{0,1},{1,0},{2,3},{3,2},{4,5},{5,4},{6,7},{7,6},{8,9},{9,8},{10,11... | collective-permute-start | bytes 1572872 | tf_op jit(solution)/shard_map/ppermute | solution.py:457
  4.7 14.0 %collective-permute-start.4 = (bf16[512,256]{1,0:T(8,128)(2,1)S(1)}, bf16[512,256]{1,0:T(8,128)(2,1)S(1)}, u32[]{:S(2)}, u32[]{:S(2)}) collective-permute-start(bf16[512,256]{1,0:T(8,128)(2,1)S(1)} %pad_maximum_fusion.5.kv_ref), channel_id=1, source_target_pairs={{0,4},{1,5},{2,6},{3,7},{4,0},{5,1},{6,2},{7,3},{8,12},{9,13},{10,... | collective-permute-start | bytes 786440 | tf_op jit(solution)/shard_map/ppermute | solution.py:457
  7.3 12.5 %collective-permute-start.6 = (bf16[512,256]{1,0:T(8,128)(2,1)S(1)}, bf16[512,256]{1,0:T(8,128)(2,1)S(1)}, u32[]{:S(2)}, u32[]{:S(2)}) collective-permute-start(bf16[512,256]{1,0:T(8,128)(2,1)S(1)} %pad_maximum_fusion.5.kv_ref), channel_id=1, source_target_pairs={{0,2},{1,3},{2,0},{3,1},{4,6},{5,7},{6,4},{7,5},{8,10},{9,11},{10,... | collective-permute-start | bytes 786440 | tf_op jit(solution)/shard_map/ppermute | solution.py:457
  7.9 16.2 %collective-permute-start.1 = (bf16[256,1280]{1,0:T(8,128)(2,1)S(1)}, bf16[256,1280]{1,0:T(8,128)(2,1)S(1)}, u32[]{:S(2)}, u32[]{:S(2)}) collective-permute-start(bf16[256,1280]{1,0:T(8,128)(2,1)S(1)} %pad_maximum_fusion.4), channel_id=1, source_target_pairs={{0,1},{1,0},{2,3},{3,2},{4,5},{5,4},{6,7},{7,6},{8,9},{9,8},{10,11... | collective-permute-start | bytes 1966088 | tf_op jit(solution)/shard_map/ppermute | solution.py:457
  18.8 14.8 %collective-permute-start.5 = (bf16[512,256]{1,0:T(8,128)(2,1)S(1)}, bf16[512,256]{1,0:T(8,128)(2,1)S(1)}, u32[]{:S(2)}, u32[]{:S(2)}) collective-permute-start(bf16[512,256]{1,0:T(8,128)(2,1)S(1)} %collective-permute-done.4.kv_ref), channel_id=1, source_target_pairs={{4,6},{5,7},{6,4},{7,5},{12,14},{13,15},{14,12},{15,13},{20,22},{2... | collective-permute-start | bytes 786440 | tf_op jit(solution)/shard_map/ppermute | solution.py:481
  26.6 8.7 %collective-permute-start.7 = (f16[144,1024]{1,0:T(8,128)(2,1)S(1)}, f16[144,1024]{1,0:T(8,128)(2,1)S(1)}, u32[]{:S(2)}, u32[]{:S(2)}) collective-permute-start(f16[144,1024]{1,0:T(8,128)(2,1)S(1)} %convert_element_type.39), channel_id=1, source_target_pairs={{0,2},{1,3},{2,0},{3,1},{4,6},{5,7},{6,4},{7,5},{8,10},{9,11},{10,... | collective-permute-start | bytes 884744 | tf_op jit(solution)/shard_map/ppermute | solution.py:457
  35.5 23.3 %collective-permute-start.8 = (f16[144,1024]{1,0:T(8,128)(2,1)S(1)}, f16[144,1024]{1,0:T(8,128)(2,1)S(1)}, u32[]{:S(2)}, u32[]{:S(2)}) collective-permute-start(f16[144,1024]{1,0:T(8,128)(2,1)S(1)} %convert_element_type.41), channel_id=1, source_target_pairs={{0,4},{1,5},{2,6},{3,7},{4,0},{5,1},{6,2},{7,3},{8,12},{9,13},{10,... | collective-permute-start | bytes 884744 | tf_op jit(solution)/shard_map/ppermute | solution.py:457
  60.6 0.8 copy-start.2
  61.4 14.1 %copy-start.5 = (f32[32,256]{1,0:T(8,128)S(1)}, f32[32,256]{1,0:T(8,128)}, u32[]{:S(2)}) copy-start(f32[32,256]{1,0:T(8,128)} %ld_ref.1) | copy-start | bytes 98308
  61.4 14.1 %copy-start.6 = (f32[32,256]{1,0:T(8,128)S(1)}, f32[32,256]{1,0:T(8,128)}, u32[]{:S(2)}) copy-start(f32[32,256]{1,0:T(8,128)} %ls_ref.1) | copy-start | bytes 98308
  69.4 0.8 copy-start.3
  70.3 6.3 %collective-permute-start.14 = (f32[256,256]{1,0:T(8,128)S(1)}, f32[256,256]{1,0:T(8,128)}, u32[]{:S(2)}, u32[]{:S(2)}) collective-permute-start(f32[256,256]{1,0:T(8,128)S(1)} %constant_dynamic-slice_fusion), channel_id=1, source_target_pairs={{0,1},{1,0},{2,3},{3,2},{4,5},{5,4},{6,7},{7,6},{8,9},{9,8},{10,11... | collective-permute-start | bytes 786440 | tf_op jit(solution)/shard_map/ppermute | solution.py:457
  70.3 6.2 %copy-start.4 = (f32[512,256]{1,0:T(8,128)S(1)}, f32[512,256]{1,0:T(8,128)}, u32[]{:S(2)}) copy-start(f32[512,256]{1,0:T(8,128)} %copy-done.3) | copy-start | bytes 1572868
  71.5 15.1 %collective-permute-start.10 = (f16[144,1024]{1,0:T(8,128)(2,1)S(1)}, f16[144,1024]{1,0:T(8,128)(2,1)S(1)}, u32[]{:S(2)}, u32[]{:S(2)}) collective-permute-start(f16[144,1024]{1,0:T(8,128)(2,1)S(1)} %convert_element_type.43), channel_id=1, source_target_pairs={{0,2},{1,3},{2,0},{3,1},{4,6},{5,7},{6,4},{7,5},{8,10},{9,11},{10,... | collective-permute-start | bytes 884744 | tf_op jit(solution)/shard_map/ppermute | solution.py:457
  73.8 21.3 %collective-permute-start.11 = (f16[144,1024]{1,0:T(8,128)(2,1)S(1)}, f16[144,1024]{1,0:T(8,128)(2,1)S(1)}, u32[]{:S(2)}, u32[]{:S(2)}) collective-permute-start(f16[144,1024]{1,0:T(8,128)(2,1)S(1)} %convert_element_type.43), channel_id=1, source_target_pairs={{0,4},{1,5},{2,6},{3,7},{4,0},{5,1},{6,2},{7,3},{8,12},{9,13},{10,... | collective-permute-start | bytes 884744 | tf_op jit(solution)/shard_map/ppermute | solution.py:457
  75.0 26.9 %collective-permute-start.12 = (f16[144,1024]{1,0:T(8,128)(2,1)S(1)}, f16[144,1024]{1,0:T(8,128)(2,1)S(1)}, u32[]{:S(2)}, u32[]{:S(2)}) collective-permute-start(f16[144,1024]{1,0:T(8,128)(2,1)S(1)} %convert_element_type.43), channel_id=1, source_target_pairs={{0,6},{1,7},{2,4},{3,5},{4,2},{5,3},{6,0},{7,1},{8,14},{9,15},{10,... | collective-permute-start | bytes 884744 | tf_op jit(solution)/shard_map/ppermute | solution.py:457
  102.3 8.1 %collective-permute-start.13 = (f32[128,1024]{1,0:T(8,128)S(1)}, f32[128,1024]{1,0:T(8,128)S(1)}, u32[]{:S(2)}, u32[]{:S(2)}) collective-permute-start(f32[128,1024]{1,0:T(8,128)S(1)} %fusion), channel_id=1, source_target_pairs={{0,1},{1,0},{2,3},{3,2},{4,5},{5,4},{6,7},{7,6},{8,9},{9,8},{10,11... | collective-permute-start | bytes 1572872 | tf_op jit(solution)/shard_map/ppermute | solution.py:457
  102.4 4.6 %collective-permute-start.19 = (f32[128,128]{1,0:T(8,128)S(1)}, f32[128,128]{1,0:T(8,128)S(1)}, u32[]{:S(2)}, u32[]{:S(2)}) collective-permute-start(f32[128,128]{1,0:T(8,128)S(1)} %get-tuple-element.97), channel_id=1, source_target_pairs={{0,8},{8,0},{16,24},{24,16},{1,9},{9,1},{17,25},{25,17},{2,10},{10... | collective-permute-start | bytes 196616 | tf_op jit(solution)/shard_map/ppermute | solution.py:600
  104.0 4.3 %collective-permute-start.21 = (f32[128,128]{1,0:T(8,128)S(1)}, f32[128,128]{1,0:T(8,128)S(1)}, u32[]{:S(2)}, u32[]{:S(2)}) collective-permute-start(f32[128,128]{1,0:T(8,128)S(1)} %get-tuple-element.98), channel_id=1, source_target_pairs={{0,16},{8,24},{16,0},{24,8},{1,17},{9,25},{17,1},{25,9},{2,18},{10... | collective-permute-start | bytes 196616 | tf_op jit(solution)/shard_map/ppermute | solution.py:600
  105.6 17.4 %collective-permute-start.9 = (f32[256,1024]{1,0:T(8,128)S(1)}, f32[256,1024]{1,0:T(8,128)S(1)}, u32[]{:S(2)}, u32[]{:S(2)}) collective-permute-start(f32[256,1024]{1,0:T(8,128)S(1)} %constant_dynamic-slice_fusion.1), channel_id=1, source_target_pairs={{0,1},{1,0},{2,3},{3,2},{4,5},{5,4},{6,7},{7,6},{8,9},{9,8},{10,11... | collective-permute-start | bytes 3145736 | tf_op jit(solution)/shard_map/ppermute | solution.py:457
  108.3 5.3 %collective-permute-start.20 = (f32[128,128]{1,0:T(8,128)S(1)}, f32[128,128]{1,0:T(8,128)S(1)}, u32[]{:S(2)}, u32[]{:S(2)}) collective-permute-start(f32[128,128]{1,0:T(8,128)S(1)} %get-tuple-element.95), channel_id=1, source_target_pairs={{0,16},{8,24},{16,0},{24,8},{1,17},{9,25},{17,1},{25,9},{2,18},{10... | collective-permute-start | bytes 196616 | tf_op jit(solution)/shard_map/ppermute | solution.py:600
  109.8 4.5 %collective-permute-start.22 = (f32[128,128]{1,0:T(8,128)S(1)}, f32[128,128]{1,0:T(8,128)S(1)}, u32[]{:S(2)}, u32[]{:S(2)}) collective-permute-start(f32[128,128]{1,0:T(8,128)S(1)} %get-tuple-element.96), channel_id=1, source_target_pairs={{0,8},{8,0},{16,24},{24,16},{1,9},{9,1},{17,25},{25,17},{2,10},{10... | collective-permute-start | bytes 196616 | tf_op jit(solution)/shard_map/ppermute | solution.py:600
  111.5 4.3 %collective-permute-start.15 = (f32[128,128]{1,0:T(8,128)S(1)}, f32[128,128]{1,0:T(8,128)S(1)}, u32[]{:S(2)}, u32[]{:S(2)}) collective-permute-start(f32[128,128]{1,0:T(8,128)S(1)} %get-tuple-element.73), channel_id=1, source_target_pairs={{0,8},{8,0},{16,24},{24,16},{1,9},{9,1},{17,25},{25,17},{2,10},{10... | collective-permute-start | bytes 196616 | tf_op jit(solution)/shard_map/ppermute | solution.py:600
  113.0 4.9 %collective-permute-start.17 = (f32[128,128]{1,0:T(8,128)S(1)}, f32[128,128]{1,0:T(8,128)S(1)}, u32[]{:S(2)}, u32[]{:S(2)}) collective-permute-start(f32[128,128]{1,0:T(8,128)S(1)} %get-tuple-element.74), channel_id=1, source_target_pairs={{0,16},{8,24},{16,0},{24,8},{1,17},{9,25},{17,1},{25,9},{2,18},{10... | collective-permute-start | bytes 196616 | tf_op jit(solution)/shard_map/ppermute | solution.py:600
  115.8 4.3 %collective-permute-start.16 = (f32[128,128]{1,0:T(8,128)S(1)}, f32[128,128]{1,0:T(8,128)S(1)}, u32[]{:S(2)}, u32[]{:S(2)}) collective-permute-start(f32[128,128]{1,0:T(8,128)S(1)} %add.142), channel_id=1, source_target_pairs={{0,16},{8,24},{16,0},{24,8},{1,17},{9,25},{17,1},{25,9},{2,18},{10... | collective-permute-start | bytes 196616 | tf_op jit(solution)/shard_map/ppermute | solution.py:600
  117.9 4.3 %collective-permute-start.18 = (f32[128,128]{1,0:T(8,128)S(1)}, f32[128,128]{1,0:T(8,128)S(1)}, u32[]{:S(2)}, u32[]{:S(2)}) collective-permute-start(f32[128,128]{1,0:T(8,128)S(1)} %add.144), channel_id=1, source_target_pairs={{0,8},{8,0},{16,24},{24,16},{1,9},{9,1},{17,25},{25,17},{2,10},{10... | collective-permute-start | bytes 196616 | tf_op jit(solution)/shard_map/ppermute | solution.py:600

commit v8 on v7

--- a/solution.py
+++ b/solution.py
@@ -314,7 +314,7 @@
 
 def back_kernel(
     res_ref, x_ref, w_ref, r_ref, clsx_ref, crow_ref, fs_ref, wexp_ref, sin_ref, st0_ref, d1_ref,
-    back_ref, shared_ref, a_ref, pair,
+    back_ref, first_ref, second_ref, a_ref, pair,
 ):
     t = x_ref.shape[0] // 2
     th = t // 2
@@ -381,8 +381,9 @@
         ph, plo = split2(jnp.where(keep, pair[...], 0.0))
         n = w.shape[1]
         mixed = nn(ph, r) + nn(plo, r)
-        shared_ref[rows, :n] = mixed if gw is None else mixed + gw
-        shared_ref[rows, n:] = gr + tn(ph, w) + tn(plo, w)
+        shared_ref = second_ref if b else first_ref
+        shared_ref[:, :n] = mixed if gw is None else mixed + gw
+        shared_ref[:, n:] = gr + tn(ph, w) + tn(plo, w)
 
 
 def ready_kernel(x_ref, ls_ref, ld_ref, extra_ref, wexp_ref, xh_ref, xl_ref):
@@ -576,8 +577,8 @@
     coming = []
     for d in range(1, chips):
         coming.append(swap(sent, 2 * d))
-    back, shared = call(
-        back_kernel, [((2 * t, hc), F32), ((2 * t, 2 * n), F32)],
+    back, *shared = call(
+        back_kernel, [((2 * t, hc), F32), ((t, 2 * n), F32), ((t, 2 * n), F32)],
         (res, xc, wc, rc, clsx, crow, fs, wexpc, incoming, st0, d1),
         scratch=[pltpu.VMEM((t, t), F32), pltpu.VMEM((t, t), F32)],
         flops=16 * mm,
@@ -604,12 +605,12 @@
         return parts
 
     back_all = joined(*home(back), 1)
-    own, other = home(shared)
-    grads = own + other
+    grads = jnp.where(core == 0, *shared) + swap(jnp.where(core == 0, *shared[::-1]), 1)
     gw0, gr0 = grads[:, :n], grads[:, n:]
-    grad_read = jnp.concatenate(tp_sum([gr0[: t // 2], gr0[t // 2 :]]), axis=0)
+    (grad_read,) = tp_sum([gr0])
     arriving = combine(coming)
-    arrived = joined(arriving, swap(arriving, 1), 1)
+    met = swap(arriving, 1)
+    arrived = joined(arriving, met, 1)
     gwp = call(write_kernel, [((t // 2, n), F32)] * 2, (xh, xl, arrived, gw0), flops=4 * mm)
     grad_write = jnp.concatenate(tp_sum(gwp), axis=0)
     gi, gls = call(

time: 126 us -> 120 us (0.952)
  the two profiles are of different devices: /device:TPU:8 before, /device:TPU:12 now
where the time goes in v8:
time: 120 us
  waiting for transfers between devices  48.8 us (41%)
  Pallas kernels  30.4 us (25%)
  starting transfers between devices  26 us (22%)
  other arithmetic  8.59 us (7%)
  local copies, waits for them, and re-layouts  4.93 us (4%)
    ppermute x14, waiting for transfers between devices, swap(): return lax.ppermute(a, 'seq', [(i, i ^ bits) for i in range(count)])  39.3 us
    pallas_call x12, Pallas kernels, call(): pl.pallas_call(kernel, out_shape=shapes, in_specs=in_specs or [VM] * len(...  30.4 us
    ppermute x14, starting transfers between devices, swap(): return lax.ppermute(a, 'seq', [(i, i ^ bits) for i in range(count)])  19 us
    ppermute x6, waiting for transfers between devices, tp_sum(): lax.ppermute(a, 'tp', [(i, i ^ 1 << (step + k) % bits) for i in range(tp)])  9.57 us
    ppermute x6, starting transfers between devices, tp_sum(): lax.ppermute(a, 'tp', [(i, i ^ 1 << (step + k) % bits) for i in range(tp)])  6.31 us
    select_n x7, other arithmetic, joined(): a = jnp.where(core == 0, own, other)  2.97 us
    unnamed x18, local copies, waits for them, and re-layouts  2.75 us
    add x6, other arithmetic, tp_sum(): parts = [a + b for a, b in zip(parts, sent)]  2.47 us
  transfers between devices with their start and end apart: 21, of which 12 were waited for; matrix products, arithmetic and copies ran while one was open for 6% of the time, Pallas kernels for 22%

profile of v8, /device:TPU:12, one launch (start us, length us, event | category | flops | bytes accessed | tf_op | source)
XLA Modules:
  0.0 119.9 jit_solution(5931808502490428003)
XLA Ops:
  0.7 0.9 pad_maximum_fusion.11
  1.6 1.0 constant_dynamic-slice_fusion.5
  2.6 0.5 collective-permute-start
  3.2 0.1 slice_reduce_fusion.3
  3.3 0.8 dynamic-slice_select_fusion.3
  4.0 0.1 collective-permute-done
  4.3 0.4 collective-permute-start.3
  4.8 1.0 shard_map.120
  5.7 1.4 %copy-done.1 = f32[256,2048]{1,0:T(8,128)} copy-done((f32[256,2048]{1,0:T(8,128)}, f32[256,2048]{1,0:T(8,128)S(1)}, u32[]{:S(2)}) %copy-start.1) | copy-done | bytes 2097176
  7.1 2.6 %collective-permute-start.4 = (bf16[512,256]{1,0:T(8,128)(2,1)S(1)}, bf16[512,256]{1,0:T(8,128)(2,1)S(1)}, u32[]{:S(2)}, u32[]{:S(2)}) collective-permute-start(bf16[512,256]{1,0:T(8,128)(2,1)S(1)} %pad_maximum_fusion.5.kv_ref), channel_id=1, source_target_pairs={{0,4},{1,5},{2,6},{3,7},{4,0},{5,1},{6,2},{7,3},{8,12},{9,13},{10,... | collective-permute-start | bytes 786440 | tf_op jit(solution)/shard_map/ppermute | solution.py:458
  9.7 0.5 collective-permute-start.6
  10.3 0.1 collective-permute-start.1
  10.4 0.2 broadcast_select_fusion.1
  10.6 0.1 pad_maximum_fusion.2.q_ref
  10.7 3.1 %shard_map.113 = (bf16[512,2048]{1,0:T(8,128)(2,1)S(1)}, f32[1024,512]{1,0:T(8,128)S(1)}, f32[8,512]{1,0:T(8,128)S(1)}, f32[8,512]{1,0:T(8,128)S(1)}) custom-call(bf16[512,1024]{1,0:T(8,128)(2,1)S(1)} %pad_maximum_fusion.2.q_ref, bf16[512,256]{1,0:T(8,128)(2,1)S(1)} %pad_maximum_fusion.5.kv_ref), custom_call_target="tpu_custom_call" | custom-call | flops 1073741824 | bytes 1310720 | tf_op jit(solution)/shard_map/pallas_call | solution.py:425
  13.8 7.3 %collective-permute-done.4.kv_ref = bf16[512,256]{1,0:T(8,128)(2,1)S(1)} collective-permute-done((bf16[512,256]{1,0:T(8,128)(2,1)S(1)}, bf16[512,256]{1,0:T(8,128)(2,1)S(1)}, u32[]{:S(2)}, u32[]{:S(2)}) %collective-permute-start.4) | collective-permute-done | bytes 262176 | tf_op jit(solution)/shard_map/ppermute | solution.py:458
  21.1 0.7 collective-permute-start.5
  21.8 0.4 collective-permute-done.6.kv_ref
  22.1 4.0 %shard_map.114 = (f32[1024,512]{1,0:T(8,128)S(1)}, f32[8,512]{1,0:T(8,128)S(1)}, f32[8,512]{1,0:T(8,128)S(1)}) custom-call(s32[1]{0:T(128)} %bitcast.2.flag, bf16[512,2048]{1,0:T(8,128)(2,1)S(1)} %get-tuple-element.47.qs_ref, bf16[512,256]{1,0:T(8,128)(2,1)S(1)} %collective-permute-done.6.kv_ref, ...), custom_call_target="tpu_custom_call", output_to_operand_aliasing={{0}: (3, {}), {1}: (4, {}), {2}: (5, {})} | custom-call | flops 1073741824 | bytes 4489220 | tf_op jit(solution)/shard_map/pallas_call | solution.py:425
  26.1 0.3 shard_map.115
  26.5 0.2 broadcast_select_fusion.3
  26.7 0.1 pad_maximum_fusion.1.x_ref
  26.8 2.0 %shard_map.111 = (f32[128,1024]{1,0:T(8,128)S(1)}, f32[144,1024]{1,0:T(8,128)S(1)}, f32[512,1024]{1,0:T(8,128)S(1)}) custom-call(bf16[512,1024]{1,0:T(8,128)(2,1)S(1)} %pad_maximum_fusion.1.x_ref, bf16[512,128]{1,0:T(8,128)(2,1)S(1)} %pad_maximum_fusion.8.w_ref, f32[16,512]{1,0:T(8,128)S(1)} %pad_maximum_fusion.12.ls_ref, ...), custom_call_target="tpu_custom_call" | custom-call | flops 536870912 | bytes 1245184 | tf_op jit(solution)/shard_map/pallas_call | solution.py:425
  28.8 0.1 collective-permute-start.7
  28.9 6.9 %shard_map.112 = (f32[512,1024]{1,0:T(8,128)S(1)}, f32[512,1024]{1,0:T(8,128)S(1)}, f32[512,1024]{1,0:T(8,128)S(1)}, f32[16,512]{1,0:T(8,128)S(1)}) custom-call(bf16[512,1024]{1,0:T(8,128)(2,1)S(1)} %pad_maximum_fusion.1.x_ref, bf16[512,128]{1,0:T(8,128)(2,1)S(1)} %pad_maximum_fusion.8.w_ref, bf16[512,128]{1,0:T(8,128)(2,1)S(1)} %pad_maximum_fusion.9.r_ref, ...), custom_call_target="tpu_custom_call" | custom-call | flops 1073741824 | bytes 1900544 | tf_op jit(solution)/shard_map/pallas_call | solution.py:425
  35.8 0.5 shard_map.116
  36.3 1.2 collective-permute-done.7
  37.5 0.2 shard_map.117
  37.8 10.5 %collective-permute-start.8 = (f16[144,1024]{1,0:T(8,128)(2,1)S(1)}, f16[144,1024]{1,0:T(8,128)(2,1)S(1)}, u32[]{:S(2)}, u32[]{:S(2)}) collective-permute-start(f16[144,1024]{1,0:T(8,128)(2,1)S(1)} %convert_element_type.41), channel_id=1, source_target_pairs={{0,4},{1,5},{2,6},{3,7},{4,0},{5,1},{6,2},{7,3},{8,12},{9,13},{10,... | collective-permute-start | bytes 884744 | tf_op jit(solution)/shard_map/ppermute | solution.py:458
  48.4 12.7 %collective-permute-done.8 = f16[144,1024]{1,0:T(8,128)(2,1)S(1)} collective-permute-done((f16[144,1024]{1,0:T(8,128)(2,1)S(1)}, f16[144,1024]{1,0:T(8,128)(2,1)S(1)}, u32[]{:S(2)}, u32[]{:S(2)}) %collective-permute-start.8) | collective-permute-done | bytes 294944 | tf_op jit(solution)/shard_map/ppermute | solution.py:458
  61.2 0.1 fusion.2.sin_ref
  61.4 1.5 %shard_map.118 = (f32[512,1024]{1,0:T(8,128)S(1)}, f32[128,1024]{1,0:T(8,128)S(1)}, f32[144,1024]{1,0:T(8,128)S(1)}) custom-call(f32[512,1024]{1,0:T(8,128)S(1)} %get-tuple-element.45.y_ref, f32[1024,512]{1,0:T(8,128)S(1)} %get-tuple-element.58.acc_ref, f32[8,512]{1,0:T(8,128)S(1)} %get-tuple-element.59.l_ref, bf16[512,128]{1,0:T(8,128)(2,1)S(1)} %pad_maximum_fusion.9.r_ref, ...), custom_call_target="tpu_custom_call" | custom-call | flops 1073741824 | bytes 6963200 | tf_op jit(solution)/shard_map/pallas_call | solution.py:425
  62.9 2.3 %collective-permute-start.10 = (f16[144,1024]{1,0:T(8,128)(2,1)S(1)}, f16[144,1024]{1,0:T(8,128)(2,1)S(1)}, u32[]{:S(2)}, u32[]{:S(2)}) collective-permute-start(f16[144,1024]{1,0:T(8,128)(2,1)S(1)} %convert_element_type.43), channel_id=1, source_target_pairs={{0,2},{1,3},{2,0},{3,1},{4,6},{5,7},{6,4},{7,5},{8,10},{9,11},{10,... | collective-permute-start | bytes 884744 | tf_op jit(solution)/shard_map/ppermute | solution.py:458
  65.2 1.3 %collective-permute-start.11 = (f16[144,1024]{1,0:T(8,128)(2,1)S(1)}, f16[144,1024]{1,0:T(8,128)(2,1)S(1)}, u32[]{:S(2)}, u32[]{:S(2)}) collective-permute-start(f16[144,1024]{1,0:T(8,128)(2,1)S(1)} %convert_element_type.43), channel_id=1, source_target_pairs={{0,4},{1,5},{2,6},{3,7},{4,0},{5,1},{6,2},{7,3},{8,12},{9,13},{10,... | collective-permute-start | bytes 884744 | tf_op jit(solution)/shard_map/ppermute | solution.py:458
  66.4 0.5 collective-permute-start.12
  66.9 8.0 %shard_map.119 = (f32[512,1024]{1,0:T(8,128)S(1)}, f32[256,256]{1,0:T(8,128)S(1)}, f32[256,256]{1,0:T(8,128)S(1)}) custom-call(f32[512,1024]{1,0:T(8,128)S(1)} %get-tuple-element.62.res_ref, bf16[512,1024]{1,0:T(8,128)(2,1)S(1)} %pad_maximum_fusion.1.x_ref, bf16[512,128]{1,0:T(8,128)(2,1)S(1)} %pad_maximum_fusion.8.w_ref, ...), custom_call_target="tpu_custom_call" | custom-call | flops 2147483648 | bytes 11304960 | tf_op jit(solution)/shard_map/pallas_call | solution.py:425
  75.0 0.1 collective-permute-start.14
  75.1 2.1 %collective-permute-done.10 = f16[144,1024]{1,0:T(8,128)(2,1)S(1)} collective-permute-done((f16[144,1024]{1,0:T(8,128)(2,1)S(1)}, f16[144,1024]{1,0:T(8,128)(2,1)S(1)}, u32[]{:S(2)}, u32[]{:S(2)}) %collective-permute-start.10) | collective-permute-done | bytes 294944 | tf_op jit(solution)/shard_map/ppermute | solution.py:458
  77.2 9.3 %collective-permute-done.11 = f16[144,1024]{1,0:T(8,128)(2,1)S(1)} collective-permute-done((f16[144,1024]{1,0:T(8,128)(2,1)S(1)}, f16[144,1024]{1,0:T(8,128)(2,1)S(1)}, u32[]{:S(2)}, u32[]{:S(2)}) %collective-permute-start.11) | collective-permute-done | bytes 294944 | tf_op jit(solution)/shard_map/ppermute | solution.py:458
  86.5 6.2 %collective-permute-done.12 = f16[144,1024]{1,0:T(8,128)(2,1)S(1)} collective-permute-done((f16[144,1024]{1,0:T(8,128)(2,1)S(1)}, f16[144,1024]{1,0:T(8,128)(2,1)S(1)}, u32[]{:S(2)}, u32[]{:S(2)}) %collective-permute-start.12) | collective-permute-done | bytes 294944 | tf_op jit(solution)/shard_map/ppermute | solution.py:458
  92.6 0.2 maximum_convert_fusion
  92.9 0.2 fusion
  93.1 0.1 collective-permute-start.13
  93.2 1.6 %collective-permute-start.19 = (f32[256,128]{1,0:T(8,128)S(1)}, f32[256,128]{1,0:T(8,128)S(1)}, u32[]{:S(2)}, u32[]{:S(2)}) collective-permute-start(f32[256,128]{1,0:T(8,128)S(1)} %slice.104), channel_id=1, source_target_pairs={{0,8},{8,0},{16,24},{24,16},{1,9},{9,1},{17,25},{25,17},{2,10},{10... | collective-permute-start | bytes 393224 | tf_op jit(solution)/shard_map/ppermute | solution.py:601
  94.8 1.1 constant_dynamic-slice_fusion
  95.9 0.2 collective-permute-start.9
  96.1 3.1 %collective-permute-done.19 = f32[256,128]{1,0:T(8,128)S(1)} collective-permute-done((f32[256,128]{1,0:T(8,128)S(1)}, f32[256,128]{1,0:T(8,128)S(1)}, u32[]{:S(2)}, u32[]{:S(2)}) %collective-permute-start.19) | collective-permute-done | bytes 131104 | tf_op jit(solution)/shard_map/ppermute | solution.py:601
  99.2 0.3 broadcast_select_fusion.5
  99.6 0.8 shard_map.122
  100.3 1.6 %collective-permute-start.15 = (f32[128,128]{1,0:T(8,128)S(1)}, f32[128,128]{1,0:T(8,128)S(1)}, u32[]{:S(2)}, u32[]{:S(2)}) collective-permute-start(f32[128,128]{1,0:T(8,128)S(1)} %get-tuple-element.75), channel_id=1, source_target_pairs={{0,8},{8,0},{16,24},{24,16},{1,9},{9,1},{17,25},{25,17},{2,10},{10... | collective-permute-start | bytes 196616 | tf_op jit(solution)/shard_map/ppermute | solution.py:601
  101.9 0.5 collective-permute-start.20
  102.4 1.5 %collective-permute-start.17 = (f32[128,128]{1,0:T(8,128)S(1)}, f32[128,128]{1,0:T(8,128)S(1)}, u32[]{:S(2)}, u32[]{:S(2)}) collective-permute-start(f32[128,128]{1,0:T(8,128)S(1)} %get-tuple-element.76), channel_id=1, source_target_pairs={{0,16},{8,24},{16,0},{24,8},{1,17},{9,25},{17,1},{25,9},{2,18},{10... | collective-permute-start | bytes 196616 | tf_op jit(solution)/shard_map/ppermute | solution.py:601
  103.9 0.7 collective-permute-done.15
  104.7 0.6 collective-permute-start.16
  105.2 3.5 %collective-permute-done.17 = f32[128,128]{1,0:T(8,128)S(1)} collective-permute-done((f32[128,128]{1,0:T(8,128)S(1)}, f32[128,128]{1,0:T(8,128)S(1)}, u32[]{:S(2)}, u32[]{:S(2)}) %collective-permute-start.17) | collective-permute-done | bytes 65568 | tf_op jit(solution)/shard_map/ppermute | solution.py:601
  108.8 0.6 collective-permute-start.18
  109.4 1.6 %add.139 = f32[256,128]{1,0:T(8,128)} add(f32[256,128]{1,0:T(8,128)S(1)} %get-tuple-element.97, f32[256,128]{1,0:T(8,128)} %collective-permute-done.20) | non-fusion elementwise | flops 32768 | bytes 393216 | tf_op jit(solution)/shard_map/add | solution.py:604
  111.0 2.2 %collective-permute-done.18 = f32[128,128]{1,0:T(8,128)} collective-permute-done((f32[128,128]{1,0:T(8,128)S(1)}, f32[128,128]{1,0:T(8,128)}, u32[]{:S(2)}, u32[]{:S(2)}) %collective-permute-start.18) | collective-permute-done | bytes 65568 | tf_op jit(solution)/shard_map/ppermute | solution.py:601
  113.2 0.8 add.137
  114.1 0.7 pad_maximum_fusion.10
  114.7 1.4 %dynamic-slice_select_fusion.1 = (f32[256,1024]{1,0:T(8,128)S(1)}, f32[256,1024]{1,0:T(8,128)S(1)}) fusion(f32[256,1024]{1,0:T(8,128)S(1)} %collective-permute-done.9, f32[512,1024]{1,0:T(8,128)} %copy-done.3, s32[]{:T(128)S(6)} %select_n.388, pred[]{:T(512)S(6)} %eq.11), kind=kLoop, calls=%fused_computation.5 | loop fusion | flops 524288 | bytes 4194309 | tf_op jit(solution)/shard_map/jit(_where)/select_n | solution.py:464
  116.1 0.2 pad_maximum_fusion.back_ref
  116.4 1.4 %copy-done.2 = f32[256,2048]{1,0:T(8,128)S(1)} copy-done((f32[256,2048]{1,0:T(8,128)S(1)}, f32[256,2048]{1,0:T(8,128)}, u32[]{:S(2)}) %copy-start.2) | copy-done | bytes 2097176
  117.7 2.2 %shard_map.121 = (f32[256,2048]{1,0:T(8,128)}, f32[32,256]{1,0:T(8,128)}) custom-call(f32[256,2048]{1,0:T(8,128)S(1)} %pad_maximum_fusion.back_ref, f32[256,2048]{1,0:T(8,128)S(1)} %copy-done.2, bf16[256,2048]{1,0:T(8,128)(2,1)S(1)} %copy-done, bf16[256,128]{1,0:T(8,128)(2,1)S(1)} %copy-done.4, f32[128,2048]{1,0:T(8,128)S(1)} %pad_maximum_fusion.3.g_ref), custom_call_target="tpu_custom_call" | custom-call | flops 1073741824 | bytes 6356992 | tf_op jit(solution)/shard_map/pallas_call | solution.py:425
  (57 shorter events, 0.9 us)
Async XLA Ops:
  0.6 4.1 %copy-start.6 = (f32[32,256]{1,0:T(8,128)S(1)}, f32[32,256]{1,0:T(8,128)}, u32[]{:S(2)}) copy-start(f32[32,256]{1,0:T(8,128)} %ls_ref.1) | copy-start | bytes 98308
  0.6 4.1 %copy-start.5 = (f32[32,256]{1,0:T(8,128)S(1)}, f32[32,256]{1,0:T(8,128)}, u32[]{:S(2)}) copy-start(f32[32,256]{1,0:T(8,128)} %ld_ref.1) | copy-start | bytes 98308
  0.7 4.1 %copy-start = (bf16[256,2048]{1,0:T(8,128)(2,1)S(1)}, bf16[256,2048]{1,0:T(8,128)(2,1)}, u32[]{:S(2)}) copy-start(bf16[256,2048]{1,0:T(8,128)(2,1)} %x_ref.3) | copy-start | bytes 3145732
  0.7 3.6 %copy-start.7 = (bf16[256,2048]{1,0:T(8,128)(2,1)S(1)}, bf16[256,2048]{1,0:T(8,128)(2,1)}, u32[]{:S(2)}) copy-start(bf16[256,2048]{1,0:T(8,128)(2,1)} %param.8) | copy-start | bytes 3145732
  1.6 1.6 %collective-permute-start.2 = (f32[64,256]{1,0:T(8,128)S(1)}, f32[64,256]{1,0:T(8,128)S(1)}, u32[]{:S(2)}, u32[]{:S(2)}) collective-permute-start(f32[64,256]{1,0:T(8,128)S(1)} %pad_maximum_fusion.11), channel_id=1, source_target_pairs={{0,1},{1,0},{2,3},{3,2},{4,5},{5,4},{6,7},{7,6},{8,9},{9,8},{10,11... | collective-permute-start | bytes 196616 | tf_op jit(solution)/shard_map/ppermute | solution.py:458
  2.6 1.5 %collective-permute-start = (bf16[256,256]{1,0:T(8,128)(2,1)S(1)}, bf16[256,256]{1,0:T(8,128)(2,1)S(1)}, u32[]{:S(2)}, u32[]{:S(2)}) collective-permute-start(bf16[256,256]{1,0:T(8,128)(2,1)S(1)} %pad_maximum_fusion.7), channel_id=1, source_target_pairs={{0,1},{1,0},{2,3},{3,2},{4,5},{5,4},{6,7},{7,6},{8,9},{9,8},{10,11... | collective-permute-start | bytes 393224 | tf_op jit(solution)/shard_map/ppermute | solution.py:458
  4.1 6.0 %copy-start.4 = (bf16[256,128]{1,0:T(8,128)(2,1)S(1)}, bf16[256,128]{1,0:T(8,128)(2,1)}, u32[]{:S(2)}) copy-start(bf16[256,128]{1,0:T(8,128)(2,1)} %w_ref.1) | copy-start | bytes 196612
  4.2 6.0 %copy-start.8 = (bf16[256,128]{1,0:T(8,128)(2,1)S(1)}, bf16[256,128]{1,0:T(8,128)(2,1)}, u32[]{:S(2)}) copy-start(bf16[256,128]{1,0:T(8,128)(2,1)} %param.13) | copy-start | bytes 196612
  4.3 6.0 %collective-permute-start.3 = (bf16[256,1024]{1,0:T(8,128)(2,1)S(1)}, bf16[256,1024]{1,0:T(8,128)(2,1)S(1)}, u32[]{:S(2)}, u32[]{:S(2)}) collective-permute-start(bf16[256,1024]{1,0:T(8,128)(2,1)S(1)} %constant_dynamic-slice_fusion.1), channel_id=1, source_target_pairs={{0,1},{1,0},{2,3},{3,2},{4,5},{5,4},{6,7},{7,6},{8,9},{9,8},{10,11... | collective-permute-start | bytes 1572872 | tf_op jit(solution)/shard_map/ppermute | solution.py:458
  5.7 1.4 %copy-start.1 = (f32[256,2048]{1,0:T(8,128)}, f32[256,2048]{1,0:T(8,128)S(1)}, u32[]{:S(2)}) copy-start(f32[256,2048]{1,0:T(8,128)S(1)} %get-tuple-element.68.wexp_ref) | copy-start | bytes 6291460
  7.1 14.0 %collective-permute-start.4 = (bf16[512,256]{1,0:T(8,128)(2,1)S(1)}, bf16[512,256]{1,0:T(8,128)(2,1)S(1)}, u32[]{:S(2)}, u32[]{:S(2)}) collective-permute-start(bf16[512,256]{1,0:T(8,128)(2,1)S(1)} %pad_maximum_fusion.5.kv_ref), channel_id=1, source_target_pairs={{0,4},{1,5},{2,6},{3,7},{4,0},{5,1},{6,2},{7,3},{8,12},{9,13},{10,... | collective-permute-start | bytes 786440 | tf_op jit(solution)/shard_map/ppermute | solution.py:458
  9.7 12.4 %collective-permute-start.6 = (bf16[512,256]{1,0:T(8,128)(2,1)S(1)}, bf16[512,256]{1,0:T(8,128)(2,1)S(1)}, u32[]{:S(2)}, u32[]{:S(2)}) collective-permute-start(bf16[512,256]{1,0:T(8,128)(2,1)S(1)} %pad_maximum_fusion.5.kv_ref), channel_id=1, source_target_pairs={{0,2},{1,3},{2,0},{3,1},{4,6},{5,7},{6,4},{7,5},{8,10},{9,11},{10,... | collective-permute-start | bytes 786440 | tf_op jit(solution)/shard_map/ppermute | solution.py:458
  10.3 16.1 %collective-permute-start.1 = (bf16[256,1280]{1,0:T(8,128)(2,1)S(1)}, bf16[256,1280]{1,0:T(8,128)(2,1)S(1)}, u32[]{:S(2)}, u32[]{:S(2)}) collective-permute-start(bf16[256,1280]{1,0:T(8,128)(2,1)S(1)} %pad_maximum_fusion.4), channel_id=1, source_target_pairs={{0,1},{1,0},{2,3},{3,2},{4,5},{5,4},{6,7},{7,6},{8,9},{9,8},{10,11... | collective-permute-start | bytes 1966088 | tf_op jit(solution)/shard_map/ppermute | solution.py:458
  21.1 14.8 %collective-permute-start.5 = (bf16[512,256]{1,0:T(8,128)(2,1)S(1)}, bf16[512,256]{1,0:T(8,128)(2,1)S(1)}, u32[]{:S(2)}, u32[]{:S(2)}) collective-permute-start(bf16[512,256]{1,0:T(8,128)(2,1)S(1)} %collective-permute-done.4.kv_ref), channel_id=1, source_target_pairs={{4,6},{5,7},{6,4},{7,5},{12,14},{13,15},{14,12},{15,13},{20,22},{2... | collective-permute-start | bytes 786440 | tf_op jit(solution)/shard_map/ppermute | solution.py:482
  28.8 8.7 %collective-permute-start.7 = (f16[144,1024]{1,0:T(8,128)(2,1)S(1)}, f16[144,1024]{1,0:T(8,128)(2,1)S(1)}, u32[]{:S(2)}, u32[]{:S(2)}) collective-permute-start(f16[144,1024]{1,0:T(8,128)(2,1)S(1)} %convert_element_type.39), channel_id=1, source_target_pairs={{0,2},{1,3},{2,0},{3,1},{4,6},{5,7},{6,4},{7,5},{8,10},{9,11},{10,... | collective-permute-start | bytes 884744 | tf_op jit(solution)/shard_map/ppermute | solution.py:458
  37.8 23.3 %collective-permute-start.8 = (f16[144,1024]{1,0:T(8,128)(2,1)S(1)}, f16[144,1024]{1,0:T(8,128)(2,1)S(1)}, u32[]{:S(2)}, u32[]{:S(2)}) collective-permute-start(f16[144,1024]{1,0:T(8,128)(2,1)S(1)} %convert_element_type.41), channel_id=1, source_target_pairs={{0,4},{1,5},{2,6},{3,7},{4,0},{5,1},{6,2},{7,3},{8,12},{9,13},{10,... | collective-permute-start | bytes 884744 | tf_op jit(solution)/shard_map/ppermute | solution.py:458
  62.9 14.3 %collective-permute-start.10 = (f16[144,1024]{1,0:T(8,128)(2,1)S(1)}, f16[144,1024]{1,0:T(8,128)(2,1)S(1)}, u32[]{:S(2)}, u32[]{:S(2)}) collective-permute-start(f16[144,1024]{1,0:T(8,128)(2,1)S(1)} %convert_element_type.43), channel_id=1, source_target_pairs={{0,2},{1,3},{2,0},{3,1},{4,6},{5,7},{6,4},{7,5},{8,10},{9,11},{10,... | collective-permute-start | bytes 884744 | tf_op jit(solution)/shard_map/ppermute | solution.py:458
  65.2 21.3 %collective-permute-start.11 = (f16[144,1024]{1,0:T(8,128)(2,1)S(1)}, f16[144,1024]{1,0:T(8,128)(2,1)S(1)}, u32[]{:S(2)}, u32[]{:S(2)}) collective-permute-start(f16[144,1024]{1,0:T(8,128)(2,1)S(1)} %convert_element_type.43), channel_id=1, source_target_pairs={{0,4},{1,5},{2,6},{3,7},{4,0},{5,1},{6,2},{7,3},{8,12},{9,13},{10,... | collective-permute-start | bytes 884744 | tf_op jit(solution)/shard_map/ppermute | solution.py:458
  66.4 26.2 %collective-permute-start.12 = (f16[144,1024]{1,0:T(8,128)(2,1)S(1)}, f16[144,1024]{1,0:T(8,128)(2,1)S(1)}, u32[]{:S(2)}, u32[]{:S(2)}) collective-permute-start(f16[144,1024]{1,0:T(8,128)(2,1)S(1)} %convert_element_type.43), channel_id=1, source_target_pairs={{0,6},{1,7},{2,4},{3,5},{4,2},{5,3},{6,0},{7,1},{8,14},{9,15},{10,... | collective-permute-start | bytes 884744 | tf_op jit(solution)/shard_map/ppermute | solution.py:458
  75.0 19.8 %copy-start.3 = (f32[512,1024]{1,0:T(8,128)}, f32[512,1024]{1,0:T(8,128)S(1)}, u32[]{:S(2)}) copy-start(f32[512,1024]{1,0:T(8,128)S(1)} %get-tuple-element.67) | copy-start | bytes 6291460
  75.0 18.1 %collective-permute-start.14 = (f32[256,256]{1,0:T(8,128)S(1)}, f32[256,256]{1,0:T(8,128)S(1)}, u32[]{:S(2)}, u32[]{:S(2)}) collective-permute-start(f32[256,256]{1,0:T(8,128)S(1)} %broadcast_select_fusion.6), channel_id=1, source_target_pairs={{0,1},{1,0},{2,3},{3,2},{4,5},{5,4},{6,7},{7,6},{8,9},{9,8},{10,11... | collective-permute-start | bytes 786440 | tf_op jit(solution)/shard_map/ppermute | solution.py:458
  93.1 6.1 %collective-permute-start.13 = (f32[128,1024]{1,0:T(8,128)S(1)}, f32[128,1024]{1,0:T(8,128)S(1)}, u32[]{:S(2)}, u32[]{:S(2)}) collective-permute-start(f32[128,1024]{1,0:T(8,128)S(1)} %fusion), channel_id=1, source_target_pairs={{0,1},{1,0},{2,3},{3,2},{4,5},{5,4},{6,7},{7,6},{8,9},{9,8},{10,11... | collective-permute-start | bytes 1572872 | tf_op jit(solution)/shard_map/ppermute | solution.py:458
  93.2 6.0 %collective-permute-start.19 = (f32[256,128]{1,0:T(8,128)S(1)}, f32[256,128]{1,0:T(8,128)S(1)}, u32[]{:S(2)}, u32[]{:S(2)}) collective-permute-start(f32[256,128]{1,0:T(8,128)S(1)} %slice.104), channel_id=1, source_target_pairs={{0,8},{8,0},{16,24},{24,16},{1,9},{9,1},{17,25},{25,17},{2,10},{10... | collective-permute-start | bytes 393224 | tf_op jit(solution)/shard_map/ppermute | solution.py:601
  95.9 18.8 %collective-permute-start.9 = (f32[256,1024]{1,0:T(8,128)}, f32[256,1024]{1,0:T(8,128)S(1)}, u32[]{:S(2)}, u32[]{:S(2)}) collective-permute-start(f32[256,1024]{1,0:T(8,128)} %constant_dynamic-slice_fusion), channel_id=1, source_target_pairs={{0,1},{1,0},{2,3},{3,2},{4,5},{5,4},{6,7},{7,6},{8,9},{9,8},{10,11... | collective-permute-start | bytes 3145736 | tf_op jit(solution)/shard_map/ppermute | solution.py:458
  100.3 4.3 %collective-permute-start.15 = (f32[128,128]{1,0:T(8,128)S(1)}, f32[128,128]{1,0:T(8,128)S(1)}, u32[]{:S(2)}, u32[]{:S(2)}) collective-permute-start(f32[128,128]{1,0:T(8,128)S(1)} %get-tuple-element.75), channel_id=1, source_target_pairs={{0,8},{8,0},{16,24},{24,16},{1,9},{9,1},{17,25},{25,17},{2,10},{10... | collective-permute-start | bytes 196616 | tf_op jit(solution)/shard_map/ppermute | solution.py:601
  101.9 7.5 %collective-permute-start.20 = (f32[256,128]{1,0:T(8,128)S(1)}, f32[256,128]{1,0:T(8,128)}, u32[]{:S(2)}, u32[]{:S(2)}) collective-permute-start(f32[256,128]{1,0:T(8,128)S(1)} %get-tuple-element.97), channel_id=1, source_target_pairs={{0,16},{8,24},{16,0},{24,8},{1,17},{9,25},{17,1},{25,9},{2,18},{10... | collective-permute-start | bytes 393224 | tf_op jit(solution)/shard_map/ppermute | solution.py:601
  102.4 6.4 %collective-permute-start.17 = (f32[128,128]{1,0:T(8,128)S(1)}, f32[128,128]{1,0:T(8,128)S(1)}, u32[]{:S(2)}, u32[]{:S(2)}) collective-permute-start(f32[128,128]{1,0:T(8,128)S(1)} %get-tuple-element.76), channel_id=1, source_target_pairs={{0,16},{8,24},{16,0},{24,8},{1,17},{9,25},{17,1},{25,9},{2,18},{10... | collective-permute-start | bytes 196616 | tf_op jit(solution)/shard_map/ppermute | solution.py:601
  104.7 6.3 %collective-permute-start.16 = (f32[128,128]{1,0:T(8,128)S(1)}, f32[128,128]{1,0:T(8,128)S(1)}, u32[]{:S(2)}, u32[]{:S(2)}) collective-permute-start(f32[128,128]{1,0:T(8,128)S(1)} %add.134), channel_id=1, source_target_pairs={{0,16},{8,24},{16,0},{24,8},{1,17},{9,25},{17,1},{25,9},{2,18},{10... | collective-permute-start | bytes 196616 | tf_op jit(solution)/shard_map/ppermute | solution.py:601
  108.8 4.4 %collective-permute-start.18 = (f32[128,128]{1,0:T(8,128)S(1)}, f32[128,128]{1,0:T(8,128)}, u32[]{:S(2)}, u32[]{:S(2)}) collective-permute-start(f32[128,128]{1,0:T(8,128)S(1)} %add.136), channel_id=1, source_target_pairs={{0,8},{8,0},{16,24},{24,16},{1,9},{9,1},{17,25},{25,17},{2,10},{10... | collective-permute-start | bytes 196616 | tf_op jit(solution)/shard_map/ppermute | solution.py:601
  116.1 1.6 %copy-start.2 = (f32[256,2048]{1,0:T(8,128)S(1)}, f32[256,2048]{1,0:T(8,128)}, u32[]{:S(2)}) copy-start(f32[256,2048]{1,0:T(8,128)} %copy-done.1) | copy-start | bytes 6291460

commit v9 on v7

--- a/solution.py
+++ b/solution.py
@@ -607,9 +607,10 @@
     own, other = home(shared)
     grads = own + other
     gw0, gr0 = grads[:, :n], grads[:, n:]
-    grad_read = jnp.concatenate(tp_sum([gr0[: t // 2], gr0[t // 2 :]]), axis=0)
+    (grad_read,) = tp_sum([gr0])
     arriving = combine(coming)
-    arrived = joined(arriving, swap(arriving, 1), 1)
+    met = swap(arriving, 1)
+    arrived = joined(arriving, met, 1)
     gwp = call(write_kernel, [((t // 2, n), F32)] * 2, (xh, xl, arrived, gw0), flops=4 * mm)
     grad_write = jnp.concatenate(tp_sum(gwp), axis=0)
     gi, gls = call(

time: 126 us -> 115 us (0.913)
  waiting for transfers between devices: 56 us -> 49.6 us
  other arithmetic: 7.75 us -> 5.6 us
  local copies, waits for them, and re-layouts: 2.81 us -> 1.18 us
    ppermute x14, waiting for transfers between devices: 46.1 us -> 39.2 us  [swap(): return lax.ppermute(a, 'seq', [(i, i ^ bits) for i in range(count)])]
    unnamed x18 -> x12, local copies, waits for them, and re-layouts: 1.63 us -> 0.03 us
    ppermute x8 -> x6, starting transfers between devices: 7.9 us -> 7.33 us  [tp_sum(): lax.ppermute(a, 'tp', [(i, i ^ 1 << (step + k) % bits) for i in range(tp)])]
    ppermute x8 -> x6, waiting for transfers between devices: 9.93 us -> 10.3 us  [tp_sum(): lax.ppermute(a, 'tp', [(i, i ^ 1 << (step + k) % bits) for i in range(tp)])]
  transfers between devices with their start and end apart: 23 -> 21, of which waited for: 15 -> 12; matrix products, arithmetic and copies ran while one was open for 5% -> 4% of each run, Pallas kernels for 15% -> 23%
where the time goes in v9:
time: 115 us
  waiting for transfers between devices  49.6 us (43%)
  Pallas kernels  30.2 us (26%)
  starting transfers between devices  27.2 us (24%)
  other arithmetic  5.6 us (5%)
  local copies, waits for them, and re-layouts  1.18 us (1%)
  between operations  1.18 us (1%)
    ppermute x14, waiting for transfers between devices, swap(): return lax.ppermute(a, 'seq', [(i, i ^ bits) for i in range(count)])  39.2 us
    pallas_call x12, Pallas kernels, call(): pl.pallas_call(kernel, out_shape=shapes, in_specs=in_specs or [VM] * len(...  30.2 us
    ppermute x14, starting transfers between devices, swap(): return lax.ppermute(a, 'seq', [(i, i ^ bits) for i in range(count)])  19.2 us
    ppermute x6, waiting for transfers between devices, tp_sum(): lax.ppermute(a, 'tp', [(i, i ^ 1 << (step + k) % bits) for i in range(tp)])  10.3 us
    ppermute x6, starting transfers between devices, tp_sum(): lax.ppermute(a, 'tp', [(i, i ^ 1 << (step + k) % bits) for i in range(tp)])  7.33 us
  transfers between devices with their start and end apart: 21, of which 12 were waited for; matrix products, arithmetic and copies ran while one was open for 4% of the time, Pallas kernels for 23%

profile of v9, /device:TPU:8, one launch (start us, length us, event | category | flops | bytes accessed | tf_op | source)
XLA Modules:
  0.0 114.9 jit_solution(18386122978524201160)
XLA Ops:
  0.7 0.9 pad_maximum_fusion.11
  1.6 1.0 constant_dynamic-slice_fusion.6
  2.6 0.5 collective-permute-start
  3.2 0.1 slice_reduce_fusion.3
  3.3 0.8 dynamic-slice_select_fusion.3
  4.0 0.1 collective-permute-done
  4.2 0.1 broadcast_select_fusion.7
  4.3 0.4 collective-permute-start.3
  4.8 1.0 shard_map.120
  5.7 2.7 %collective-permute-start.4 = (bf16[512,256]{1,0:T(8,128)(2,1)S(1)}, bf16[512,256]{1,0:T(8,128)(2,1)S(1)}, u32[]{:S(2)}, u32[]{:S(2)}) collective-permute-start(bf16[512,256]{1,0:T(8,128)(2,1)S(1)} %pad_maximum_fusion.5.kv_ref), channel_id=1, source_target_pairs={{0,4},{1,5},{2,6},{3,7},{4,0},{5,1},{6,2},{7,3},{8,12},{9,13},{10,... | collective-permute-start | bytes 786440 | tf_op jit(solution)/shard_map/ppermute | solution.py:457
  8.4 0.4 collective-permute-start.6
  8.9 0.1 pad_maximum_fusion.4
  9.0 0.1 collective-permute-start.1
  9.1 0.3 broadcast_select_fusion.1
  9.4 0.1 pad_maximum_fusion.2.q_ref
  9.4 3.1 %shard_map.113 = (bf16[512,2048]{1,0:T(8,128)(2,1)S(1)}, f32[1024,512]{1,0:T(8,128)S(1)}, f32[8,512]{1,0:T(8,128)S(1)}, f32[8,512]{1,0:T(8,128)S(1)}) custom-call(bf16[512,1024]{1,0:T(8,128)(2,1)S(1)} %pad_maximum_fusion.2.q_ref, bf16[512,256]{1,0:T(8,128)(2,1)S(1)} %pad_maximum_fusion.5.kv_ref), custom_call_target="tpu_custom_call" | custom-call | flops 1073741824 | bytes 1310720 | tf_op jit(solution)/shard_map/pallas_call | solution.py:424
  12.5 7.2 %collective-permute-done.4.kv_ref = bf16[512,256]{1,0:T(8,128)(2,1)S(1)} collective-permute-done((bf16[512,256]{1,0:T(8,128)(2,1)S(1)}, bf16[512,256]{1,0:T(8,128)(2,1)S(1)}, u32[]{:S(2)}, u32[]{:S(2)}) %collective-permute-start.4) | collective-permute-done | bytes 262176 | tf_op jit(solution)/shard_map/ppermute | solution.py:457
  19.8 0.7 collective-permute-start.5
  20.5 0.4 collective-permute-done.6.kv_ref
  20.8 3.9 %shard_map.114 = (f32[1024,512]{1,0:T(8,128)S(1)}, f32[8,512]{1,0:T(8,128)S(1)}, f32[8,512]{1,0:T(8,128)S(1)}) custom-call(s32[1]{0:T(128)} %bitcast.2.flag, bf16[512,2048]{1,0:T(8,128)(2,1)S(1)} %get-tuple-element.46.qs_ref, bf16[512,256]{1,0:T(8,128)(2,1)S(1)} %collective-permute-done.6.kv_ref, ...), custom_call_target="tpu_custom_call", output_to_operand_aliasing={{0}: (3, {}), {1}: (4, {}), {2}: (5, {})} | custom-call | flops 1073741824 | bytes 4489220 | tf_op jit(solution)/shard_map/pallas_call | solution.py:424
  24.8 0.3 shard_map.115
  25.1 0.3 broadcast_select_fusion.3
  25.4 0.1 pad_maximum_fusion.1.x_ref
  25.5 2.0 %shard_map.111 = (f32[128,1024]{1,0:T(8,128)S(1)}, f32[144,1024]{1,0:T(8,128)S(1)}, f32[512,1024]{1,0:T(8,128)S(1)}) custom-call(bf16[512,1024]{1,0:T(8,128)(2,1)S(1)} %pad_maximum_fusion.1.x_ref, bf16[512,128]{1,0:T(8,128)(2,1)S(1)} %pad_maximum_fusion.8.w_ref, f32[16,512]{1,0:T(8,128)S(1)} %pad_maximum_fusion.12.ls_ref, ...), custom_call_target="tpu_custom_call" | custom-call | flops 536870912 | bytes 1245184 | tf_op jit(solution)/shard_map/pallas_call | solution.py:424
  27.6 0.1 collective-permute-start.7
  27.7 6.9 %shard_map.112 = (f32[512,1024]{1,0:T(8,128)S(1)}, f32[512,1024]{1,0:T(8,128)S(1)}, f32[512,1024]{1,0:T(8,128)S(1)}, f32[16,512]{1,0:T(8,128)S(1)}) custom-call(bf16[512,1024]{1,0:T(8,128)(2,1)S(1)} %pad_maximum_fusion.1.x_ref, bf16[512,128]{1,0:T(8,128)(2,1)S(1)} %pad_maximum_fusion.8.w_ref, bf16[512,128]{1,0:T(8,128)(2,1)S(1)} %pad_maximum_fusion.9.r_ref, ...), custom_call_target="tpu_custom_call" | custom-call | flops 1073741824 | bytes 1900544 | tf_op jit(solution)/shard_map/pallas_call | solution.py:424
  34.6 0.5 shard_map.116
  35.0 1.2 %collective-permute-done.7 = f16[144,1024]{1,0:T(8,128)(2,1)S(1)} collective-permute-done((f16[144,1024]{1,0:T(8,128)(2,1)S(1)}, f16[144,1024]{1,0:T(8,128)(2,1)S(1)}, u32[]{:S(2)}, u32[]{:S(2)}) %collective-permute-start.7) | collective-permute-done | bytes 294944 | tf_op jit(solution)/shard_map/ppermute | solution.py:457
  36.3 0.2 shard_map.117
  36.5 10.5 %collective-permute-start.8 = (f16[144,1024]{1,0:T(8,128)(2,1)S(1)}, f16[144,1024]{1,0:T(8,128)(2,1)S(1)}, u32[]{:S(2)}, u32[]{:S(2)}) collective-permute-start(f16[144,1024]{1,0:T(8,128)(2,1)S(1)} %convert_element_type.41), channel_id=1, source_target_pairs={{0,4},{1,5},{2,6},{3,7},{4,0},{5,1},{6,2},{7,3},{8,12},{9,13},{10,... | collective-permute-start | bytes 884744 | tf_op jit(solution)/shard_map/ppermute | solution.py:457
  47.1 12.7 %collective-permute-done.8 = f16[144,1024]{1,0:T(8,128)(2,1)S(1)} collective-permute-done((f16[144,1024]{1,0:T(8,128)(2,1)S(1)}, f16[144,1024]{1,0:T(8,128)(2,1)S(1)}, u32[]{:S(2)}, u32[]{:S(2)}) %collective-permute-start.8) | collective-permute-done | bytes 294944 | tf_op jit(solution)/shard_map/ppermute | solution.py:457
  60.0 0.1 fusion.2.sin_ref
  60.0 1.4 %shard_map.118 = (f32[512,1024]{1,0:T(8,128)S(1)}, f32[128,1024]{1,0:T(8,128)S(1)}, f32[144,1024]{1,0:T(8,128)S(1)}) custom-call(f32[512,1024]{1,0:T(8,128)S(1)} %get-tuple-element.44.y_ref, f32[1024,512]{1,0:T(8,128)S(1)} %get-tuple-element.57.acc_ref, f32[8,512]{1,0:T(8,128)S(1)} %get-tuple-element.58.l_ref, bf16[512,128]{1,0:T(8,128)(2,1)S(1)} %pad_maximum_fusion.9.r_ref, ...), custom_call_target="tpu_custom_call" | custom-call | flops 1073741824 | bytes 6963200 | tf_op jit(solution)/shard_map/pallas_call | solution.py:424
  61.5 2.3 %collective-permute-start.10 = (f16[144,1024]{1,0:T(8,128)(2,1)S(1)}, f16[144,1024]{1,0:T(8,128)(2,1)S(1)}, u32[]{:S(2)}, u32[]{:S(2)}) collective-permute-start(f16[144,1024]{1,0:T(8,128)(2,1)S(1)} %convert_element_type.43), channel_id=1, source_target_pairs={{0,2},{1,3},{2,0},{3,1},{4,6},{5,7},{6,4},{7,5},{8,10},{9,11},{10,... | collective-permute-start | bytes 884744 | tf_op jit(solution)/shard_map/ppermute | solution.py:457
  63.8 1.2 %collective-permute-start.11 = (f16[144,1024]{1,0:T(8,128)(2,1)S(1)}, f16[144,1024]{1,0:T(8,128)(2,1)S(1)}, u32[]{:S(2)}, u32[]{:S(2)}) collective-permute-start(f16[144,1024]{1,0:T(8,128)(2,1)S(1)} %convert_element_type.43), channel_id=1, source_target_pairs={{0,4},{1,5},{2,6},{3,7},{4,0},{5,1},{6,2},{7,3},{8,12},{9,13},{10,... | collective-permute-start | bytes 884744 | tf_op jit(solution)/shard_map/ppermute | solution.py:457
  65.0 0.5 collective-permute-start.12
  65.5 8.0 %shard_map.119 = (f32[512,1024]{1,0:T(8,128)S(1)}, f32[512,256]{1,0:T(8,128)S(1)}) custom-call(f32[512,1024]{1,0:T(8,128)S(1)} %get-tuple-element.61.res_ref, bf16[512,1024]{1,0:T(8,128)(2,1)S(1)} %pad_maximum_fusion.1.x_ref, bf16[512,128]{1,0:T(8,128)(2,1)S(1)} %pad_maximum_fusion.8.w_ref, bf16[512,128]{1,0:T(8,128)(2,1)S(1)} %pad_maximum_fusion.9.r_ref, ...), custom_call_target="tpu_custom_call" | custom-call | flops 2147483648 | bytes 11304960 | tf_op jit(solution)/shard_map/pallas_call | solution.py:424
  73.6 0.1 collective-permute-start.14
  73.7 2.1 %collective-permute-done.10 = f16[144,1024]{1,0:T(8,128)(2,1)S(1)} collective-permute-done((f16[144,1024]{1,0:T(8,128)(2,1)S(1)}, f16[144,1024]{1,0:T(8,128)(2,1)S(1)}, u32[]{:S(2)}, u32[]{:S(2)}) %collective-permute-start.10) | collective-permute-done | bytes 294944 | tf_op jit(solution)/shard_map/ppermute | solution.py:457
  75.8 9.3 %collective-permute-done.11 = f16[144,1024]{1,0:T(8,128)(2,1)S(1)} collective-permute-done((f16[144,1024]{1,0:T(8,128)(2,1)S(1)}, f16[144,1024]{1,0:T(8,128)(2,1)S(1)}, u32[]{:S(2)}, u32[]{:S(2)}) %collective-permute-start.11) | collective-permute-done | bytes 294944 | tf_op jit(solution)/shard_map/ppermute | solution.py:457
  85.1 6.2 %collective-permute-done.12 = f16[144,1024]{1,0:T(8,128)(2,1)S(1)} collective-permute-done((f16[144,1024]{1,0:T(8,128)(2,1)S(1)}, f16[144,1024]{1,0:T(8,128)(2,1)S(1)}, u32[]{:S(2)}, u32[]{:S(2)}) %collective-permute-start.12) | collective-permute-done | bytes 294944 | tf_op jit(solution)/shard_map/ppermute | solution.py:457
  91.2 0.2 maximum_convert_fusion
  91.5 0.2 fusion
  91.7 0.1 collective-permute-start.13
  91.8 1.6 %collective-permute-start.19 = (f32[256,128]{1,0:T(8,128)S(1)}, f32[256,128]{1,0:T(8,128)S(1)}, u32[]{:S(2)}, u32[]{:S(2)}) collective-permute-start(f32[256,128]{1,0:T(8,128)S(1)} %slice.104), channel_id=1, source_target_pairs={{0,8},{8,0},{16,24},{24,16},{1,9},{9,1},{17,25},{25,17},{2,10},{10... | collective-permute-start | bytes 393224 | tf_op jit(solution)/shard_map/ppermute | solution.py:600
  93.4 0.1 constant_dynamic-slice_fusion.1
  93.5 0.3 collective-permute-start.9
  93.7 4.0 %collective-permute-done.19 = f32[256,128]{1,0:T(8,128)S(1)} collective-permute-done((f32[256,128]{1,0:T(8,128)S(1)}, f32[256,128]{1,0:T(8,128)S(1)}, u32[]{:S(2)}, u32[]{:S(2)}) %collective-permute-start.19) | collective-permute-done | bytes 131104 | tf_op jit(solution)/shard_map/ppermute | solution.py:600
  97.8 0.2 broadcast_select_fusion.5
  98.0 0.1 pad_maximum_fusion.3.g_ref
  98.1 0.8 shard_map.122
  98.9 1.6 %collective-permute-start.15 = (f32[128,128]{1,0:T(8,128)S(1)}, f32[128,128]{1,0:T(8,128)S(1)}, u32[]{:S(2)}, u32[]{:S(2)}) collective-permute-start(f32[128,128]{1,0:T(8,128)S(1)} %get-tuple-element.73), channel_id=1, source_target_pairs={{0,8},{8,0},{16,24},{24,16},{1,9},{9,1},{17,25},{25,17},{2,10},{10... | collective-permute-start | bytes 196616 | tf_op jit(solution)/shard_map/ppermute | solution.py:600
  100.4 1.5 %collective-permute-start.20 = (f32[256,128]{1,0:T(8,128)S(1)}, f32[256,128]{1,0:T(8,128)S(1)}, u32[]{:S(2)}, u32[]{:S(2)}) collective-permute-start(f32[256,128]{1,0:T(8,128)S(1)} %get-tuple-element.95), channel_id=1, source_target_pairs={{0,16},{8,24},{16,0},{24,8},{1,17},{9,25},{17,1},{25,9},{2,18},{10... | collective-permute-start | bytes 393224 | tf_op jit(solution)/shard_map/ppermute | solution.py:600
  102.0 0.5 collective-permute-start.17
  102.5 0.7 collective-permute-done.15
  103.2 1.6 %collective-permute-start.16 = (f32[128,128]{1,0:T(8,128)S(1)}, f32[128,128]{1,0:T(8,128)S(1)}, u32[]{:S(2)}, u32[]{:S(2)}) collective-permute-start(f32[128,128]{1,0:T(8,128)S(1)} %add.136), channel_id=1, source_target_pairs={{0,16},{8,24},{16,0},{24,8},{1,17},{9,25},{17,1},{25,9},{2,18},{10... | collective-permute-start | bytes 196616 | tf_op jit(solution)/shard_map/ppermute | solution.py:600
  104.8 2.5 %collective-permute-done.17 = f32[128,128]{1,0:T(8,128)S(1)} collective-permute-done((f32[128,128]{1,0:T(8,128)S(1)}, f32[128,128]{1,0:T(8,128)S(1)}, u32[]{:S(2)}, u32[]{:S(2)}) %collective-permute-start.17) | collective-permute-done | bytes 65568 | tf_op jit(solution)/shard_map/ppermute | solution.py:600
  107.3 0.6 collective-permute-start.18
  107.9 0.7 add.141
  108.6 3.0 %collective-permute-done.18 = f32[128,128]{1,0:T(8,128)S(1)} collective-permute-done((f32[128,128]{1,0:T(8,128)S(1)}, f32[128,128]{1,0:T(8,128)S(1)}, u32[]{:S(2)}, u32[]{:S(2)}) %collective-permute-start.18) | collective-permute-done | bytes 65568 | tf_op jit(solution)/shard_map/ppermute | solution.py:600
  111.7 0.7 pad_maximum_fusion.10
  112.3 0.2 dynamic-slice_select_fusion.1
  112.5 0.2 pad_maximum_fusion.back_ref
  112.8 2.2 %shard_map.121 = (f32[256,2048]{1,0:T(8,128)}, f32[32,256]{1,0:T(8,128)}) custom-call(f32[256,2048]{1,0:T(8,128)S(1)} %pad_maximum_fusion.back_ref, f32[256,2048]{1,0:T(8,128)S(1)} %get-tuple-element.67.wexp_ref, bf16[256,2048]{1,0:T(8,128)(2,1)S(1)} %copy-done, bf16[256,128]{1,0:T(8,128)(2,1)S(1)} %copy-done.1, f32[128,2048]{1,0:T(8,128)S(1)} %pad_maximum_fusion.3.g_ref), custom_call_target="tpu_custom_call" | custom-call | flops 1073741824 | bytes 6356992 | tf_op jit(solution)/shard_map/pallas_call | solution.py:424
  (51 shorter events, 0.7 us)
Async XLA Ops:
  0.6 4.1 %copy-start.3 = (f32[32,256]{1,0:T(8,128)S(1)}, f32[32,256]{1,0:T(8,128)}, u32[]{:S(2)}) copy-start(f32[32,256]{1,0:T(8,128)} %ls_ref.1) | copy-start | bytes 98308
  0.6 4.1 %copy-start.2 = (f32[32,256]{1,0:T(8,128)S(1)}, f32[32,256]{1,0:T(8,128)}, u32[]{:S(2)}) copy-start(f32[32,256]{1,0:T(8,128)} %ld_ref.1) | copy-start | bytes 98308
  0.7 4.1 %copy-start = (bf16[256,2048]{1,0:T(8,128)(2,1)S(1)}, bf16[256,2048]{1,0:T(8,128)(2,1)}, u32[]{:S(2)}) copy-start(bf16[256,2048]{1,0:T(8,128)(2,1)} %x_ref.3) | copy-start | bytes 3145732
  0.7 3.6 %copy-start.4 = (bf16[256,2048]{1,0:T(8,128)(2,1)S(1)}, bf16[256,2048]{1,0:T(8,128)(2,1)}, u32[]{:S(2)}) copy-start(bf16[256,2048]{1,0:T(8,128)(2,1)} %param.8) | copy-start | bytes 3145732
  1.6 1.6 %collective-permute-start.2 = (f32[64,256]{1,0:T(8,128)S(1)}, f32[64,256]{1,0:T(8,128)S(1)}, u32[]{:S(2)}, u32[]{:S(2)}) collective-permute-start(f32[64,256]{1,0:T(8,128)S(1)} %pad_maximum_fusion.11), channel_id=1, source_target_pairs={{0,1},{1,0},{2,3},{3,2},{4,5},{5,4},{6,7},{7,6},{8,9},{9,8},{10,11... | collective-permute-start | bytes 196616 | tf_op jit(solution)/shard_map/ppermute | solution.py:457
  2.6 1.5 %collective-permute-start = (bf16[256,256]{1,0:T(8,128)(2,1)S(1)}, bf16[256,256]{1,0:T(8,128)(2,1)S(1)}, u32[]{:S(2)}, u32[]{:S(2)}) collective-permute-start(bf16[256,256]{1,0:T(8,128)(2,1)S(1)} %pad_maximum_fusion.7), channel_id=1, source_target_pairs={{0,1},{1,0},{2,3},{3,2},{4,5},{5,4},{6,7},{7,6},{8,9},{9,8},{10,11... | collective-permute-start | bytes 393224 | tf_op jit(solution)/shard_map/ppermute | solution.py:457
  4.1 4.7 %copy-start.1 = (bf16[256,128]{1,0:T(8,128)(2,1)S(1)}, bf16[256,128]{1,0:T(8,128)(2,1)}, u32[]{:S(2)}) copy-start(bf16[256,128]{1,0:T(8,128)(2,1)} %w_ref.1) | copy-start | bytes 196612
  4.2 4.7 %copy-start.5 = (bf16[256,128]{1,0:T(8,128)(2,1)S(1)}, bf16[256,128]{1,0:T(8,128)(2,1)}, u32[]{:S(2)}) copy-start(bf16[256,128]{1,0:T(8,128)(2,1)} %param.13) | copy-start | bytes 196612
  4.3 4.7 %collective-permute-start.3 = (bf16[256,1024]{1,0:T(8,128)(2,1)S(1)}, bf16[256,1024]{1,0:T(8,128)(2,1)S(1)}, u32[]{:S(2)}, u32[]{:S(2)}) collective-permute-start(bf16[256,1024]{1,0:T(8,128)(2,1)S(1)} %constant_dynamic-slice_fusion.2), channel_id=1, source_target_pairs={{0,1},{1,0},{2,3},{3,2},{4,5},{5,4},{6,7},{7,6},{8,9},{9,8},{10,11... | collective-permute-start | bytes 1572872 | tf_op jit(solution)/shard_map/ppermute | solution.py:457
  5.7 14.0 %collective-permute-start.4 = (bf16[512,256]{1,0:T(8,128)(2,1)S(1)}, bf16[512,256]{1,0:T(8,128)(2,1)S(1)}, u32[]{:S(2)}, u32[]{:S(2)}) collective-permute-start(bf16[512,256]{1,0:T(8,128)(2,1)S(1)} %pad_maximum_fusion.5.kv_ref), channel_id=1, source_target_pairs={{0,4},{1,5},{2,6},{3,7},{4,0},{5,1},{6,2},{7,3},{8,12},{9,13},{10,... | collective-permute-start | bytes 786440 | tf_op jit(solution)/shard_map/ppermute | solution.py:457
  8.4 12.4 %collective-permute-start.6 = (bf16[512,256]{1,0:T(8,128)(2,1)S(1)}, bf16[512,256]{1,0:T(8,128)(2,1)S(1)}, u32[]{:S(2)}, u32[]{:S(2)}) collective-permute-start(bf16[512,256]{1,0:T(8,128)(2,1)S(1)} %pad_maximum_fusion.5.kv_ref), channel_id=1, source_target_pairs={{0,2},{1,3},{2,0},{3,1},{4,6},{5,7},{6,4},{7,5},{8,10},{9,11},{10,... | collective-permute-start | bytes 786440 | tf_op jit(solution)/shard_map/ppermute | solution.py:457
  9.0 16.1 %collective-permute-start.1 = (bf16[256,1280]{1,0:T(8,128)(2,1)S(1)}, bf16[256,1280]{1,0:T(8,128)(2,1)S(1)}, u32[]{:S(2)}, u32[]{:S(2)}) collective-permute-start(bf16[256,1280]{1,0:T(8,128)(2,1)S(1)} %pad_maximum_fusion.4), channel_id=1, source_target_pairs={{0,1},{1,0},{2,3},{3,2},{4,5},{5,4},{6,7},{7,6},{8,9},{9,8},{10,11... | collective-permute-start | bytes 1966088 | tf_op jit(solution)/shard_map/ppermute | solution.py:457
  19.8 14.8 %collective-permute-start.5 = (bf16[512,256]{1,0:T(8,128)(2,1)S(1)}, bf16[512,256]{1,0:T(8,128)(2,1)S(1)}, u32[]{:S(2)}, u32[]{:S(2)}) collective-permute-start(bf16[512,256]{1,0:T(8,128)(2,1)S(1)} %collective-permute-done.4.kv_ref), channel_id=1, source_target_pairs={{4,6},{5,7},{6,4},{7,5},{12,14},{13,15},{14,12},{15,13},{20,22},{2... | collective-permute-start | bytes 786440 | tf_op jit(solution)/shard_map/ppermute | solution.py:481
  27.6 8.7 %collective-permute-start.7 = (f16[144,1024]{1,0:T(8,128)(2,1)S(1)}, f16[144,1024]{1,0:T(8,128)(2,1)S(1)}, u32[]{:S(2)}, u32[]{:S(2)}) collective-permute-start(f16[144,1024]{1,0:T(8,128)(2,1)S(1)} %convert_element_type.39), channel_id=1, source_target_pairs={{0,2},{1,3},{2,0},{3,1},{4,6},{5,7},{6,4},{7,5},{8,10},{9,11},{10,... | collective-permute-start | bytes 884744 | tf_op jit(solution)/shard_map/ppermute | solution.py:457
  36.5 23.3 %collective-permute-start.8 = (f16[144,1024]{1,0:T(8,128)(2,1)S(1)}, f16[144,1024]{1,0:T(8,128)(2,1)S(1)}, u32[]{:S(2)}, u32[]{:S(2)}) collective-permute-start(f16[144,1024]{1,0:T(8,128)(2,1)S(1)} %convert_element_type.41), channel_id=1, source_target_pairs={{0,4},{1,5},{2,6},{3,7},{4,0},{5,1},{6,2},{7,3},{8,12},{9,13},{10,... | collective-permute-start | bytes 884744 | tf_op jit(solution)/shard_map/ppermute | solution.py:457
  61.5 14.3 %collective-permute-start.10 = (f16[144,1024]{1,0:T(8,128)(2,1)S(1)}, f16[144,1024]{1,0:T(8,128)(2,1)S(1)}, u32[]{:S(2)}, u32[]{:S(2)}) collective-permute-start(f16[144,1024]{1,0:T(8,128)(2,1)S(1)} %convert_element_type.43), channel_id=1, source_target_pairs={{0,2},{1,3},{2,0},{3,1},{4,6},{5,7},{6,4},{7,5},{8,10},{9,11},{10,... | collective-permute-start | bytes 884744 | tf_op jit(solution)/shard_map/ppermute | solution.py:457
  63.8 21.3 %collective-permute-start.11 = (f16[144,1024]{1,0:T(8,128)(2,1)S(1)}, f16[144,1024]{1,0:T(8,128)(2,1)S(1)}, u32[]{:S(2)}, u32[]{:S(2)}) collective-permute-start(f16[144,1024]{1,0:T(8,128)(2,1)S(1)} %convert_element_type.43), channel_id=1, source_target_pairs={{0,4},{1,5},{2,6},{3,7},{4,0},{5,1},{6,2},{7,3},{8,12},{9,13},{10,... | collective-permute-start | bytes 884744 | tf_op jit(solution)/shard_map/ppermute | solution.py:457
  65.0 26.2 %collective-permute-start.12 = (f16[144,1024]{1,0:T(8,128)(2,1)S(1)}, f16[144,1024]{1,0:T(8,128)(2,1)S(1)}, u32[]{:S(2)}, u32[]{:S(2)}) collective-permute-start(f16[144,1024]{1,0:T(8,128)(2,1)S(1)} %convert_element_type.43), channel_id=1, source_target_pairs={{0,6},{1,7},{2,4},{3,5},{4,2},{5,3},{6,0},{7,1},{8,14},{9,15},{10,... | collective-permute-start | bytes 884744 | tf_op jit(solution)/shard_map/ppermute | solution.py:457
  73.6 18.2 %collective-permute-start.14 = (f32[256,256]{1,0:T(8,128)S(1)}, f32[256,256]{1,0:T(8,128)S(1)}, u32[]{:S(2)}, u32[]{:S(2)}) collective-permute-start(f32[256,256]{1,0:T(8,128)S(1)} %constant_dynamic-slice_fusion), channel_id=1, source_target_pairs={{0,1},{1,0},{2,3},{3,2},{4,5},{5,4},{6,7},{7,6},{8,9},{9,8},{10,11... | collective-permute-start | bytes 786440 | tf_op jit(solution)/shard_map/ppermute | solution.py:457
  91.7 6.1 %collective-permute-start.13 = (f32[128,1024]{1,0:T(8,128)S(1)}, f32[128,1024]{1,0:T(8,128)S(1)}, u32[]{:S(2)}, u32[]{:S(2)}) collective-permute-start(f32[128,1024]{1,0:T(8,128)S(1)} %fusion), channel_id=1, source_target_pairs={{0,1},{1,0},{2,3},{3,2},{4,5},{5,4},{6,7},{7,6},{8,9},{9,8},{10,11... | collective-permute-start | bytes 1572872 | tf_op jit(solution)/shard_map/ppermute | solution.py:457
  91.8 6.0 %collective-permute-start.19 = (f32[256,128]{1,0:T(8,128)S(1)}, f32[256,128]{1,0:T(8,128)S(1)}, u32[]{:S(2)}, u32[]{:S(2)}) collective-permute-start(f32[256,128]{1,0:T(8,128)S(1)} %slice.104), channel_id=1, source_target_pairs={{0,8},{8,0},{16,24},{24,16},{1,9},{9,1},{17,25},{25,17},{2,10},{10... | collective-permute-start | bytes 393224 | tf_op jit(solution)/shard_map/ppermute | solution.py:600
  93.5 18.9 %collective-permute-start.9 = (f32[256,1024]{1,0:T(8,128)S(1)}, f32[256,1024]{1,0:T(8,128)S(1)}, u32[]{:S(2)}, u32[]{:S(2)}) collective-permute-start(f32[256,1024]{1,0:T(8,128)S(1)} %constant_dynamic-slice_fusion.1), channel_id=1, source_target_pairs={{0,1},{1,0},{2,3},{3,2},{4,5},{5,4},{6,7},{7,6},{8,9},{9,8},{10,11... | collective-permute-start | bytes 3145736 | tf_op jit(solution)/shard_map/ppermute | solution.py:457
  98.9 4.3 %collective-permute-start.15 = (f32[128,128]{1,0:T(8,128)S(1)}, f32[128,128]{1,0:T(8,128)S(1)}, u32[]{:S(2)}, u32[]{:S(2)}) collective-permute-start(f32[128,128]{1,0:T(8,128)S(1)} %get-tuple-element.73), channel_id=1, source_target_pairs={{0,8},{8,0},{16,24},{24,16},{1,9},{9,1},{17,25},{25,17},{2,10},{10... | collective-permute-start | bytes 196616 | tf_op jit(solution)/shard_map/ppermute | solution.py:600
  100.4 7.5 %collective-permute-start.20 = (f32[256,128]{1,0:T(8,128)S(1)}, f32[256,128]{1,0:T(8,128)S(1)}, u32[]{:S(2)}, u32[]{:S(2)}) collective-permute-start(f32[256,128]{1,0:T(8,128)S(1)} %get-tuple-element.95), channel_id=1, source_target_pairs={{0,16},{8,24},{16,0},{24,8},{1,17},{9,25},{17,1},{25,9},{2,18},{10... | collective-permute-start | bytes 393224 | tf_op jit(solution)/shard_map/ppermute | solution.py:600
  102.0 5.3 %collective-permute-start.17 = (f32[128,128]{1,0:T(8,128)S(1)}, f32[128,128]{1,0:T(8,128)S(1)}, u32[]{:S(2)}, u32[]{:S(2)}) collective-permute-start(f32[128,128]{1,0:T(8,128)S(1)} %get-tuple-element.74), channel_id=1, source_target_pairs={{0,16},{8,24},{16,0},{24,8},{1,17},{9,25},{17,1},{25,9},{2,18},{10... | collective-permute-start | bytes 196616 | tf_op jit(solution)/shard_map/ppermute | solution.py:600
  103.2 5.4 %collective-permute-start.16 = (f32[128,128]{1,0:T(8,128)S(1)}, f32[128,128]{1,0:T(8,128)S(1)}, u32[]{:S(2)}, u32[]{:S(2)}) collective-permute-start(f32[128,128]{1,0:T(8,128)S(1)} %add.136), channel_id=1, source_target_pairs={{0,16},{8,24},{16,0},{24,8},{1,17},{9,25},{17,1},{25,9},{2,18},{10... | collective-permute-start | bytes 196616 | tf_op jit(solution)/shard_map/ppermute | solution.py:600
  107.3 4.3 %collective-permute-start.18 = (f32[128,128]{1,0:T(8,128)S(1)}, f32[128,128]{1,0:T(8,128)S(1)}, u32[]{:S(2)}, u32[]{:S(2)}) collective-permute-start(f32[128,128]{1,0:T(8,128)S(1)} %add.138), channel_id=1, source_target_pairs={{0,8},{8,0},{16,24},{24,16},{1,9},{9,1},{17,25},{25,17},{2,10},{10... | collective-permute-start | bytes 196616 | tf_op jit(solution)/shard_map/ppermute | solution.py:600
